TPU v7x, 32 devices: a whole 2x2x4 slice. The times are simulated.
32 devices in a mesh: group: 2 (over y), cell: 8 (over z, x), day: 2 (over core).
Axes of the slice: x: 2, y: 2, z: 4, core: 2. Of those that a mesh axis runs over, the one named last changes fastest.
Arguments:
- predictors: bfloat16 [1024, 16384], P('day', 'cell'), may hold values from -180 to 180
- predictand: bfloat16 [1024, 32768], P('day', ('group', 'cell')), parts along dimension 1, may hold values from -180 to 180
- pred_map: int32 [128], P('cell'), may hold values from 0 to 127, as said below
- cell_map: int32 [256], P(('group', 'cell')), parts along dimension 0, may hold values from 0 to 127, as said below
- start_panel: bfloat16 [64, 32768], P(None, ('group', 'cell')), parts along dimension 1, may hold values from -6 to 6
Outputs:
- pred_side: float32 [64, 32768], P(None, ('group', 'cell', 'day')), parts along dimension 1
- cell_side: float32 [64, 32768], P(None, ('group', 'cell', 'day')), parts along dimension 1
There are 2 independent parts, one for each index of `group`. A program takes and returns all parts, laid end to end along the dimension named above; an argument that names none is the same for every part. Nothing has to cross between parts.
Inputs may be any that keep to these rules, and one draw needn't show every extreme that they name: `pred_map`: aligned block s of 16 entries is a permutation of the tile numbers s * 16 to s * 16 + 15. `cell_map`: aligned block s of 16 entries is a permutation of the tile numbers s * 16 to s * 16 + 15.
All inputs are finite; a program needn't handle non-finite values.
Results may differ from a plain program's by a relative error of at most 0.02.
The roundings to bfloat16 on the way count: a program that leaves them out, or rounds other values in their place, can miss the bound.
Values may be sent and summed in bfloat16 or wider, within the bound.
No kernel may reach another device: no remote copies, remote signals or barrier semaphores. Data moves between devices by JAX's collectives and lax.ppermute only.
A program may use at most 64 MiB of HBM per device.

v0:
```python
import jax
import jax.numpy as jnp
from jax import lax
from jax.sharding import PartitionSpec as P

ITERS = 3


def natural_order(stored, tile_map):
    height = stored.shape[0]
    number = tile_map.shape[0]
    placed_slot = tile_map % number
    slots = jnp.arange(number, dtype=jnp.int32)
    inverse = jnp.sum(
        slots[None, :] * (placed_slot[None, :] == slots[:, None]).astype(jnp.int32), axis=1
    )
    blocks = stored.reshape(height, number, 128)
    return jnp.take(blocks, inverse, axis=1).reshape(height, number * 128)


def scores_over_cells(partial_value):
    return lax.psum(partial_value, "cell")


def moments_over_cells(partial_value):
    return lax.psum(partial_value, "cell")


def loads_whole(partial_value):
    return lax.psum(partial_value, "day")


def half_step(current, first_field, second_field, sum_scores, reduce_days, sum_moments, cell_count):
    contract = (((1,), (1,)), ((), ()))
    partial_value = lax.dot_general(
        current, first_field, contract, preferred_element_type=jnp.float32
    )
    scores = sum_scores(partial_value).astype(jnp.bfloat16)
    unscaled = reduce_days(jnp.dot(scores, second_field, preferred_element_type=jnp.float32))
    local_moments = jnp.dot(
        unscaled, unscaled.T, precision=lax.Precision.HIGHEST, preferred_element_type=jnp.float32
    )
    moments = sum_moments(local_moments) / cell_count
    factor = jnp.linalg.cholesky(moments)
    return lax.linalg.triangular_solve(factor, unscaled, left_side=True, lower=True)


def own_half(whole):
    half_width = whole.shape[1] // lax.axis_size("day")
    return lax.dynamic_slice_in_dim(whole, lax.axis_index("day") * half_width, half_width, 1)


def local(predictors, predictand, pred_map, cell_map, start_panel):
    pred_nat = natural_order(predictors, pred_map)
    cell_nat = natural_order(predictand, cell_map)
    pred_count = pred_nat.shape[1] * lax.axis_size("cell")
    cell_count = cell_nat.shape[1] * lax.axis_size("cell")
    current = start_panel
    pred_whole = None
    cell_whole = None
    for iteration in range(ITERS):
        pred_whole = half_step(
            current,
            cell_nat,
            pred_nat,
            scores_over_cells,
            loads_whole,
            moments_over_cells,
            pred_count,
        )
        cell_whole = half_step(
            pred_whole.astype(jnp.bfloat16),
            pred_nat,
            cell_nat,
            scores_over_cells,
            loads_whole,
            moments_over_cells,
            cell_count,
        )
        current = cell_whole.astype(jnp.bfloat16)
    return (own_half(pred_whole), own_half(cell_whole))


def solution(mesh):
    in_specs = (
        P("day", "cell"),
        P("day", ("group", "cell")),
        P("cell"),
        P(("group", "cell")),
        P(None, ("group", "cell")),
    )
    out_specs = (P(None, ("group", "cell", "day")), P(None, ("group", "cell", "day")))
    return jax.shard_map(local, mesh=mesh, in_specs=in_specs, out_specs=out_specs, check_vma=False)
```

profile of v0, /device:TPU:0, one launch (start us, length us, event | category | flops | bytes accessed | tf_op | source)
XLA Modules:
  0.0 704.0 jit_solution(246630704292377170)
XLA Ops:
  7.2 0.7 and_select_fusion
  8.9 2.9 copy.52
  11.7 2.4 copy.53
  14.1 2.5 gather_fusion.1
  16.7 1.6 select_bitcast_fusion
  18.3 2.9 copy.54
  21.2 3.9 copy.49
  25.1 3.9 copy.50
  29.0 3.7 gather_fusion
  32.7 3.1 select_bitcast_fusion.1
  35.9 3.9 copy.51
  39.8 2.1 convolution_bitcast_fusion
  41.9 40.2 %all-reduce.24 = bf16[64,512]{1,0:T(8,128)(2,1)S(1)} all-reduce(f32[64,512]{1,0:T(8,128)S(1)} %convolution_bitcast_fusion), channel_id=1, replica_groups=mesh['group'=2,'cell'=8,'day'=2] {'cell'}, use_global_device_ids=true, to_apply=%region_1.3 | all-reduce | flops 32768 | bytes 196608 | tf_op jit(solution)/shard_map/psum | solution.py:22
  82.1 1.6 fusion.59
  83.7 16.1 %all-reduce.13.cloned.1.call-done = f32[64,2048]{1,0:T(8,128)} async-done(((f32[64,2048]{1,0:T(8,128)}), f32[64,2048]{1,0:T(8,128)}) %all-reduce.13.cloned.1.call-update) | async-done | bytes 524304 | tf_op jit(solution)/shard_map/psum | solution.py:30
  99.8 1.8 fusion.44
  101.6 37.4 %psum.128 = f32[64,64]{0,1:T(8,128)S(1)} all-reduce(f32[64,64]{0,1:T(8,128)S(1)} %fusion.44), channel_id=1, replica_groups=mesh['group'=2,'cell'=8,'day'=2] {'cell'}, use_global_device_ids=true, to_apply=%region_4.6 | all-reduce | flops 4096 | bytes 32768 | tf_op jit(solution)/shard_map/psum | solution.py:26
  139.1 5.8 cholesky.104
  146.3 4.9 custom-call.10
  151.2 1.7 convolution_convert_fusion.3
  153.3 34.1 %all-reduce.25 = bf16[64,512]{1,0:T(8,128)(2,1)S(1)} all-reduce(f32[64,512]{1,0:T(8,128)S(1)} %fusion.45), channel_id=1, replica_groups=mesh['group'=2,'cell'=8,'day'=2] {'cell'}, use_global_device_ids=true, to_apply=%region_7.11 | all-reduce | flops 32768 | bytes 196608 | tf_op jit(solution)/shard_map/psum | solution.py:22
  187.5 3.2 fusion.58
  190.7 17.8 %all-reduce.15.cloned.1.call-done = f32[64,2048]{1,0:T(8,128)} async-done(((f32[64,2048]{1,0:T(8,128)}), f32[64,2048]{1,0:T(8,128)}) %all-reduce.15.cloned.1.call-update) | async-done | bytes 524304 | tf_op jit(solution)/shard_map/psum | solution.py:30
  208.5 1.8 fusion.46
  210.2 37.4 %psum.131 = f32[64,64]{0,1:T(8,128)S(1)} all-reduce(f32[64,64]{0,1:T(8,128)S(1)} %fusion.46), channel_id=1, replica_groups=mesh['group'=2,'cell'=8,'day'=2] {'cell'}, use_global_device_ids=true, to_apply=%region_9.13 | all-reduce | flops 4096 | bytes 32768 | tf_op jit(solution)/shard_map/psum | solution.py:26
  247.7 5.8 cholesky.115
  254.9 4.9 custom-call.11
  259.8 1.7 convolution_convert_fusion.2
  261.5 2.1 fusion.47
  263.5 34.3 %all-reduce.26 = bf16[64,512]{1,0:T(8,128)(2,1)S(1)} all-reduce(f32[64,512]{1,0:T(8,128)S(1)} %fusion.47), channel_id=1, replica_groups=mesh['group'=2,'cell'=8,'day'=2] {'cell'}, use_global_device_ids=true, to_apply=%region_10.14 | all-reduce | flops 32768 | bytes 196608 | tf_op jit(solution)/shard_map/psum | solution.py:22
  297.9 1.6 fusion.57
  299.5 17.8 %all-reduce.17.cloned.1.call-done = f32[64,2048]{1,0:T(8,128)} async-done(((f32[64,2048]{1,0:T(8,128)}), f32[64,2048]{1,0:T(8,128)}) %all-reduce.17.cloned.1.call-update) | async-done | bytes 524304 | tf_op jit(solution)/shard_map/psum | solution.py:30
  317.3 1.8 fusion.48
  319.0 37.4 %psum.134 = f32[64,64]{0,1:T(8,128)S(1)} all-reduce(f32[64,64]{0,1:T(8,128)S(1)} %fusion.48), channel_id=1, replica_groups=mesh['group'=2,'cell'=8,'day'=2] {'cell'}, use_global_device_ids=true, to_apply=%region_12.16 | all-reduce | flops 4096 | bytes 32768 | tf_op jit(solution)/shard_map/psum | solution.py:26
  356.5 5.8 cholesky.126
  363.7 4.9 custom-call.12
  368.6 1.7 convolution_convert_fusion.1
  370.8 34.1 %all-reduce.27 = bf16[64,512]{1,0:T(8,128)(2,1)S(1)} all-reduce(f32[64,512]{1,0:T(8,128)S(1)} %fusion.49), channel_id=1, replica_groups=mesh['group'=2,'cell'=8,'day'=2] {'cell'}, use_global_device_ids=true, to_apply=%region_13.17 | all-reduce | flops 32768 | bytes 196608 | tf_op jit(solution)/shard_map/psum | solution.py:22
  404.9 3.2 fusion.56
  408.1 17.8 %all-reduce.19.cloned.1.call-done = f32[64,2048]{1,0:T(8,128)} async-done(((f32[64,2048]{1,0:T(8,128)}), f32[64,2048]{1,0:T(8,128)}) %all-reduce.19.cloned.1.call-update) | async-done | bytes 524304 | tf_op jit(solution)/shard_map/psum | solution.py:30
  425.9 1.8 fusion.50
  427.7 37.4 %psum.137 = f32[64,64]{0,1:T(8,128)S(1)} all-reduce(f32[64,64]{0,1:T(8,128)S(1)} %fusion.50), channel_id=1, replica_groups=mesh['group'=2,'cell'=8,'day'=2] {'cell'}, use_global_device_ids=true, to_apply=%region_15.19 | all-reduce | flops 4096 | bytes 32768 | tf_op jit(solution)/shard_map/psum | solution.py:26
  465.1 5.8 cholesky.137
  472.3 4.9 custom-call.13
  477.2 1.7 convolution_convert_fusion
  478.9 2.1 fusion.51
  481.0 34.1 %all-reduce.28 = bf16[64,512]{1,0:T(8,128)(2,1)S(1)} all-reduce(f32[64,512]{1,0:T(8,128)S(1)} %fusion.51), channel_id=1, replica_groups=mesh['group'=2,'cell'=8,'day'=2] {'cell'}, use_global_device_ids=true, to_apply=%region_16.20 | all-reduce | flops 32768 | bytes 196608 | tf_op jit(solution)/shard_map/psum | solution.py:22
  515.1 1.6 fusion.55
  516.8 17.8 %all-reduce.21.cloned.1.call-done = f32[64,2048]{1,0:T(8,128)} async-done(((f32[64,2048]{1,0:T(8,128)}), f32[64,2048]{1,0:T(8,128)}) %all-reduce.21.cloned.1.call-update) | async-done | bytes 524304 | tf_op jit(solution)/shard_map/psum | solution.py:30
  534.5 1.8 fusion.52
  536.3 37.4 %psum.140 = f32[64,64]{0,1:T(8,128)S(1)} all-reduce(f32[64,64]{0,1:T(8,128)S(1)} %fusion.52), channel_id=1, replica_groups=mesh['group'=2,'cell'=8,'day'=2] {'cell'}, use_global_device_ids=true, to_apply=%region_18.22 | all-reduce | flops 4096 | bytes 32768 | tf_op jit(solution)/shard_map/psum | solution.py:26
  573.8 5.8 cholesky.148
  581.0 4.9 custom-call.14
  585.9 1.7 fusion.23
  588.0 34.4 %all-reduce.29 = bf16[64,512]{1,0:T(8,128)(2,1)S(1)} all-reduce(f32[64,512]{1,0:T(8,128)S(1)} %fusion), channel_id=1, replica_groups=mesh['group'=2,'cell'=8,'day'=2] {'cell'}, use_global_device_ids=true, to_apply=%region_19.23 | all-reduce | flops 32768 | bytes 196608 | tf_op jit(solution)/shard_map/psum | solution.py:22
  622.4 3.1 fusion.54
  625.6 0.7 constant_dynamic-slice_fusion
  626.3 17.1 %all-reduce.23.cloned.1.call-done = f32[64,2048]{1,0:T(8,128)} async-done(((f32[64,2048]{1,0:T(8,128)}), f32[64,2048]{1,0:T(8,128)}) %all-reduce.23.cloned.1.call-update) | async-done | bytes 524304 | tf_op jit(solution)/shard_map/psum | solution.py:30
  643.4 1.8 fusion.53
  645.2 37.4 %psum.143 = f32[64,64]{0,1:T(8,128)S(1)} all-reduce(f32[64,64]{0,1:T(8,128)S(1)} %fusion.53), channel_id=1, replica_groups=mesh['group'=2,'cell'=8,'day'=2] {'cell'}, use_global_device_ids=true, to_apply=%region_21.25 | all-reduce | flops 4096 | bytes 32768 | tf_op jit(solution)/shard_map/psum | solution.py:26
  682.6 5.8 cholesky.159
  689.8 4.9 custom-call.15
  694.7 1.7 fusion.20
  696.4 0.7 constant_dynamic-slice_fusion.1
  (60 shorter events, 11.2 us)
Async XLA Ops:
  7.2 32.6 %copy-start = (bf16[64,2048]{1,0:T(8,128)(2,1)S(1)}, bf16[64,2048]{1,0:T(8,128)(2,1)}, u32[]{:S(2)}) copy-start(bf16[64,2048]{1,0:T(8,128)(2,1)} %param.14) | copy-start | bytes 786436
  7.2 92.7 %all-reduce.13.cloned.1.call-start = ((), (), s32[]{:S(2)}) async-start(), calls=%async_computation | async-start | bytes 1048576 | tf_op jit(solution)/shard_map/psum | solution.py:30
  83.7 124.8 %all-reduce.15.cloned.1.call-start = ((), (), s32[]{:S(2)}) async-start(), calls=%async_computation.1 | async-start | bytes 1048576 | tf_op jit(solution)/shard_map/psum | solution.py:30
  190.6 126.6 %all-reduce.17.cloned.1.call-start = ((), (), s32[]{:S(2)}) async-start(), calls=%async_computation.2 | async-start | bytes 1048576 | tf_op jit(solution)/shard_map/psum | solution.py:30
  299.5 126.5 %all-reduce.19.cloned.1.call-start = ((), (), s32[]{:S(2)}) async-start(), calls=%async_computation.3 | async-start | bytes 1048576 | tf_op jit(solution)/shard_map/psum | solution.py:30
  408.1 126.5 %all-reduce.21.cloned.1.call-start = ((), (), s32[]{:S(2)}) async-start(), calls=%async_computation.4 | async-start | bytes 1048576 | tf_op jit(solution)/shard_map/psum | solution.py:30
  516.7 126.7 %all-reduce.23.cloned.1.call-start = ((), (), s32[]{:S(2)}) async-start(), calls=%async_computation.5 | async-start | bytes 1048576 | tf_op jit(solution)/shard_map/psum | solution.py:30
Sparse Core Ops, SparseCore 0:
  83.8 16.0 all-reduce.12
  190.8 17.6 all-reduce.14
  299.6 17.6 all-reduce.16
  408.2 17.6 all-reduce.18
  516.8 17.6 all-reduce.20
  625.7 17.6 all-reduce.22
where the time goes:
time: 705 us; the launch traced here: 704 us
  blocking collectives  435 us (62%)
  waiting for transfers between devices  104 us (15%)
  other arithmetic  78.9 us (11%)
  matrix products  42.4 us (6%)
  local copies, waits for them, and re-layouts  28.1 us (4%)
  between operations  14.5 us (2%)
    psum x6, blocking collectives, moments_over_cells(): return lax.psum(partial_value, 'cell')  224 us
    psum x6, blocking collectives, scores_over_cells(): return lax.psum(partial_value, 'cell')  211 us
    psum x6, waiting for transfers between devices, loads_whole(): return lax.psum(partial_value, 'day')  104 us
    another operation x18, other arithmetic, half_step(): factor = jnp.linalg.cholesky(moments)  39.1 us
    another operation x12, other arithmetic, half_step(): lax.linalg.triangular_solve(factor, unscaled, left_side=True, lower=True)  33.3 us
    dot_general x6, matrix products, half_step(): jnp.dot(scores, second_field, preferred_element_type=jnp.float32)  14.2 us
  transfers between devices with their start and end apart: 6, of which 6 were waited for; matrix products, arithmetic and copies ran while one was open for 0% of the time, Pallas kernels for 0%

commit v1 on v0

v1 whole, which is shorter than its diff:
```python
import functools

import jax
import jax.numpy as jnp
from jax import lax
from jax.experimental import pallas as pl
from jax.experimental.pallas import tpu as pltpu
from jax.sharding import PartitionSpec as P

ITERS = 3
LANES = 128
BLOCK = 256
SPLITS = 3
F32 = jnp.float32
BF16 = jnp.bfloat16
NT = (((1,), (1,)), ((), ()))
VMEM_BYTES = 50 * 1024 * 1024


def triangle(days):
    count = days // BLOCK
    return [(i, j) for i in range(count) for j in range(i, count)]


def any_spec():
    return pl.BlockSpec(memory_space=pl.ANY)


def smem_spec():
    return pl.BlockSpec(memory_space=pltpu.SMEM)


def params():
    return pltpu.CompilerParams(vmem_limit_bytes=VMEM_BYTES)


def place_kernel(place, pred_map, cell_map, pred, cell, pred_keep, pred_send, cell_keep, cell_send, sems):
    day = place[0]
    fields = ((pred_map, pred, pred_keep, pred_send), (cell_map, cell, cell_keep, cell_send))
    for f, (tile_map, stored, keep, send) in enumerate(fields):
        number = tile_map.shape[0]
        half = number // 2
        for t in range(number):
            slot = lax.rem(lax.rem(tile_map[t], number) + half * day, number)
            source = stored.at[:, pl.ds(t * LANES, LANES)]

            @pl.when(slot < half)
            def _():
                to = pl.multiple_of(slot * LANES, LANES)
                pltpu.make_async_copy(source, keep.at[:, pl.ds(to, LANES)], sems.at[f, t]).start()

            @pl.when(slot >= half)
            def _():
                to = pl.multiple_of((slot - half) * LANES, LANES)
                pltpu.make_async_copy(source, send.at[:, pl.ds(to, LANES)], sems.at[f, t]).start()

    for f, (tile_map, stored, keep, send) in enumerate(fields):
        for t in range(tile_map.shape[0]):
            part = pl.ds(0, LANES)
            pltpu.make_async_copy(stored.at[:, part], keep.at[:, part], sems.at[f, t]).wait()


def place_tiles(place, pred_map, cell_map, pred, cell):
    rows, width = pred.shape
    half = jax.ShapeDtypeStruct((rows, width // 2), pred.dtype)
    return pl.pallas_call(
        place_kernel,
        out_shape=(half,) * 4,
        in_specs=[smem_spec()] * 3 + [any_spec()] * 2,
        out_specs=(any_spec(),) * 4,
        scratch_shapes=[pltpu.SemaphoreType.DMA((2, pred_map.shape[0]))],
        compiler_params=params(),
        name="place_tiles",
    )(place, pred_map, cell_map, pred, cell)


def load_days(keep, recv, whole, day, sems):
    rows = keep.shape[0]
    first = pltpu.make_async_copy(
        keep, whole.at[pl.ds(pl.multiple_of(day * rows, rows), rows), :], sems.at[0]
    )
    second = pltpu.make_async_copy(
        recv, whole.at[pl.ds(pl.multiple_of((1 - day) * rows, rows), rows), :], sems.at[1]
    )
    return first, second


def store_block(scr, half, row, value):
    for c in range(value.shape[1] // LANES):
        height = value.shape[0]
        scr[half, pl.ds(row + c * height, height), :] = value[:, c * LANES : (c + 1) * LANES]


def flush(scr, keep, send, sems):
    one = pltpu.make_async_copy(scr.at[0], keep, sems.at[0])
    two = pltpu.make_async_copy(scr.at[1], send, sems.at[1])
    one.start()
    two.start()
    one.wait()
    two.wait()


def first_gram_kernel(blocks, place, pk, pr, ck, cr, start, keep, send, pred, cell, panel, scr, sems, outs):
    day = place[0]
    group = place[1]
    copies = load_days(pk, pr, pred, day, sems.at[0]) + load_days(ck, cr, cell, day, sems.at[1])
    width = panel.shape[1]
    begin = pl.multiple_of(day * width, width)
    copies += (pltpu.make_async_copy(start.at[:, pl.ds(begin, width)], panel, sems.at[2, 0]),)
    for copy in copies:
        copy.start()
    for copy in copies[:2]:
        copy.wait()
    share = len(blocks) // 2
    size = BLOCK * BLOCK // LANES
    per_half = (share + 1) // 2
    for k in range(share):
        i = blocks[k][0] + group * (blocks[share + k][0] - blocks[k][0])
        j = blocks[k][1] + group * (blocks[share + k][1] - blocks[k][1])
        left = pred[pl.ds(pl.multiple_of(i * BLOCK, BLOCK), BLOCK), :]
        right = pred[pl.ds(pl.multiple_of(j * BLOCK, BLOCK), BLOCK), :]
        value = lax.dot_general(left, right, NT, preferred_element_type=F32)
        half = day if k < per_half else 1 - day
        store_block(scr, half, (k % per_half) * size, value)
    for copy in copies[2:]:
        copy.wait()
    scores = lax.dot_general(panel[...], cell[...], NT, preferred_element_type=F32)
    store_block(scr, 1 - day, (share % per_half) * size, scores)
    flush(scr, keep, send, outs)


def second_gram_kernel(blocks, place, ck, cr, keep, send, cell, scr, sems, outs):
    day = place[0]
    copies = load_days(ck, cr, cell, day, sems)
    for copy in copies:
        copy.start()
    for copy in copies:
        copy.wait()
    size = BLOCK * BLOCK // LANES
    per_half = len(blocks) // 2
    for k, (i, j) in enumerate(blocks):
        value = lax.dot_general(
            cell[i * BLOCK : (i + 1) * BLOCK, :],
            cell[j * BLOCK : (j + 1) * BLOCK, :],
            NT,
            preferred_element_type=F32,
        )
        half = day if k < per_half else 1 - day
        store_block(scr, half, (k % per_half) * size, value)
    flush(scr, keep, send, outs)


def first_gram(place, pk, pr, ck, cr, start):
    days, width = 2 * pk.shape[0], pk.shape[1]
    blocks = triangle(days)
    rows = (len(blocks) // 2 + 1) // 2 * (BLOCK * BLOCK // LANES)
    out = jax.ShapeDtypeStruct((rows, LANES), F32)
    return pl.pallas_call(
        functools.partial(first_gram_kernel, blocks),
        out_shape=(out, out),
        in_specs=[smem_spec()] + [any_spec()] * 5,
        out_specs=(any_spec(), any_spec()),
        scratch_shapes=[
            pltpu.VMEM((days, width), BF16),
            pltpu.VMEM((days, width), BF16),
            pltpu.VMEM((start.shape[0], width), BF16),
            pltpu.VMEM((2, rows, LANES), F32),
            pltpu.SemaphoreType.DMA((3, 2)),
            pltpu.SemaphoreType.DMA((2,)),
        ],
        compiler_params=params(),
        name="first_gram",
    )(place, pk, pr, ck, cr, start)


def second_gram(place, ck, cr):
    days, width = 2 * ck.shape[0], ck.shape[1]
    blocks = triangle(days)
    rows = len(blocks) // 2 * (BLOCK * BLOCK // LANES)
    out = jax.ShapeDtypeStruct((rows, LANES), F32)
    return pl.pallas_call(
        functools.partial(second_gram_kernel, blocks),
        out_shape=(out, out),
        in_specs=[smem_spec()] + [any_spec()] * 2,
        out_specs=(any_spec(), any_spec()),
        scratch_shapes=[
            pltpu.VMEM((days, width), BF16),
            pltpu.VMEM((2, rows, LANES), F32),
            pltpu.SemaphoreType.DMA((2,)),
            pltpu.SemaphoreType.DMA((2,)),
        ],
        compiler_params=params(),
        name="second_gram",
    )(place, ck, cr)


def bit_orders(bits):
    plain = list(range(bits))
    swapped = plain[:]
    if bits > 2:
        swapped[0], swapped[1] = 1, 0
    return plain, swapped


def cell_exchange(value, orders, stage, cells):
    pairs = []
    for c in range(cells):
        for d in range(2):
            pairs.append((2 * c + d, 2 * (c ^ (1 << orders[d][stage])) + d))
    return lax.ppermute(value, ("cell", "day"), pairs)


def other_core(value):
    return lax.ppermute(value, "day", [(0, 1), (1, 0)])


def sum_over_cells(keep, send):
    cells = lax.axis_size("cell")
    bits = cells.bit_length() - 1
    orders = bit_orders(bits)
    cell = lax.axis_index("cell")
    day = lax.axis_index("day")
    recv = other_core(send)
    mine = keep
    for stage in range(bits - 1):
        bit = jnp.where(day == 0, orders[0][stage], orders[1][stage])
        own = (cell >> bit) & 1
        half = mine.shape[0] // 2
        away = lax.dynamic_slice_in_dim(mine, (1 - own) * half, half, 0)
        away = away + lax.dynamic_slice_in_dim(recv, (1 - own) * half, half, 0)
        home = lax.dynamic_slice_in_dim(mine, own * half, half, 0)
        home = home + lax.dynamic_slice_in_dim(recv, own * half, half, 0)
        recv = cell_exchange(away, orders, stage, cells)
        mine = home
    part = mine + recv
    part = part + cell_exchange(part, orders, bits - 1, cells)
    for stage in reversed(range(bits - 1)):
        part = jnp.concatenate([part, cell_exchange(part, orders, stage, cells)], axis=0)
    return part


def placed_copies(source, target, half, bits, order, cell, sem):
    pieces = 1 << (bits - 1)
    rows = source.shape[0] // pieces
    copies = []
    for p in range(pieces):
        to = 0
        for stage in range(bits - 1):
            digit = (p >> (bits - 2 - stage)) & 1
            own = (cell >> order[stage]) & 1
            to = 2 * to + (own ^ digit)
        begin = pl.multiple_of(to * rows, 8)
        copies.append(
            pltpu.make_async_copy(
                source.at[pl.ds(p * rows, rows), :], target.at[half, pl.ds(begin, rows), :], sem.at[p]
            )
        )
    return copies


def load_block(packed, half, row, height, width):
    tiles = [packed[half, pl.ds(row + c * height, height), :] for c in range(width // LANES)]
    return jnp.concatenate(tiles, axis=1)


def split3(value):
    first = value.astype(BF16)
    rest = value - first.astype(F32)
    second = rest.astype(BF16)
    third = (rest - second.astype(F32)).astype(BF16)
    return first, second, third


def assemble(packed, half, row, i, j, gram):
    value = load_block(packed, half, row, BLOCK, BLOCK)
    rows, cols = pl.ds(i * BLOCK, BLOCK), pl.ds(j * BLOCK, BLOCK)
    for s, piece in enumerate(split3(value)):
        gram[s, rows, cols] = piece
    if i != j:
        for s, piece in enumerate(split3(value.T)):
            gram[s, cols, rows] = piece


def exact_dot(left, right):
    return jnp.dot(left, right, precision=lax.Precision.HIGHEST, preferred_element_type=F32)


def inverse_factor(moments):
    k_rows = moments.shape[0]
    row_ids = lax.broadcasted_iota(jnp.int32, (k_rows, k_rows), 0)
    col_ids = lax.broadcasted_iota(jnp.int32, (k_rows, k_rows), 1)
    work = jnp.concatenate([moments, (row_ids == col_ids).astype(F32)], axis=1)
    below = lax.broadcasted_iota(jnp.int32, (k_rows, 1), 0)
    scale = jnp.ones((k_rows, 1), F32)
    for k in range(k_rows):
        row = work[k : k + 1, :]
        column = work[:, k : k + 1]
        pivot = work[k : k + 1, k : k + 1]
        factor = jnp.where(below > k, column / pivot, 0.0)
        scale = jnp.where(below == k, 1.0 / jnp.sqrt(pivot), scale)
        work = work - factor * row
    return work[:, k_rows:] * scale


def half_step(scores, gram, cells):
    value = jnp.dot(scores, gram[0], preferred_element_type=F32)
    for s in range(1, SPLITS):
        value = value + jnp.dot(scores, gram[s], preferred_element_type=F32)
    moments = sum(
        lax.dot_general(piece, scores, NT, preferred_element_type=F32) for piece in split3(value)
    )
    inverse = inverse_factor(moments / cells)
    return inverse, exact_dot(inverse, value).astype(BF16)


def chain_kernel(
    blocks, bits, orders, counts, place,
    a_own, a_twin, y_own, y_twin, b_own, b_twin, pk, pr, ck, cr,
    pred_out, cell_out,
    alpha, other, beta, pred, cell, pred_gram, cell_gram, sems, data_sems,
):
    day, group, index = place[0], place[1], place[2]
    data = load_days(pk, pr, pred, day, data_sems.at[0]) + load_days(ck, cr, cell, day, data_sems.at[1])
    for copy in data:
        copy.start()

    def gather(core):
        own, twin = orders[core], orders[1 - core]
        copies = []
        for n, (source, target, half, order) in enumerate(
            (
                (a_own, alpha, core, own),
                (a_twin, alpha, 1 - core, twin),
                (y_own, other, core, own),
                (y_twin, other, 1 - core, twin),
                (b_own, beta, core, own),
                (b_twin, beta, 1 - core, twin),
            )
        ):
            copies += placed_copies(source, target, half, bits, order, index, sems.at[n])
        for copy in copies:
            copy.start()
        for copy in copies:
            copy.wait()

    @pl.when(day == 0)
    def _():
        gather(0)

    @pl.when(day == 1)
    def _():
        gather(1)

    size = BLOCK * BLOCK // LANES
    share = len(blocks) // 2
    per_half = (share + 1) // 2

    def assemble_pred(mine, theirs):
        for g, packed in enumerate((mine, theirs)):
            for k in range(share):
                i, j = blocks[g * share + k]
                assemble(packed, k // per_half, (k % per_half) * size, i, j, pred_gram)

    @pl.when(group == 0)
    def _():
        assemble_pred(alpha, other)

    @pl.when(group == 1)
    def _():
        assemble_pred(other, alpha)

    for k, (i, j) in enumerate(blocks):
        assemble(beta, k // share, (k % share) * size, i, j, cell_gram)

    days = pred.shape[0]
    height = pred_out.shape[0]
    scores = load_block(alpha, 1, (share % per_half) * size, height, days).astype(BF16)
    pred_inverse = cell_inverse = pred_scores = loadings = None
    for _ in range(ITERS):
        pred_scores = scores
        pred_inverse, loadings = half_step(scores, pred_gram, counts[0])
        cell_inverse, scores = half_step(loadings, cell_gram, counts[1])
    for copy in data:
        copy.wait()
    raw = jnp.dot(pred_scores, pred[...], preferred_element_type=F32)
    pred_out[...] = exact_dot(pred_inverse, raw)
    raw = jnp.dot(loadings, cell[...], preferred_element_type=F32)
    cell_out[...] = exact_dot(cell_inverse, raw)


def local(predictors, predictand, pred_map, cell_map, start_panel):
    cells = lax.axis_size("cell")
    bits = cells.bit_length() - 1
    orders = bit_orders(bits)
    days = predictors.shape[0] * 2
    width = predictors.shape[1] // 2
    height = start_panel.shape[0]
    counts = (float(predictors.shape[1] * cells), float(predictand.shape[1] * cells))
    blocks = triangle(days)
    place = jnp.stack([lax.axis_index("day"), lax.axis_index("group"), lax.axis_index("cell")])
    place = place.astype(jnp.int32)

    pk, ps, ck, cs = place_tiles(place, pred_map, cell_map, predictors, predictand)
    pr = other_core(ps)
    cr = other_core(cs)
    a_keep, a_send = first_gram(place, pk, pr, ck, cr, start_panel)
    b_keep, b_send = second_gram(place, ck, cr)
    a_own = sum_over_cells(a_keep, a_send)
    y_own = lax.ppermute(a_own, "group", [(0, 1), (1, 0)])
    b_own = sum_over_cells(b_keep, b_send)
    a_twin = other_core(a_own)
    y_twin = other_core(y_own)
    b_twin = other_core(b_own)

    out = jax.ShapeDtypeStruct((height, width), F32)
    pieces = 1 << (bits - 1)
    return pl.pallas_call(
        functools.partial(chain_kernel, blocks, bits, orders, counts),
        out_shape=(out, out),
        in_specs=[smem_spec()] + [any_spec()] * 10,
        scratch_shapes=[
            pltpu.VMEM((2,) + a_own.shape, F32),
            pltpu.VMEM((2,) + a_own.shape, F32),
            pltpu.VMEM((2,) + b_own.shape, F32),
            pltpu.VMEM((days, width), BF16),
            pltpu.VMEM((days, width), BF16),
            pltpu.VMEM((SPLITS, days, days), BF16),
            pltpu.VMEM((SPLITS, days, days), BF16),
            pltpu.SemaphoreType.DMA((6, pieces)),
            pltpu.SemaphoreType.DMA((2, 2)),
        ],
        compiler_params=params(),
        name="chain",
    )(place, a_own, a_twin, y_own, y_twin, b_own, b_twin, pk, pr, ck, cr)


def solution(mesh):
    in_specs = (
        P("day", "cell"),
        P("day", ("group", "cell")),
        P("cell"),
        P(("group", "cell")),
        P(None, ("group", "cell")),
    )
    out_specs = (P(None, ("group", "cell", "day")), P(None, ("group", "cell", "day")))
    return jax.shard_map(local, mesh=mesh, in_specs=in_specs, out_specs=out_specs, check_vma=False)
```

time: 705 us -> 223 us (0.32)
  blocking collectives: 435 us -> 0 us
  Pallas kernels: 0 us -> 127 us
  other arithmetic: 78.9 us -> 7.09 us
  waiting for transfers between devices: 104 us -> 51.7 us
  matrix products: 42.4 us -> 0 us
  starting transfers between devices: 0.25 us -> 31.4 us
  local copies, waits for them, and re-layouts: 28.1 us -> 3.48 us
  between operations: 14.5 us -> 0.97 us
    psum x12 -> x0, blocking collectives: 435 us -> none  [the longest x6 224 us: moments_over_cells(): return lax.psum(partial_value, 'cell')]
    pallas_call x0 -> x4, Pallas kernels: none -> 127 us  [the longest x1 65.5 us: place_tiles(): pl.pallas_call(place_kernel, out_shape=(half,) * 4, in_specs=[smem_spec()...]
    psum x6 -> x0, waiting for transfers between devices: 104 us -> none  [loads_whole(): return lax.psum(partial_value, 'day')]
    another operation x30 -> x1, other arithmetic: 72.4 us -> 0.08 us  [local(): jnp.stack([lax.axis_index('day'), lax.axis_index('group'), lax.axis_index...]
    ppermute x0 -> x18, waiting for transfers between devices: none -> 51.7 us  [the longest x10 33.1 us: cell_exchange(): return lax.ppermute(value, ('cell', 'day'), pairs)]
    dot_general x18 -> x0, matrix products: 32.3 us -> none  [the longest x6 14.2 us: half_step(): jnp.dot(scores, second_field, preferred_element_type=jnp.float32)]
    ppermute x0 -> x18, starting transfers between devices: none -> 31.4 us  [the longest x10 28.1 us: cell_exchange(): return lax.ppermute(value, ('cell', 'day'), pairs)]
    another operation x6 -> x0, matrix products: 10.1 us -> none  [half_step(): lax.linalg.triangular_solve(factor, unscaled, left_side=True, lower=True)]
  transfers between devices with their start and end apart: 6 -> 18, of which waited for: 6 -> 10; matrix products, arithmetic and copies ran while one was open for 0% -> 3% of each run, Pallas kernels for 0% -> 2%
where the time goes in v1:
time: 223 us; the launch traced here: 222 us
  Pallas kernels  127 us (57%)
  waiting for transfers between devices  51.7 us (23%)
  starting transfers between devices  31.4 us (14%)
  other arithmetic  7.09 us (3%)
  local copies, waits for them, and re-layouts  3.48 us (2%)
    pallas_call x1, Pallas kernels, place_tiles(): pl.pallas_call(place_kernel, out_shape=(half,) * 4, in_specs=[smem_spec()...  65.5 us
    pallas_call x1, Pallas kernels, local(): pl.pallas_call(functools.partial(chain_kernel, blocks, bits, orders, coun...  54.5 us
    ppermute x10, waiting for transfers between devices, cell_exchange(): return lax.ppermute(value, ('cell', 'day'), pairs)  33.1 us
    ppermute x10, starting transfers between devices, cell_exchange(): return lax.ppermute(value, ('cell', 'day'), pairs)  28.1 us
    ppermute x1, waiting for transfers between devices, local(): y_own = lax.ppermute(a_own, 'group', [(0, 1), (1, 0)])  11 us
    ppermute x7, waiting for transfers between devices, other_core(): return lax.ppermute(value, 'day', [(0, 1), (1, 0)])  7.66 us
  transfers between devices with their start and end apart: 18, of which 10 were waited for; matrix products, arithmetic and copies ran while one was open for 3% of the time, Pallas kernels for 2%

profile of v1, /device:TPU:0, one launch (start us, length us, event | category | flops | bytes accessed | tf_op | source)
XLA Modules:
  0.0 221.7 jit_solution(15661510166510717631)
XLA Ops:
  0.6 0.1 pad_add_fusion.place
  0.7 0.0 copy-start.5
  0.7 0.7 copy-done.5
  1.4 0.0 copy-start.6
  1.4 0.7 copy-done.6
  2.0 65.5 %place_tiles.1 = (bf16[512,1024]{1,0:T(8,128)(2,1)S(1)}, bf16[512,1024]{1,0:T(8,128)(2,1)}, bf16[512,1024]{1,0:T(8,128)(2,1)S(1)}, bf16[512,1024]{1,0:T(8,128)(2,1)}) custom-call(s32[3]{0:T(128)S(1)} %pad_add_fusion.place, s32[16]{0:T(128)S(1)} %copy-done.5, s32[16]{0:T(128)S(1)} %copy-done.6, bf16[512,2048]{1,0:T(8,128)(2,1)} %pred_.1, bf16[512,2048]{1,0:T(8,128)(2,1)} %cell.1), custom_call_target="tpu_custom_call" | custom-call | tf_op jit(solution)/shard_map/place_tiles/pallas_call | solution.py:66
  67.5 0.0 copy-start
  67.5 0.0 copy-start.2
  67.5 0.5 collective-permute-start.1
  68.1 2.5 %collective-permute-done.1.cr = bf16[512,1024]{1,0:T(8,128)(2,1)S(1)} collective-permute-done((bf16[512,1024]{1,0:T(8,128)(2,1)}, bf16[512,1024]{1,0:T(8,128)(2,1)S(1)}, u32[]{:S(2)}, u32[]{:S(2)}) %collective-permute-start.1) | collective-permute-done | bytes 1048608 | tf_op jit(solution)/shard_map/ppermute | solution.py:214
  70.6 3.5 %second_gram.1 = (f32[2560,128]{1,0:T(8,128)S(1)}, f32[2560,128]{1,0:T(8,128)}) custom-call(s32[3]{0:T(128)S(1)} %pad_add_fusion.place, bf16[512,1024]{1,0:T(8,128)(2,1)S(1)} %get-tuple-element.12.ck, bf16[512,1024]{1,0:T(8,128)(2,1)S(1)} %collective-permute-done.1.cr), custom_call_target="tpu_custom_call" | custom-call | tf_op jit(solution)/shard_map/second_gram/pallas_call | solution.py:181
  74.1 0.0 copy-start.3
  74.1 1.1 copy-done.3
  75.1 0.4 collective-permute-start.11
  75.5 0.1 collective-permute-start
  75.6 2.9 %collective-permute-done.11 = f32[2560,128]{1,0:T(8,128)} collective-permute-done((f32[2560,128]{1,0:T(8,128)}, f32[2560,128]{1,0:T(8,128)}, u32[]{:S(2)}, u32[]{:S(2)}) %collective-permute-start.11) | collective-permute-done | bytes 1310752 | tf_op jit(solution)/shard_map/ppermute | solution.py:214
  78.5 2.9 %dynamic-slice_add_fusion.1 = (f32[1280,128]{1,0:T(8,128)}, f32[1280,128]{1,0:T(8,128)}) fusion(f32[2560,128]{1,0:T(8,128)} %collective-permute-done.11, s32[]{:T(128)S(6)} %select_n.47, f32[2560,128]{1,0:T(8,128)} %copy-done.3, s32[]{:T(128)S(6)} %select_n.49), kind=kLoop, calls=%fused_computation.4 | loop fusion | flops 327680 | bytes 3932168 | tf_op jit(solution)/shard_map/add | solution.py:232
  81.5 0.0 copy-done
  81.5 0.0 copy-done.1
  81.5 2.8 %collective-permute-start.12 = (f32[1280,128]{1,0:T(8,128)}, f32[1280,128]{1,0:T(8,128)}, u32[]{:S(2)}, u32[]{:S(2)}) collective-permute-start(f32[1280,128]{1,0:T(8,128)} %get-tuple-element.19), channel_id=1, source_target_pairs={{0,2},{1,5},{2,0},{3,7},{4,6},{5,1},{6,4},{7,3},{8,10},{9,13},{10,... | collective-permute-start | bytes 1966088 | tf_op jit(solution)/shard_map/ppermute | solution.py:210
  84.3 0.0 collective-permute-done.pr
  84.3 0.0 copy-done.2
  84.3 0.0 copy-done.4
  84.3 0.0 copy-start.8
  84.3 3.7 %first_gram.1 = (f32[1536,128]{1,0:T(8,128)S(1)}, f32[1536,128]{1,0:T(8,128)S(1)}) custom-call(s32[3]{0:T(128)S(1)} %pad_add_fusion.place, bf16[512,1024]{1,0:T(8,128)(2,1)S(1)} %get-tuple-element.10.pk, bf16[512,1024]{1,0:T(8,128)(2,1)} %collective-permute-done.pr, bf16[512,1024]{1,0:T(8,128)(2,1)} %copy-done, bf16[512,1024]{1,0:T(8,128)(2,1)} %copy-done.1, ...), custom_call_target="tpu_custom_call" | custom-call | tf_op jit(solution)/shard_map/first_gram/pallas_call | solution.py:158
  88.0 0.1 collective-permute-start.2
  88.1 5.1 %collective-permute-done.12 = f32[1280,128]{1,0:T(8,128)} collective-permute-done((f32[1280,128]{1,0:T(8,128)}, f32[1280,128]{1,0:T(8,128)}, u32[]{:S(2)}, u32[]{:S(2)}) %collective-permute-start.12) | collective-permute-done | bytes 655392 | tf_op jit(solution)/shard_map/ppermute | solution.py:210
  93.2 0.0 copy-done.8
  93.2 1.7 dynamic-slice_add_fusion.4
  94.9 2.1 collective-permute-start.13
  97.0 0.0 collective-permute-done.2
  97.0 0.8 dynamic-slice_add_fusion.3
  97.9 1.5 collective-permute-start.3
  99.4 5.8 %collective-permute-done.13 = f32[640,128]{1,0:T(8,128)} collective-permute-done((f32[640,128]{1,0:T(8,128)}, f32[640,128]{1,0:T(8,128)}, u32[]{:S(2)}, u32[]{:S(2)}) %collective-permute-start.13) | collective-permute-done | bytes 327712 | tf_op jit(solution)/shard_map/ppermute | solution.py:210
  105.2 1.2 add_add_fusion
  106.3 3.6 %collective-permute-start.14 = (f32[640,128]{1,0:T(8,128)S(1)}, f32[640,128]{1,0:T(8,128)S(1)}, u32[]{:S(2)}, u32[]{:S(2)}) collective-permute-start(f32[640,128]{1,0:T(8,128)S(1)} %add_add_fusion), channel_id=1, source_target_pairs={{0,8},{1,9},{2,10},{3,11},{4,12},{5,13},{6,14},{7,15},{8,0},{9,1},... | collective-permute-start | bytes 983048 | tf_op jit(solution)/shard_map/ppermute | solution.py:210
  109.9 0.0 collective-permute-done.3
  110.0 1.6 collective-permute-start.4
  111.6 8.5 %collective-permute-done.14 = f32[640,128]{1,0:T(8,128)S(1)} collective-permute-done((f32[640,128]{1,0:T(8,128)S(1)}, f32[640,128]{1,0:T(8,128)S(1)}, u32[]{:S(2)}, u32[]{:S(2)}) %collective-permute-start.14) | collective-permute-done | bytes 327712 | tf_op jit(solution)/shard_map/ppermute | solution.py:210
  120.1 3.3 %collective-permute-start.15 = (f32[640,128]{1,0:T(8,128)S(1)}, f32[640,128]{1,0:T(8,128)S(1)}, u32[]{:S(2)}, u32[]{:S(2)}) collective-permute-start(f32[640,128]{1,0:T(8,128)S(1)} %add.87), channel_id=1, source_target_pairs={{0,4},{1,3},{2,6},{3,1},{4,0},{5,7},{6,2},{7,5},{8,12},{9,11},{10,... | collective-permute-start | bytes 983048 | tf_op jit(solution)/shard_map/ppermute | solution.py:210
  123.5 0.0 collective-permute-done.4
  123.5 3.4 %collective-permute-start.5 = (f32[384,128]{1,0:T(8,128)S(1)}, f32[384,128]{1,0:T(8,128)S(1)}, u32[]{:S(2)}, u32[]{:S(2)}) collective-permute-start(f32[384,128]{1,0:T(8,128)S(1)} %add_add_fusion.1), channel_id=1, source_target_pairs={{0,8},{1,9},{2,10},{3,11},{4,12},{5,13},{6,14},{7,15},{8,0},{9,1},... | collective-permute-start | bytes 589832 | tf_op jit(solution)/shard_map/ppermute | solution.py:210
  126.9 3.7 %collective-permute-done.5 = f32[384,128]{1,0:T(8,128)S(1)} collective-permute-done((f32[384,128]{1,0:T(8,128)S(1)}, f32[384,128]{1,0:T(8,128)S(1)}, u32[]{:S(2)}, u32[]{:S(2)}) %collective-permute-start.5) | collective-permute-done | bytes 196640 | tf_op jit(solution)/shard_map/ppermute | solution.py:210
  130.6 4.2 %collective-permute-start.6 = (f32[384,128]{1,0:T(8,128)S(1)}, f32[384,128]{1,0:T(8,128)S(1)}, u32[]{:S(2)}, u32[]{:S(2)}) collective-permute-start(f32[384,128]{1,0:T(8,128)S(1)} %add.77), channel_id=1, source_target_pairs={{0,4},{1,3},{2,6},{3,1},{4,0},{5,7},{6,2},{7,5},{8,12},{9,11},{10,... | collective-permute-start | bytes 589832 | tf_op jit(solution)/shard_map/ppermute | solution.py:210
  134.8 0.0 collective-permute-done.15
  134.9 2.7 %collective-permute-start.16 = (f32[1280,128]{1,0:T(8,128)S(1)}, f32[1280,128]{1,0:T(8,128)S(1)}, u32[]{:S(2)}, u32[]{:S(2)}) collective-permute-start(f32[1280,128]{1,0:T(8,128)S(1)} %pad_maximum_fusion.2), channel_id=1, source_target_pairs={{0,2},{1,5},{2,0},{3,7},{4,6},{5,1},{6,4},{7,3},{8,10},{9,13},{10,... | collective-permute-start | bytes 1966088 | tf_op jit(solution)/shard_map/ppermute | solution.py:210
  137.6 3.0 %collective-permute-done.6 = f32[384,128]{1,0:T(8,128)S(1)} collective-permute-done((f32[384,128]{1,0:T(8,128)S(1)}, f32[384,128]{1,0:T(8,128)S(1)}, u32[]{:S(2)}, u32[]{:S(2)}) %collective-permute-start.6) | collective-permute-done | bytes 196640 | tf_op jit(solution)/shard_map/ppermute | solution.py:210
  140.7 2.7 %collective-permute-start.7 = (f32[768,128]{1,0:T(8,128)S(1)}, f32[768,128]{1,0:T(8,128)S(1)}, u32[]{:S(2)}, u32[]{:S(2)}) collective-permute-start(f32[768,128]{1,0:T(8,128)S(1)} %pad_maximum_fusion.3), channel_id=1, source_target_pairs={{0,2},{1,5},{2,0},{3,7},{4,6},{5,1},{6,4},{7,3},{8,10},{9,13},{10,... | collective-permute-start | bytes 1179656 | tf_op jit(solution)/shard_map/ppermute | solution.py:210
  143.4 7.0 %collective-permute-done.7 = f32[768,128]{1,0:T(8,128)S(1)} collective-permute-done((f32[768,128]{1,0:T(8,128)S(1)}, f32[768,128]{1,0:T(8,128)S(1)}, u32[]{:S(2)}, u32[]{:S(2)}) %collective-permute-start.7) | collective-permute-done | bytes 393248 | tf_op jit(solution)/shard_map/ppermute | solution.py:210
  150.4 0.1 pad_maximum_fusion.1.a_own
  150.4 1.6 collective-permute-start.9
  152.0 0.0 collective-permute-done.16
  152.0 0.1 pad_maximum_fusion.b_own
  152.1 0.0 copy-start.7
  152.1 0.1 collective-permute-start.17
  152.2 0.5 collective-permute-start.8
  152.7 11.0 %collective-permute-done.9.y_own = f32[1536,128]{1,0:T(8,128)S(1)} collective-permute-done((f32[1536,128]{1,0:T(8,128)S(1)}, f32[1536,128]{1,0:T(8,128)S(1)}, u32[]{:S(2)}, u32[]{:S(2)}) %collective-permute-start.9) | collective-permute-done | bytes 786464 | tf_op jit(solution)/shard_map/ppermute | solution.py:409
  163.7 0.0 collective-permute-start.10
  163.7 0.0 collective-permute-done.8.a_twin
  163.7 2.3 %collective-permute-done.10.y_twin = f32[1536,128]{1,0:T(8,128)S(1)} collective-permute-done((f32[1536,128]{1,0:T(8,128)S(1)}, f32[1536,128]{1,0:T(8,128)S(1)}, u32[]{:S(2)}, u32[]{:S(2)}) %collective-permute-start.10) | collective-permute-done | bytes 786464 | tf_op jit(solution)/shard_map/ppermute | solution.py:214
  166.0 0.0 collective-permute-done.17.b_twin
  166.0 0.0 copy-done.7
  166.0 1.1 copy-done.9
  167.1 54.5 %chain.1 = (f32[64,1024]{1,0:T(8,128)}, f32[64,1024]{1,0:T(8,128)}) custom-call(s32[3]{0:T(128)S(1)} %pad_add_fusion.place, f32[1536,128]{1,0:T(8,128)S(1)} %pad_maximum_fusion.1.a_own, f32[1536,128]{1,0:T(8,128)S(1)} %collective-permute-done.8.a_twin, f32[1536,128]{1,0:T(8,128)S(1)} %collective-permute-done.9.y_own, ...), custom_call_target="tpu_custom_call" | custom-call | tf_op jit(solution)/shard_map/chain/pallas_call | solution.py:417
  (9 shorter events, 0.2 us)
Async XLA Ops:
  0.7 0.7 copy-start.5
  1.4 0.7 copy-start.6
  67.5 13.9 %copy-start = (bf16[512,1024]{1,0:T(8,128)(2,1)}, bf16[512,1024]{1,0:T(8,128)(2,1)S(1)}, u32[]{:S(2)}) copy-start(bf16[512,1024]{1,0:T(8,128)(2,1)S(1)} %get-tuple-element.12.ck) | copy-start | bytes 3145732
  67.5 16.8 %copy-start.2 = (bf16[512,1024]{1,0:T(8,128)(2,1)}, bf16[512,1024]{1,0:T(8,128)(2,1)S(1)}, u32[]{:S(2)}) copy-start(bf16[512,1024]{1,0:T(8,128)(2,1)S(1)} %get-tuple-element.10.pk) | copy-start | bytes 3145732
  67.5 3.0 %collective-permute-start.1 = (bf16[512,1024]{1,0:T(8,128)(2,1)}, bf16[512,1024]{1,0:T(8,128)(2,1)S(1)}, u32[]{:S(2)}, u32[]{:S(2)}) collective-permute-start(bf16[512,1024]{1,0:T(8,128)(2,1)} %get-tuple-element.13), channel_id=1, source_target_pairs={{0,1},{1,0},{2,3},{3,2},{4,5},{5,4},{6,7},{7,6},{8,9},{9,8},{10,11... | collective-permute-start | bytes 3145736 | tf_op jit(solution)/shard_map/ppermute | solution.py:214
  70.6 10.9 %copy-start.1 = (bf16[512,1024]{1,0:T(8,128)(2,1)}, bf16[512,1024]{1,0:T(8,128)(2,1)S(1)}, u32[]{:S(2)}) copy-start(bf16[512,1024]{1,0:T(8,128)(2,1)S(1)} %collective-permute-done.1.cr) | copy-start | bytes 3145732
  74.1 1.1 copy-start.3
  75.1 3.4 %collective-permute-start.11 = (f32[2560,128]{1,0:T(8,128)}, f32[2560,128]{1,0:T(8,128)}, u32[]{:S(2)}, u32[]{:S(2)}) collective-permute-start(f32[2560,128]{1,0:T(8,128)} %get-tuple-element.17), channel_id=1, source_target_pairs={{0,1},{1,0},{2,3},{3,2},{4,5},{5,4},{6,7},{7,6},{8,9},{9,8},{10,11... | collective-permute-start | bytes 3932168 | tf_op jit(solution)/shard_map/ppermute | solution.py:214
  75.5 8.8 %collective-permute-start = (bf16[512,1024]{1,0:T(8,128)(2,1)}, bf16[512,1024]{1,0:T(8,128)(2,1)}, u32[]{:S(2)}, u32[]{:S(2)}) collective-permute-start(bf16[512,1024]{1,0:T(8,128)(2,1)} %get-tuple-element.11), channel_id=1, source_target_pairs={{0,1},{1,0},{2,3},{3,2},{4,5},{5,4},{6,7},{7,6},{8,9},{9,8},{10,11... | collective-permute-start | bytes 3145736 | tf_op jit(solution)/shard_map/ppermute | solution.py:214
  78.5 5.8 %copy-start.4 = (bf16[64,2048]{1,0:T(8,128)(2,1)S(1)}, bf16[64,2048]{1,0:T(8,128)(2,1)}, u32[]{:S(2)}) copy-start(bf16[64,2048]{1,0:T(8,128)(2,1)} %start.1) | copy-start | bytes 786436
  81.5 11.7 %collective-permute-start.12 = (f32[1280,128]{1,0:T(8,128)}, f32[1280,128]{1,0:T(8,128)}, u32[]{:S(2)}, u32[]{:S(2)}) collective-permute-start(f32[1280,128]{1,0:T(8,128)} %get-tuple-element.19), channel_id=1, source_target_pairs={{0,2},{1,5},{2,0},{3,7},{4,6},{5,1},{6,4},{7,3},{8,10},{9,13},{10,... | collective-permute-start | bytes 1966088 | tf_op jit(solution)/shard_map/ppermute | solution.py:210
  84.3 8.9 %copy-start.8 = (f32[1280,128]{1,0:T(8,128)S(1)}, f32[1280,128]{1,0:T(8,128)}, u32[]{:S(2)}) copy-start(f32[1280,128]{1,0:T(8,128)} %get-tuple-element.18) | copy-start | bytes 1966084
  88.0 9.0 %collective-permute-start.2 = (f32[1536,128]{1,0:T(8,128)S(1)}, f32[1536,128]{1,0:T(8,128)S(1)}, u32[]{:S(2)}, u32[]{:S(2)}) collective-permute-start(f32[1536,128]{1,0:T(8,128)S(1)} %get-tuple-element.15), channel_id=1, source_target_pairs={{0,1},{1,0},{2,3},{3,2},{4,5},{5,4},{6,7},{7,6},{8,9},{9,8},{10,11... | collective-permute-start | bytes 2359304 | tf_op jit(solution)/shard_map/ppermute | solution.py:214
  94.9 10.2 %collective-permute-start.13 = (f32[640,128]{1,0:T(8,128)}, f32[640,128]{1,0:T(8,128)}, u32[]{:S(2)}, u32[]{:S(2)}) collective-permute-start(f32[640,128]{1,0:T(8,128)} %dynamic-slice_add_fusion.4), channel_id=1, source_target_pairs={{0,4},{1,3},{2,6},{3,1},{4,0},{5,7},{6,2},{7,5},{8,12},{9,11},{10,... | collective-permute-start | bytes 983048 | tf_op jit(solution)/shard_map/ppermute | solution.py:210
  97.9 12.0 %collective-permute-start.3 = (f32[768,128]{1,0:T(8,128)}, f32[768,128]{1,0:T(8,128)S(1)}, u32[]{:S(2)}, u32[]{:S(2)}) collective-permute-start(f32[768,128]{1,0:T(8,128)} %get-tuple-element.21), channel_id=1, source_target_pairs={{0,2},{1,5},{2,0},{3,7},{4,6},{5,1},{6,4},{7,3},{8,10},{9,13},{10,... | collective-permute-start | bytes 1179656 | tf_op jit(solution)/shard_map/ppermute | solution.py:210
  106.3 13.7 %collective-permute-start.14 = (f32[640,128]{1,0:T(8,128)S(1)}, f32[640,128]{1,0:T(8,128)S(1)}, u32[]{:S(2)}, u32[]{:S(2)}) collective-permute-start(f32[640,128]{1,0:T(8,128)S(1)} %add_add_fusion), channel_id=1, source_target_pairs={{0,8},{1,9},{2,10},{3,11},{4,12},{5,13},{6,14},{7,15},{8,0},{9,1},... | collective-permute-start | bytes 983048 | tf_op jit(solution)/shard_map/ppermute | solution.py:210
  110.0 13.5 %collective-permute-start.4 = (f32[384,128]{1,0:T(8,128)S(1)}, f32[384,128]{1,0:T(8,128)S(1)}, u32[]{:S(2)}, u32[]{:S(2)}) collective-permute-start(f32[384,128]{1,0:T(8,128)S(1)} %dynamic-slice_add_fusion.5), channel_id=1, source_target_pairs={{0,4},{1,3},{2,6},{3,1},{4,0},{5,7},{6,2},{7,5},{8,12},{9,11},{10,... | collective-permute-start | bytes 589832 | tf_op jit(solution)/shard_map/ppermute | solution.py:210
  120.1 14.7 %collective-permute-start.15 = (f32[640,128]{1,0:T(8,128)S(1)}, f32[640,128]{1,0:T(8,128)S(1)}, u32[]{:S(2)}, u32[]{:S(2)}) collective-permute-start(f32[640,128]{1,0:T(8,128)S(1)} %add.87), channel_id=1, source_target_pairs={{0,4},{1,3},{2,6},{3,1},{4,0},{5,7},{6,2},{7,5},{8,12},{9,11},{10,... | collective-permute-start | bytes 983048 | tf_op jit(solution)/shard_map/ppermute | solution.py:210
  123.5 7.1 %collective-permute-start.5 = (f32[384,128]{1,0:T(8,128)S(1)}, f32[384,128]{1,0:T(8,128)S(1)}, u32[]{:S(2)}, u32[]{:S(2)}) collective-permute-start(f32[384,128]{1,0:T(8,128)S(1)} %add_add_fusion.1), channel_id=1, source_target_pairs={{0,8},{1,9},{2,10},{3,11},{4,12},{5,13},{6,14},{7,15},{8,0},{9,1},... | collective-permute-start | bytes 589832 | tf_op jit(solution)/shard_map/ppermute | solution.py:210
  130.6 10.0 %collective-permute-start.6 = (f32[384,128]{1,0:T(8,128)S(1)}, f32[384,128]{1,0:T(8,128)S(1)}, u32[]{:S(2)}, u32[]{:S(2)}) collective-permute-start(f32[384,128]{1,0:T(8,128)S(1)} %add.77), channel_id=1, source_target_pairs={{0,4},{1,3},{2,6},{3,1},{4,0},{5,7},{6,2},{7,5},{8,12},{9,11},{10,... | collective-permute-start | bytes 589832 | tf_op jit(solution)/shard_map/ppermute | solution.py:210
  134.9 17.2 %collective-permute-start.16 = (f32[1280,128]{1,0:T(8,128)S(1)}, f32[1280,128]{1,0:T(8,128)S(1)}, u32[]{:S(2)}, u32[]{:S(2)}) collective-permute-start(f32[1280,128]{1,0:T(8,128)S(1)} %pad_maximum_fusion.2), channel_id=1, source_target_pairs={{0,2},{1,5},{2,0},{3,7},{4,6},{5,1},{6,4},{7,3},{8,10},{9,13},{10,... | collective-permute-start | bytes 1966088 | tf_op jit(solution)/shard_map/ppermute | solution.py:210
  140.7 9.7 %collective-permute-start.7 = (f32[768,128]{1,0:T(8,128)S(1)}, f32[768,128]{1,0:T(8,128)S(1)}, u32[]{:S(2)}, u32[]{:S(2)}) collective-permute-start(f32[768,128]{1,0:T(8,128)S(1)} %pad_maximum_fusion.3), channel_id=1, source_target_pairs={{0,2},{1,5},{2,0},{3,7},{4,6},{5,1},{6,4},{7,3},{8,10},{9,13},{10,... | collective-permute-start | bytes 1179656 | tf_op jit(solution)/shard_map/ppermute | solution.py:210
  150.4 13.2 %collective-permute-start.9 = (f32[1536,128]{1,0:T(8,128)S(1)}, f32[1536,128]{1,0:T(8,128)S(1)}, u32[]{:S(2)}, u32[]{:S(2)}) collective-permute-start(f32[1536,128]{1,0:T(8,128)S(1)} %pad_maximum_fusion.1.a_own), channel_id=1, source_target_pairs={{0,16},{16,0},{1,17},{17,1},{2,18},{18,2},{3,19},{19,3},{4,20},{20... | collective-permute-start | bytes 2359304 | tf_op jit(solution)/shard_map/ppermute | solution.py:409
  152.1 13.9 %copy-start.7 = (f32[2560,128]{1,0:T(8,128)}, f32[2560,128]{1,0:T(8,128)S(1)}, u32[]{:S(2)}) copy-start(f32[2560,128]{1,0:T(8,128)S(1)} %pad_maximum_fusion.b_own) | copy-start | bytes 3932164
  152.1 13.8 %collective-permute-start.17 = (f32[2560,128]{1,0:T(8,128)S(1)}, f32[2560,128]{1,0:T(8,128)S(1)}, u32[]{:S(2)}, u32[]{:S(2)}) collective-permute-start(f32[2560,128]{1,0:T(8,128)S(1)} %pad_maximum_fusion.b_own), channel_id=1, source_target_pairs={{0,1},{1,0},{2,3},{3,2},{4,5},{5,4},{6,7},{7,6},{8,9},{9,8},{10,11... | collective-permute-start | bytes 3932168 | tf_op jit(solution)/shard_map/ppermute | solution.py:214
  152.2 11.5 %collective-permute-start.8 = (f32[1536,128]{1,0:T(8,128)S(1)}, f32[1536,128]{1,0:T(8,128)S(1)}, u32[]{:S(2)}, u32[]{:S(2)}) collective-permute-start(f32[1536,128]{1,0:T(8,128)S(1)} %pad_maximum_fusion.1.a_own), channel_id=1, source_target_pairs={{0,1},{1,0},{2,3},{3,2},{4,5},{5,4},{6,7},{7,6},{8,9},{9,8},{10,11... | collective-permute-start | bytes 2359304 | tf_op jit(solution)/shard_map/ppermute | solution.py:214
  163.7 2.3 %collective-permute-start.10 = (f32[1536,128]{1,0:T(8,128)S(1)}, f32[1536,128]{1,0:T(8,128)S(1)}, u32[]{:S(2)}, u32[]{:S(2)}) collective-permute-start(f32[1536,128]{1,0:T(8,128)S(1)} %collective-permute-done.9.y_own), channel_id=1, source_target_pairs={{0,1},{1,0},{2,3},{3,2},{4,5},{5,4},{6,7},{7,6},{8,9},{9,8},{10,11... | collective-permute-start | bytes 2359304 | tf_op jit(solution)/shard_map/ppermute | solution.py:214
  166.0 1.1 copy-start.9

commit v2 on v1

--- a/solution.py
+++ b/solution.py
@@ -34,30 +34,38 @@
     return pltpu.CompilerParams(vmem_limit_bytes=VMEM_BYTES)
 
 
-def place_kernel(place, pred_map, cell_map, pred, cell, pred_keep, pred_send, cell_keep, cell_send, sems):
+def place_kernel(
+    place, pred_map, cell_map, pred, cell, pred_keep, pred_send, cell_keep, cell_send, pred_buf, cell_buf, sems, outs
+):
     day = place[0]
-    fields = ((pred_map, pred, pred_keep, pred_send), (cell_map, cell, cell_keep, cell_send))
-    for f, (tile_map, stored, keep, send) in enumerate(fields):
+    fields = ((pred_map, pred, pred_buf, pred_keep, pred_send), (cell_map, cell, cell_buf, cell_keep, cell_send))
+    loads = []
+    for f, (tile_map, stored, buf, keep, send) in enumerate(fields):
         number = tile_map.shape[0]
         half = number // 2
         for t in range(number):
             slot = lax.rem(lax.rem(tile_map[t], number) + half * day, number)
-            source = stored.at[:, pl.ds(t * LANES, LANES)]
-
-            @pl.when(slot < half)
-            def _():
-                to = pl.multiple_of(slot * LANES, LANES)
-                pltpu.make_async_copy(source, keep.at[:, pl.ds(to, LANES)], sems.at[f, t]).start()
-
-            @pl.when(slot >= half)
-            def _():
-                to = pl.multiple_of((slot - half) * LANES, LANES)
-                pltpu.make_async_copy(source, send.at[:, pl.ds(to, LANES)], sems.at[f, t]).start()
-
-    for f, (tile_map, stored, keep, send) in enumerate(fields):
-        for t in range(tile_map.shape[0]):
-            part = pl.ds(0, LANES)
-            pltpu.make_async_copy(stored.at[:, part], keep.at[:, part], sems.at[f, t]).wait()
+            to = pl.multiple_of(lax.rem(slot, half) * LANES, LANES)
+            loads.append(
+                pltpu.make_async_copy(
+                    stored.at[:, pl.ds(t * LANES, LANES)],
+                    buf.at[lax.div(slot, half), :, pl.ds(to, LANES)],
+                    sems.at[f, t],
+                )
+            )
+    for copy in loads:
+        copy.start()
+    stores = []
+    number = pred_map.shape[0]
+    for f, (tile_map, stored, buf, keep, send) in enumerate(fields):
+        for copy in loads[f * number : (f + 1) * number]:
+            copy.wait()
+        for n, target in ((1, send), (0, keep)):
+            copy = pltpu.make_async_copy(buf.at[n], target, outs.at[f, n])
+            copy.start()
+            stores.append(copy)
+    for copy in stores:
+        copy.wait()
 
 
 def place_tiles(place, pred_map, cell_map, pred, cell):
@@ -68,7 +76,12 @@
         out_shape=(half,) * 4,
         in_specs=[smem_spec()] * 3 + [any_spec()] * 2,
         out_specs=(any_spec(),) * 4,
-        scratch_shapes=[pltpu.SemaphoreType.DMA((2, pred_map.shape[0]))],
+        scratch_shapes=[
+            pltpu.VMEM((2, rows, width // 2), pred.dtype),
+            pltpu.VMEM((2, rows, width // 2), pred.dtype),
+            pltpu.SemaphoreType.DMA((2, pred_map.shape[0])),
+            pltpu.SemaphoreType.DMA((2, 2)),
+        ],
         compiler_params=params(),
         name="place_tiles",
     )(place, pred_map, cell_map, pred, cell)
@@ -129,7 +142,7 @@
     flush(scr, keep, send, outs)
 
 
-def second_gram_kernel(blocks, place, ck, cr, keep, send, cell, scr, sems, outs):
+def second_gram_kernel(blocks, place, ck, cr, after, keep, send, cell, scr, sems, outs):
     day = place[0]
     copies = load_days(ck, cr, cell, day, sems)
     for copy in copies:
@@ -173,7 +186,7 @@
     )(place, pk, pr, ck, cr, start)
 
 
-def second_gram(place, ck, cr):
+def second_gram(place, ck, cr, after):
     days, width = 2 * ck.shape[0], ck.shape[1]
     blocks = triangle(days)
     rows = len(blocks) // 2 * (BLOCK * BLOCK // LANES)
@@ -181,7 +194,7 @@
     return pl.pallas_call(
         functools.partial(second_gram_kernel, blocks),
         out_shape=(out, out),
-        in_specs=[smem_spec()] + [any_spec()] * 2,
+        in_specs=[smem_spec()] + [any_spec()] * 3,
         out_specs=(any_spec(), any_spec()),
         scratch_shapes=[
             pltpu.VMEM((days, width), BF16),
@@ -191,7 +204,7 @@
         ],
         compiler_params=params(),
         name="second_gram",
-    )(place, ck, cr)
+    )(place, ck, cr, after)
 
 
 def bit_orders(bits):
@@ -404,7 +417,7 @@
     pr = other_core(ps)
     cr = other_core(cs)
     a_keep, a_send = first_gram(place, pk, pr, ck, cr, start_panel)
-    b_keep, b_send = second_gram(place, ck, cr)
+    b_keep, b_send = second_gram(place, ck, cr, a_keep)
     a_own = sum_over_cells(a_keep, a_send)
     y_own = lax.ppermute(a_own, "group", [(0, 1), (1, 0)])
     b_own = sum_over_cells(b_keep, b_send)

time: 223 us -> 170 us (0.76)
  Pallas kernels: 127 us -> 65.7 us
  waiting for transfers between devices: 51.7 us -> 59.3 us
  local copies, waits for them, and re-layouts: 3.48 us -> 7.87 us
    pallas_call x1, Pallas kernels: 65.5 us -> 4.25 us  [place_tiles(): pl.pallas_call(place_kernel, out_shape=(half,) * 4, in_specs=[smem_spec()...]
    ppermute x10, waiting for transfers between devices: 33.1 us -> 39 us  [cell_exchange(): return lax.ppermute(value, ('cell', 'day'), pairs)]
    unnamed x20 -> x32, local copies, waits for them, and re-layouts: 3.48 us -> 7.87 us
  transfers between devices with their start and end apart: 18 -> 18, of which waited for: 10 -> 11; matrix products, arithmetic and copies ran while one was open for 3% -> 2% of each run, Pallas kernels for 2% -> 0%
where the time goes in v2:
time: 170 us
  Pallas kernels  65.7 us (39%)
  waiting for transfers between devices  59.3 us (35%)
  starting transfers between devices  30 us (18%)
  local copies, waits for them, and re-layouts  7.87 us (5%)
  other arithmetic  6.14 us (4%)
    pallas_call x1, Pallas kernels, local(): pl.pallas_call(functools.partial(chain_kernel, blocks, bits, orders, coun...  54.5 us
    ppermute x10, waiting for transfers between devices, cell_exchange(): return lax.ppermute(value, ('cell', 'day'), pairs)  39 us
    ppermute x10, starting transfers between devices, cell_exchange(): return lax.ppermute(value, ('cell', 'day'), pairs)  26.9 us
    ppermute x1, waiting for transfers between devices, local(): y_own = lax.ppermute(a_own, 'group', [(0, 1), (1, 0)])  11.4 us
    ppermute x7, waiting for transfers between devices, other_core(): return lax.ppermute(value, 'day', [(0, 1), (1, 0)])  8.89 us
    unnamed x32, local copies, waits for them, and re-layouts  7.87 us
    pallas_call x1, Pallas kernels, place_tiles(): pl.pallas_call(place_kernel, out_shape=(half,) * 4, in_specs=[smem_spec()...  4.25 us
    pallas_call x1, Pallas kernels, second_gram(): pl.pallas_call(functools.partial(second_gram_kernel, blocks), out_shape=(...  3.78 us
  transfers between devices with their start and end apart: 18, of which 11 were waited for; matrix products, arithmetic and copies ran while one was open for 2% of the time, Pallas kernels for 0%

profile of v2, /device:TPU:0, one launch (start us, length us, event | category | flops | bytes accessed | tf_op | source)
XLA Modules:
  0.0 170.0 jit_solution(1727427288012577622)
XLA Ops:
  0.6 0.1 pad_add_fusion.place
  0.7 0.7 copy-done.9
  1.4 0.7 copy-done.10
  2.0 4.3 %place_tiles.1 = (bf16[512,1024]{1,0:T(8,128)(2,1)S(1)}, bf16[512,1024]{1,0:T(8,128)(2,1)S(1)}, bf16[512,1024]{1,0:T(8,128)(2,1)S(1)}, bf16[512,1024]{1,0:T(8,128)(2,1)}) custom-call(s32[3]{0:T(128)S(1)} %pad_add_fusion.place, s32[16]{0:T(128)S(1)} %copy-done.9, s32[16]{0:T(128)S(1)} %copy-done.10, bf16[512,2048]{1,0:T(8,128)(2,1)} %pred_.1, ...), custom_call_target="tpu_custom_call" | custom-call | tf_op jit(solution)/shard_map/place_tiles/pallas_call | solution.py:74
  6.3 0.0 copy-start
  6.3 1.0 copy-done
  7.3 0.5 collective-permute-start.1
  7.7 0.1 collective-permute-start
  7.8 3.4 %collective-permute-done.1.cr = bf16[512,1024]{1,0:T(8,128)(2,1)S(1)} collective-permute-done((bf16[512,1024]{1,0:T(8,128)(2,1)}, bf16[512,1024]{1,0:T(8,128)(2,1)S(1)}, u32[]{:S(2)}, u32[]{:S(2)}) %collective-permute-start.1) | collective-permute-done | bytes 1048608 | tf_op jit(solution)/shard_map/ppermute | solution.py:227
  11.2 0.4 collective-permute-done.pr
  11.5 0.6 copy-done.2
  12.1 0.0 copy-done.8
  12.1 3.2 %first_gram.1 = (f32[1536,128]{1,0:T(8,128)S(1)}, f32[1536,128]{1,0:T(8,128)S(1)}) custom-call(s32[3]{0:T(128)S(1)} %pad_add_fusion.place, bf16[512,1024]{1,0:T(8,128)(2,1)S(1)} %get-tuple-element.10.pk, bf16[512,1024]{1,0:T(8,128)(2,1)S(1)} %collective-permute-done.pr, bf16[512,1024]{1,0:T(8,128)(2,1)} %copy-done, bf16[512,1024]{1,0:T(8,128)(2,1)} %copy-done.2, ...), custom_call_target="tpu_custom_call" | custom-call | tf_op jit(solution)/shard_map/first_gram/pallas_call | solution.py:171
  15.3 0.0 copy-done.5
  15.3 0.0 copy-start.4
  15.3 1.0 copy-done.4
  16.3 0.0 copy-done.1
  16.3 1.8 %copy-done.3 = bf16[512,1024]{1,0:T(8,128)(2,1)S(1)} copy-done((bf16[512,1024]{1,0:T(8,128)(2,1)S(1)}, bf16[512,1024]{1,0:T(8,128)(2,1)}, u32[]{:S(2)}) %copy-start.3) | copy-done | bytes 1048600
  18.1 3.8 %second_gram.1 = (f32[2560,128]{1,0:T(8,128)}, f32[2560,128]{1,0:T(8,128)}) custom-call(s32[3]{0:T(128)S(1)} %pad_add_fusion.place, bf16[512,1024]{1,0:T(8,128)(2,1)S(1)} %copy-done.1, bf16[512,1024]{1,0:T(8,128)(2,1)S(1)} %copy-done.3, f32[1536,128]{1,0:T(8,128)S(1)} %get-tuple-element.14.after), custom_call_target="tpu_custom_call" | custom-call | tf_op jit(solution)/shard_map/second_gram/pallas_call | solution.py:194
  21.9 0.0 copy-done.6
  21.9 0.0 copy-done.11
  21.9 0.4 collective-permute-start.11
  22.4 2.9 %collective-permute-done.11 = f32[2560,128]{1,0:T(8,128)S(1)} collective-permute-done((f32[2560,128]{1,0:T(8,128)}, f32[2560,128]{1,0:T(8,128)S(1)}, u32[]{:S(2)}, u32[]{:S(2)}) %collective-permute-start.11) | collective-permute-done | bytes 1310752 | tf_op jit(solution)/shard_map/ppermute | solution.py:227
  25.2 1.1 copy-done.15
  26.3 2.8 %dynamic-slice_add_fusion.1 = (f32[1280,128]{1,0:T(8,128)S(1)}, f32[1280,128]{1,0:T(8,128)}) fusion(f32[2560,128]{1,0:T(8,128)} %copy-done.15, s32[]{:T(128)S(6)} %select_n.47, f32[2560,128]{1,0:T(8,128)} %get-tuple-element.16, s32[]{:T(128)S(6)} %select_n.49), kind=kLoop, calls=%fused_computation.4 | loop fusion | flops 327680 | bytes 3932168 | tf_op jit(solution)/shard_map/add | solution.py:245
  29.1 3.4 %collective-permute-start.12 = (f32[1280,128]{1,0:T(8,128)}, f32[1280,128]{1,0:T(8,128)}, u32[]{:S(2)}, u32[]{:S(2)}) collective-permute-start(f32[1280,128]{1,0:T(8,128)} %get-tuple-element.19), channel_id=1, source_target_pairs={{0,2},{1,5},{2,0},{3,7},{4,6},{5,1},{6,4},{7,3},{8,10},{9,13},{10,... | collective-permute-start | bytes 1966088 | tf_op jit(solution)/shard_map/ppermute | solution.py:223
  32.5 0.0 copy-done.12
  32.5 0.0 collective-permute-start.2
  32.5 8.9 %collective-permute-done.12 = f32[1280,128]{1,0:T(8,128)} collective-permute-done((f32[1280,128]{1,0:T(8,128)}, f32[1280,128]{1,0:T(8,128)}, u32[]{:S(2)}, u32[]{:S(2)}) %collective-permute-start.12) | collective-permute-done | bytes 655392 | tf_op jit(solution)/shard_map/ppermute | solution.py:223
  41.4 1.7 %dynamic-slice_add_fusion.4 = f32[640,128]{1,0:T(8,128)} fusion(f32[1280,128]{1,0:T(8,128)} %collective-permute-done.12, s32[]{:T(128)S(6)} %select_n.50, f32[1280,128]{1,0:T(8,128)S(1)} %get-tuple-element.18), kind=kLoop, calls=%fused_computation.8 | loop fusion | flops 81920 | bytes 983044 | tf_op jit(solution)/shard_map/add | solution.py:243
  43.1 2.1 %collective-permute-start.13 = (f32[640,128]{1,0:T(8,128)}, f32[640,128]{1,0:T(8,128)}, u32[]{:S(2)}, u32[]{:S(2)}) collective-permute-start(f32[640,128]{1,0:T(8,128)} %dynamic-slice_add_fusion.4), channel_id=1, source_target_pairs={{0,4},{1,3},{2,6},{3,1},{4,0},{5,7},{6,2},{7,5},{8,12},{9,11},{10,... | collective-permute-start | bytes 983048 | tf_op jit(solution)/shard_map/ppermute | solution.py:223
  45.2 0.0 collective-permute-done.2
  45.2 0.0 copy-done.7
  45.2 0.1 dynamic-slice_add_fusion.3
  45.3 1.6 collective-permute-start.3
  46.9 7.2 %collective-permute-done.13 = f32[640,128]{1,0:T(8,128)} collective-permute-done((f32[640,128]{1,0:T(8,128)}, f32[640,128]{1,0:T(8,128)}, u32[]{:S(2)}, u32[]{:S(2)}) %collective-permute-start.13) | collective-permute-done | bytes 327712 | tf_op jit(solution)/shard_map/ppermute | solution.py:223
  54.1 1.2 add_add_fusion
  55.3 3.0 %collective-permute-start.14 = (f32[640,128]{1,0:T(8,128)S(1)}, f32[640,128]{1,0:T(8,128)S(1)}, u32[]{:S(2)}, u32[]{:S(2)}) collective-permute-start(f32[640,128]{1,0:T(8,128)S(1)} %add_add_fusion), channel_id=1, source_target_pairs={{0,8},{1,9},{2,10},{3,11},{4,12},{5,13},{6,14},{7,15},{8,0},{9,1},... | collective-permute-start | bytes 983048 | tf_op jit(solution)/shard_map/ppermute | solution.py:223
  58.3 0.0 collective-permute-done.3
  58.3 1.6 collective-permute-start.4
  60.0 8.5 %collective-permute-done.14 = f32[640,128]{1,0:T(8,128)S(1)} collective-permute-done((f32[640,128]{1,0:T(8,128)S(1)}, f32[640,128]{1,0:T(8,128)S(1)}, u32[]{:S(2)}, u32[]{:S(2)}) %collective-permute-start.14) | collective-permute-done | bytes 327712 | tf_op jit(solution)/shard_map/ppermute | solution.py:223
  68.5 0.8 collective-permute-start.15
  69.3 0.0 collective-permute-done.4
  69.4 3.4 %collective-permute-start.5 = (f32[384,128]{1,0:T(8,128)S(1)}, f32[384,128]{1,0:T(8,128)S(1)}, u32[]{:S(2)}, u32[]{:S(2)}) collective-permute-start(f32[384,128]{1,0:T(8,128)S(1)} %add_add_fusion.1), channel_id=1, source_target_pairs={{0,8},{1,9},{2,10},{3,11},{4,12},{5,13},{6,14},{7,15},{8,0},{9,1},... | collective-permute-start | bytes 589832 | tf_op jit(solution)/shard_map/ppermute | solution.py:223
  72.8 4.8 %collective-permute-done.5 = f32[384,128]{1,0:T(8,128)S(1)} collective-permute-done((f32[384,128]{1,0:T(8,128)S(1)}, f32[384,128]{1,0:T(8,128)S(1)}, u32[]{:S(2)}, u32[]{:S(2)}) %collective-permute-start.5) | collective-permute-done | bytes 196640 | tf_op jit(solution)/shard_map/ppermute | solution.py:223
  77.6 4.6 %collective-permute-start.6 = (f32[384,128]{1,0:T(8,128)S(1)}, f32[384,128]{1,0:T(8,128)S(1)}, u32[]{:S(2)}, u32[]{:S(2)}) collective-permute-start(f32[384,128]{1,0:T(8,128)S(1)} %add.77), channel_id=1, source_target_pairs={{0,4},{1,3},{2,6},{3,1},{4,0},{5,7},{6,2},{7,5},{8,12},{9,11},{10,... | collective-permute-start | bytes 589832 | tf_op jit(solution)/shard_map/ppermute | solution.py:223
  82.2 0.0 collective-permute-done.15
  82.2 3.1 %collective-permute-start.16 = (f32[1280,128]{1,0:T(8,128)S(1)}, f32[1280,128]{1,0:T(8,128)S(1)}, u32[]{:S(2)}, u32[]{:S(2)}) collective-permute-start(f32[1280,128]{1,0:T(8,128)S(1)} %pad_maximum_fusion.2), channel_id=1, source_target_pairs={{0,2},{1,5},{2,0},{3,7},{4,6},{5,1},{6,4},{7,3},{8,10},{9,13},{10,... | collective-permute-start | bytes 1966088 | tf_op jit(solution)/shard_map/ppermute | solution.py:223
  85.4 2.6 %collective-permute-done.6 = f32[384,128]{1,0:T(8,128)S(1)} collective-permute-done((f32[384,128]{1,0:T(8,128)S(1)}, f32[384,128]{1,0:T(8,128)S(1)}, u32[]{:S(2)}, u32[]{:S(2)}) %collective-permute-start.6) | collective-permute-done | bytes 196640 | tf_op jit(solution)/shard_map/ppermute | solution.py:223
  88.0 3.1 %collective-permute-start.7 = (f32[768,128]{1,0:T(8,128)S(1)}, f32[768,128]{1,0:T(8,128)S(1)}, u32[]{:S(2)}, u32[]{:S(2)}) collective-permute-start(f32[768,128]{1,0:T(8,128)S(1)} %pad_maximum_fusion.3), channel_id=1, source_target_pairs={{0,2},{1,5},{2,0},{3,7},{4,6},{5,1},{6,4},{7,3},{8,10},{9,13},{10,... | collective-permute-start | bytes 1179656 | tf_op jit(solution)/shard_map/ppermute | solution.py:223
  91.2 7.0 %collective-permute-done.7 = f32[768,128]{1,0:T(8,128)S(1)} collective-permute-done((f32[768,128]{1,0:T(8,128)S(1)}, f32[768,128]{1,0:T(8,128)S(1)}, u32[]{:S(2)}, u32[]{:S(2)}) %collective-permute-start.7) | collective-permute-done | bytes 393248 | tf_op jit(solution)/shard_map/ppermute | solution.py:223
  98.2 0.1 pad_maximum_fusion.1.a_own
  98.2 1.6 collective-permute-start.9
  99.8 0.0 collective-permute-done.16
  99.8 0.1 pad_maximum_fusion.b_own
  99.9 0.1 collective-permute-start.17
  100.0 0.5 collective-permute-start.8
  100.5 11.4 %collective-permute-done.9.y_own = f32[1536,128]{1,0:T(8,128)S(1)} collective-permute-done((f32[1536,128]{1,0:T(8,128)S(1)}, f32[1536,128]{1,0:T(8,128)S(1)}, u32[]{:S(2)}, u32[]{:S(2)}) %collective-permute-start.9) | collective-permute-done | bytes 786464 | tf_op jit(solution)/shard_map/ppermute | solution.py:422
  111.9 0.0 collective-permute-start.10
  111.9 0.0 collective-permute-done.8.a_twin
  111.9 2.3 %collective-permute-done.10.y_twin = f32[1536,128]{1,0:T(8,128)S(1)} collective-permute-done((f32[1536,128]{1,0:T(8,128)S(1)}, f32[1536,128]{1,0:T(8,128)S(1)}, u32[]{:S(2)}, u32[]{:S(2)}) %collective-permute-start.10) | collective-permute-done | bytes 786464 | tf_op jit(solution)/shard_map/ppermute | solution.py:227
  114.2 0.0 collective-permute-done.17.b_twin
  114.2 1.1 copy-done.14
  115.3 54.5 %chain.1 = (f32[64,1024]{1,0:T(8,128)}, f32[64,1024]{1,0:T(8,128)}) custom-call(s32[3]{0:T(128)S(1)} %pad_add_fusion.place, f32[1536,128]{1,0:T(8,128)S(1)} %pad_maximum_fusion.1.a_own, f32[1536,128]{1,0:T(8,128)S(1)} %collective-permute-done.8.a_twin, f32[1536,128]{1,0:T(8,128)S(1)} %collective-permute-done.9.y_own, ...), custom_call_target="tpu_custom_call" | custom-call | tf_op jit(solution)/shard_map/chain/pallas_call | solution.py:430
  (21 shorter events, 0.2 us)
Async XLA Ops:
  0.7 0.7 copy-start.9
  1.4 0.7 copy-start.10
  2.0 10.1 %copy-start.8 = (bf16[64,2048]{1,0:T(8,128)(2,1)S(1)}, bf16[64,2048]{1,0:T(8,128)(2,1)}, u32[]{:S(2)}) copy-start(bf16[64,2048]{1,0:T(8,128)(2,1)} %start.1) | copy-start | bytes 786436
  6.3 1.0 copy-start
  7.3 3.9 %collective-permute-start.1 = (bf16[512,1024]{1,0:T(8,128)(2,1)}, bf16[512,1024]{1,0:T(8,128)(2,1)S(1)}, u32[]{:S(2)}, u32[]{:S(2)}) collective-permute-start(bf16[512,1024]{1,0:T(8,128)(2,1)} %get-tuple-element.13), channel_id=1, source_target_pairs={{0,1},{1,0},{2,3},{3,2},{4,5},{5,4},{6,7},{7,6},{8,9},{9,8},{10,11... | collective-permute-start | bytes 3145736 | tf_op jit(solution)/shard_map/ppermute | solution.py:227
  7.7 3.8 %collective-permute-start = (bf16[512,1024]{1,0:T(8,128)(2,1)S(1)}, bf16[512,1024]{1,0:T(8,128)(2,1)S(1)}, u32[]{:S(2)}, u32[]{:S(2)}) collective-permute-start(bf16[512,1024]{1,0:T(8,128)(2,1)S(1)} %get-tuple-element.11), channel_id=1, source_target_pairs={{0,1},{1,0},{2,3},{3,2},{4,5},{5,4},{6,7},{7,6},{8,9},{9,8},{10,11... | collective-permute-start | bytes 3145736 | tf_op jit(solution)/shard_map/ppermute | solution.py:227
  11.2 1.0 copy-start.2
  11.5 3.8 %copy-start.5 = (bf16[512,1024]{1,0:T(8,128)(2,1)}, bf16[512,1024]{1,0:T(8,128)(2,1)S(1)}, u32[]{:S(2)}) copy-start(bf16[512,1024]{1,0:T(8,128)(2,1)S(1)} %collective-permute-done.pr) | copy-start | bytes 3145732
  12.1 4.2 %copy-start.1 = (bf16[512,1024]{1,0:T(8,128)(2,1)S(1)}, bf16[512,1024]{1,0:T(8,128)(2,1)}, u32[]{:S(2)}) copy-start(bf16[512,1024]{1,0:T(8,128)(2,1)} %copy-done) | copy-start | bytes 3145732
  15.3 1.0 copy-start.4
  16.3 5.6 %copy-start.6 = (f32[1536,128]{1,0:T(8,128)}, f32[1536,128]{1,0:T(8,128)S(1)}, u32[]{:S(2)}) copy-start(f32[1536,128]{1,0:T(8,128)S(1)} %get-tuple-element.14.after) | copy-start | bytes 2359300
  16.3 5.6 %copy-start.11 = (f32[1536,128]{1,0:T(8,128)}, f32[1536,128]{1,0:T(8,128)S(1)}, u32[]{:S(2)}) copy-start(f32[1536,128]{1,0:T(8,128)S(1)} %get-tuple-element.15) | copy-start | bytes 2359300
  16.3 1.8 %copy-start.3 = (bf16[512,1024]{1,0:T(8,128)(2,1)S(1)}, bf16[512,1024]{1,0:T(8,128)(2,1)}, u32[]{:S(2)}) copy-start(bf16[512,1024]{1,0:T(8,128)(2,1)} %copy-done.2) | copy-start | bytes 3145732
  21.9 3.3 %collective-permute-start.11 = (f32[2560,128]{1,0:T(8,128)}, f32[2560,128]{1,0:T(8,128)S(1)}, u32[]{:S(2)}, u32[]{:S(2)}) collective-permute-start(f32[2560,128]{1,0:T(8,128)} %get-tuple-element.17), channel_id=1, source_target_pairs={{0,1},{1,0},{2,3},{3,2},{4,5},{5,4},{6,7},{7,6},{8,9},{9,8},{10,11... | collective-permute-start | bytes 3932168 | tf_op jit(solution)/shard_map/ppermute | solution.py:227
  25.2 1.1 copy-start.15
  26.3 6.2 %copy-start.12 = (f32[1536,128]{1,0:T(8,128)S(1)}, f32[1536,128]{1,0:T(8,128)}, u32[]{:S(2)}) copy-start(f32[1536,128]{1,0:T(8,128)} %copy-done.11) | copy-start | bytes 2359300
  29.1 16.1 %copy-start.7 = (f32[1536,128]{1,0:T(8,128)S(1)}, f32[1536,128]{1,0:T(8,128)}, u32[]{:S(2)}) copy-start(f32[1536,128]{1,0:T(8,128)} %copy-done.6) | copy-start | bytes 2359300
  29.1 12.3 %collective-permute-start.12 = (f32[1280,128]{1,0:T(8,128)}, f32[1280,128]{1,0:T(8,128)}, u32[]{:S(2)}, u32[]{:S(2)}) collective-permute-start(f32[1280,128]{1,0:T(8,128)} %get-tuple-element.19), channel_id=1, source_target_pairs={{0,2},{1,5},{2,0},{3,7},{4,6},{5,1},{6,4},{7,3},{8,10},{9,13},{10,... | collective-permute-start | bytes 1966088 | tf_op jit(solution)/shard_map/ppermute | solution.py:223
  32.5 12.7 %collective-permute-start.2 = (f32[1536,128]{1,0:T(8,128)S(1)}, f32[1536,128]{1,0:T(8,128)S(1)}, u32[]{:S(2)}, u32[]{:S(2)}) collective-permute-start(f32[1536,128]{1,0:T(8,128)S(1)} %copy-done.12), channel_id=1, source_target_pairs={{0,1},{1,0},{2,3},{3,2},{4,5},{5,4},{6,7},{7,6},{8,9},{9,8},{10,11... | collective-permute-start | bytes 2359304 | tf_op jit(solution)/shard_map/ppermute | solution.py:227
  43.1 11.0 %collective-permute-start.13 = (f32[640,128]{1,0:T(8,128)}, f32[640,128]{1,0:T(8,128)}, u32[]{:S(2)}, u32[]{:S(2)}) collective-permute-start(f32[640,128]{1,0:T(8,128)} %dynamic-slice_add_fusion.4), channel_id=1, source_target_pairs={{0,4},{1,3},{2,6},{3,1},{4,0},{5,7},{6,2},{7,5},{8,12},{9,11},{10,... | collective-permute-start | bytes 983048 | tf_op jit(solution)/shard_map/ppermute | solution.py:223
  45.3 13.0 %collective-permute-start.3 = (f32[768,128]{1,0:T(8,128)S(1)}, f32[768,128]{1,0:T(8,128)S(1)}, u32[]{:S(2)}, u32[]{:S(2)}) collective-permute-start(f32[768,128]{1,0:T(8,128)S(1)} %get-tuple-element.21), channel_id=1, source_target_pairs={{0,2},{1,5},{2,0},{3,7},{4,6},{5,1},{6,4},{7,3},{8,10},{9,13},{10,... | collective-permute-start | bytes 1179656 | tf_op jit(solution)/shard_map/ppermute | solution.py:223
  55.3 13.2 %collective-permute-start.14 = (f32[640,128]{1,0:T(8,128)S(1)}, f32[640,128]{1,0:T(8,128)S(1)}, u32[]{:S(2)}, u32[]{:S(2)}) collective-permute-start(f32[640,128]{1,0:T(8,128)S(1)} %add_add_fusion), channel_id=1, source_target_pairs={{0,8},{1,9},{2,10},{3,11},{4,12},{5,13},{6,14},{7,15},{8,0},{9,1},... | collective-permute-start | bytes 983048 | tf_op jit(solution)/shard_map/ppermute | solution.py:223
  58.3 11.0 %collective-permute-start.4 = (f32[384,128]{1,0:T(8,128)S(1)}, f32[384,128]{1,0:T(8,128)S(1)}, u32[]{:S(2)}, u32[]{:S(2)}) collective-permute-start(f32[384,128]{1,0:T(8,128)S(1)} %dynamic-slice_add_fusion.5), channel_id=1, source_target_pairs={{0,4},{1,3},{2,6},{3,1},{4,0},{5,7},{6,2},{7,5},{8,12},{9,11},{10,... | collective-permute-start | bytes 589832 | tf_op jit(solution)/shard_map/ppermute | solution.py:223
  68.5 13.7 %collective-permute-start.15 = (f32[640,128]{1,0:T(8,128)S(1)}, f32[640,128]{1,0:T(8,128)S(1)}, u32[]{:S(2)}, u32[]{:S(2)}) collective-permute-start(f32[640,128]{1,0:T(8,128)S(1)} %add.87), channel_id=1, source_target_pairs={{0,4},{1,3},{2,6},{3,1},{4,0},{5,7},{6,2},{7,5},{8,12},{9,11},{10,... | collective-permute-start | bytes 983048 | tf_op jit(solution)/shard_map/ppermute | solution.py:223
  69.4 8.2 %collective-permute-start.5 = (f32[384,128]{1,0:T(8,128)S(1)}, f32[384,128]{1,0:T(8,128)S(1)}, u32[]{:S(2)}, u32[]{:S(2)}) collective-permute-start(f32[384,128]{1,0:T(8,128)S(1)} %add_add_fusion.1), channel_id=1, source_target_pairs={{0,8},{1,9},{2,10},{3,11},{4,12},{5,13},{6,14},{7,15},{8,0},{9,1},... | collective-permute-start | bytes 589832 | tf_op jit(solution)/shard_map/ppermute | solution.py:223
  77.6 10.4 %collective-permute-start.6 = (f32[384,128]{1,0:T(8,128)S(1)}, f32[384,128]{1,0:T(8,128)S(1)}, u32[]{:S(2)}, u32[]{:S(2)}) collective-permute-start(f32[384,128]{1,0:T(8,128)S(1)} %add.77), channel_id=1, source_target_pairs={{0,4},{1,3},{2,6},{3,1},{4,0},{5,7},{6,2},{7,5},{8,12},{9,11},{10,... | collective-permute-start | bytes 589832 | tf_op jit(solution)/shard_map/ppermute | solution.py:223
  82.2 17.6 %collective-permute-start.16 = (f32[1280,128]{1,0:T(8,128)S(1)}, f32[1280,128]{1,0:T(8,128)S(1)}, u32[]{:S(2)}, u32[]{:S(2)}) collective-permute-start(f32[1280,128]{1,0:T(8,128)S(1)} %pad_maximum_fusion.2), channel_id=1, source_target_pairs={{0,2},{1,5},{2,0},{3,7},{4,6},{5,1},{6,4},{7,3},{8,10},{9,13},{10,... | collective-permute-start | bytes 1966088 | tf_op jit(solution)/shard_map/ppermute | solution.py:223
  88.0 10.1 %collective-permute-start.7 = (f32[768,128]{1,0:T(8,128)S(1)}, f32[768,128]{1,0:T(8,128)S(1)}, u32[]{:S(2)}, u32[]{:S(2)}) collective-permute-start(f32[768,128]{1,0:T(8,128)S(1)} %pad_maximum_fusion.3), channel_id=1, source_target_pairs={{0,2},{1,5},{2,0},{3,7},{4,6},{5,1},{6,4},{7,3},{8,10},{9,13},{10,... | collective-permute-start | bytes 1179656 | tf_op jit(solution)/shard_map/ppermute | solution.py:223
  98.2 13.7 %collective-permute-start.9 = (f32[1536,128]{1,0:T(8,128)S(1)}, f32[1536,128]{1,0:T(8,128)S(1)}, u32[]{:S(2)}, u32[]{:S(2)}) collective-permute-start(f32[1536,128]{1,0:T(8,128)S(1)} %pad_maximum_fusion.1.a_own), channel_id=1, source_target_pairs={{0,16},{16,0},{1,17},{17,1},{2,18},{18,2},{3,19},{19,3},{4,20},{20... | collective-permute-start | bytes 2359304 | tf_op jit(solution)/shard_map/ppermute | solution.py:422
  99.9 14.3 %copy-start.13 = (f32[2560,128]{1,0:T(8,128)}, f32[2560,128]{1,0:T(8,128)S(1)}, u32[]{:S(2)}) copy-start(f32[2560,128]{1,0:T(8,128)S(1)} %pad_maximum_fusion.b_own) | copy-start | bytes 3932164
  99.9 14.3 %collective-permute-start.17 = (f32[2560,128]{1,0:T(8,128)S(1)}, f32[2560,128]{1,0:T(8,128)S(1)}, u32[]{:S(2)}, u32[]{:S(2)}) collective-permute-start(f32[2560,128]{1,0:T(8,128)S(1)} %pad_maximum_fusion.b_own), channel_id=1, source_target_pairs={{0,1},{1,0},{2,3},{3,2},{4,5},{5,4},{6,7},{7,6},{8,9},{9,8},{10,11... | collective-permute-start | bytes 3932168 | tf_op jit(solution)/shard_map/ppermute | solution.py:227
  100.0 11.9 %collective-permute-start.8 = (f32[1536,128]{1,0:T(8,128)S(1)}, f32[1536,128]{1,0:T(8,128)S(1)}, u32[]{:S(2)}, u32[]{:S(2)}) collective-permute-start(f32[1536,128]{1,0:T(8,128)S(1)} %pad_maximum_fusion.1.a_own), channel_id=1, source_target_pairs={{0,1},{1,0},{2,3},{3,2},{4,5},{5,4},{6,7},{7,6},{8,9},{9,8},{10,11... | collective-permute-start | bytes 2359304 | tf_op jit(solution)/shard_map/ppermute | solution.py:227
  111.9 2.3 %collective-permute-start.10 = (f32[1536,128]{1,0:T(8,128)S(1)}, f32[1536,128]{1,0:T(8,128)S(1)}, u32[]{:S(2)}, u32[]{:S(2)}) collective-permute-start(f32[1536,128]{1,0:T(8,128)S(1)} %collective-permute-done.9.y_own), channel_id=1, source_target_pairs={{0,1},{1,0},{2,3},{3,2},{4,5},{5,4},{6,7},{7,6},{8,9},{9,8},{10,11... | collective-permute-start | bytes 2359304 | tf_op jit(solution)/shard_map/ppermute | solution.py:227
  114.2 1.1 copy-start.14

commit v3 on v2

--- a/solution.py
+++ b/solution.py
@@ -11,6 +11,7 @@
 LANES = 128
 BLOCK = 256
 SPLITS = 3
+SUB = 8
 F32 = jnp.float32
 BF16 = jnp.bfloat16
 NT = (((1,), (1,)), ((), ()))
@@ -299,20 +300,44 @@
 
 
 def inverse_factor(moments):
-    k_rows = moments.shape[0]
-    row_ids = lax.broadcasted_iota(jnp.int32, (k_rows, k_rows), 0)
-    col_ids = lax.broadcasted_iota(jnp.int32, (k_rows, k_rows), 1)
-    work = jnp.concatenate([moments, (row_ids == col_ids).astype(F32)], axis=1)
-    below = lax.broadcasted_iota(jnp.int32, (k_rows, 1), 0)
-    scale = jnp.ones((k_rows, 1), F32)
-    for k in range(k_rows):
-        row = work[k : k + 1, :]
-        column = work[:, k : k + 1]
-        pivot = work[k : k + 1, k : k + 1]
-        factor = jnp.where(below > k, column / pivot, 0.0)
-        scale = jnp.where(below == k, 1.0 / jnp.sqrt(pivot), scale)
-        work = work - factor * row
-    return work[:, k_rows:] * scale
+    size = moments.shape[0]
+    row_ids = lax.broadcasted_iota(jnp.int32, (size, size), 0)
+    col_ids = lax.broadcasted_iota(jnp.int32, (size, size), 1)
+    work = jnp.concatenate([(row_ids == col_ids).astype(F32), moments], axis=1)
+    shape = (SUB, 2 * size)
+    sub = lax.broadcasted_iota(jnp.int32, shape, 0)
+    rows = [work[SUB * i : SUB * i + SUB, :] for i in range(size // SUB)]
+    out = []
+    for b in range(size // SUB):
+        lane = size + SUB * b
+        head = rows[b]
+        cols = [jnp.broadcast_to(head[:, lane + c : lane + c + 1], shape) for c in range(SUB)]
+        entry = [[jnp.broadcast_to(cols[c][r : r + 1, :], shape) for c in range(r + 1)] for r in range(SUB)]
+        y = [jnp.broadcast_to(head[r : r + 1, :], shape) for r in range(SUB)]
+        inverse = []
+        factor = [[None] * SUB for _ in range(SUB)]
+        for k in range(SUB):
+            inverse.append(1.0 / entry[k][k])
+            for i in range(k + 1, SUB):
+                factor[i][k] = entry[i][k] * inverse[k]
+                for j in range(k + 1, i + 1):
+                    entry[i][j] = entry[i][j] - factor[i][k] * entry[j][k]
+                y[i] = y[i] - factor[i][k] * y[k]
+        p = [y[k] * inverse[k] for k in range(SUB)]
+        for i in reversed(range(SUB)):
+            for k in range(i):
+                p[k] = p[k] - factor[i][k] * p[i]
+        for i in range(b + 1, size // SUB):
+            terms = [jnp.broadcast_to(rows[i][:, lane + k : lane + k + 1], shape) * p[k] for k in range(SUB)]
+            while len(terms) > 1:
+                terms = [terms[t] + terms[t + 1] for t in range(0, len(terms), 2)]
+            rows[i] = rows[i] - terms[0]
+        result, pivot = y[0], entry[0][0]
+        for k in range(1, SUB):
+            result = jnp.where(sub == k, y[k], result)
+            pivot = jnp.where(sub == k, entry[k][k], pivot)
+        out.append(result * (1.0 / jnp.sqrt(pivot)))
+    return jnp.concatenate(out, axis=0)[:, :size]
 
 
 def half_step(scores, gram, cells):

time: 170 us -> 149 us (0.88)
  Pallas kernels: 65.7 us -> 44.2 us
    pallas_call x1, Pallas kernels: 54.5 us -> 32.9 us  [local(): pl.pallas_call(functools.partial(chain_kernel, blocks, bits, orders, coun...]
where the time goes in v3:
time: 149 us; the launch traced here: 148 us
  waiting for transfers between devices  59.3 us (40%)
  Pallas kernels  44.2 us (30%)
  starting transfers between devices  30 us (20%)
  local copies, waits for them, and re-layouts  7.87 us (5%)
  other arithmetic  6.14 us (4%)
    ppermute x10, waiting for transfers between devices, cell_exchange(): return lax.ppermute(value, ('cell', 'day'), pairs)  39 us
    pallas_call x1, Pallas kernels, local(): pl.pallas_call(functools.partial(chain_kernel, blocks, bits, orders, coun...  32.9 us
    ppermute x10, starting transfers between devices, cell_exchange(): return lax.ppermute(value, ('cell', 'day'), pairs)  26.9 us
    ppermute x1, waiting for transfers between devices, local(): y_own = lax.ppermute(a_own, 'group', [(0, 1), (1, 0)])  11.4 us
    ppermute x7, waiting for transfers between devices, other_core(): return lax.ppermute(value, 'day', [(0, 1), (1, 0)])  8.89 us
    unnamed x32, local copies, waits for them, and re-layouts  7.87 us
    pallas_call x1, Pallas kernels, place_tiles(): pl.pallas_call(place_kernel, out_shape=(half,) * 4, in_specs=[smem_spec()...  4.25 us
    pallas_call x1, Pallas kernels, second_gram(): pl.pallas_call(functools.partial(second_gram_kernel, blocks), out_shape=(...  3.78 us
  transfers between devices with their start and end apart: 18, of which 11 were waited for; matrix products, arithmetic and copies ran while one was open for 2% of the time, Pallas kernels for 0%

profile of v3, /device:TPU:0, one launch (start us, length us, event | category | flops | bytes accessed | tf_op | source)
XLA Modules:
  0.0 148.4 jit_solution(4622135312174211552)
XLA Ops:
  0.6 0.1 pad_add_fusion.place
  0.7 0.7 copy-done.9
  1.4 0.7 copy-done.10
  2.0 4.3 %place_tiles.1 = (bf16[512,1024]{1,0:T(8,128)(2,1)S(1)}, bf16[512,1024]{1,0:T(8,128)(2,1)S(1)}, bf16[512,1024]{1,0:T(8,128)(2,1)S(1)}, bf16[512,1024]{1,0:T(8,128)(2,1)}) custom-call(s32[3]{0:T(128)S(1)} %pad_add_fusion.place, s32[16]{0:T(128)S(1)} %copy-done.9, s32[16]{0:T(128)S(1)} %copy-done.10, bf16[512,2048]{1,0:T(8,128)(2,1)} %pred_.1, ...), custom_call_target="tpu_custom_call" | custom-call | tf_op jit(solution)/shard_map/place_tiles/pallas_call | solution.py:75
  6.3 0.0 copy-start
  6.3 1.0 copy-done
  7.3 0.5 collective-permute-start.1
  7.7 0.1 collective-permute-start
  7.8 3.4 %collective-permute-done.1.cr = bf16[512,1024]{1,0:T(8,128)(2,1)S(1)} collective-permute-done((bf16[512,1024]{1,0:T(8,128)(2,1)}, bf16[512,1024]{1,0:T(8,128)(2,1)S(1)}, u32[]{:S(2)}, u32[]{:S(2)}) %collective-permute-start.1) | collective-permute-done | bytes 1048608 | tf_op jit(solution)/shard_map/ppermute | solution.py:228
  11.2 0.4 collective-permute-done.pr
  11.5 0.6 copy-done.2
  12.1 0.0 copy-done.8
  12.1 3.2 %first_gram.1 = (f32[1536,128]{1,0:T(8,128)S(1)}, f32[1536,128]{1,0:T(8,128)S(1)}) custom-call(s32[3]{0:T(128)S(1)} %pad_add_fusion.place, bf16[512,1024]{1,0:T(8,128)(2,1)S(1)} %get-tuple-element.10.pk, bf16[512,1024]{1,0:T(8,128)(2,1)S(1)} %collective-permute-done.pr, bf16[512,1024]{1,0:T(8,128)(2,1)} %copy-done, bf16[512,1024]{1,0:T(8,128)(2,1)} %copy-done.2, ...), custom_call_target="tpu_custom_call" | custom-call | tf_op jit(solution)/shard_map/first_gram/pallas_call | solution.py:172
  15.3 0.0 copy-done.5
  15.3 0.0 copy-start.4
  15.3 1.0 copy-done.4
  16.3 0.0 copy-done.1
  16.3 1.8 %copy-done.3 = bf16[512,1024]{1,0:T(8,128)(2,1)S(1)} copy-done((bf16[512,1024]{1,0:T(8,128)(2,1)S(1)}, bf16[512,1024]{1,0:T(8,128)(2,1)}, u32[]{:S(2)}) %copy-start.3) | copy-done | bytes 1048600
  18.1 3.8 %second_gram.1 = (f32[2560,128]{1,0:T(8,128)}, f32[2560,128]{1,0:T(8,128)}) custom-call(s32[3]{0:T(128)S(1)} %pad_add_fusion.place, bf16[512,1024]{1,0:T(8,128)(2,1)S(1)} %copy-done.1, bf16[512,1024]{1,0:T(8,128)(2,1)S(1)} %copy-done.3, f32[1536,128]{1,0:T(8,128)S(1)} %get-tuple-element.14.after), custom_call_target="tpu_custom_call" | custom-call | tf_op jit(solution)/shard_map/second_gram/pallas_call | solution.py:195
  21.9 0.0 copy-done.6
  21.9 0.0 copy-done.11
  21.9 0.4 collective-permute-start.11
  22.4 2.9 %collective-permute-done.11 = f32[2560,128]{1,0:T(8,128)S(1)} collective-permute-done((f32[2560,128]{1,0:T(8,128)}, f32[2560,128]{1,0:T(8,128)S(1)}, u32[]{:S(2)}, u32[]{:S(2)}) %collective-permute-start.11) | collective-permute-done | bytes 1310752 | tf_op jit(solution)/shard_map/ppermute | solution.py:228
  25.2 1.1 copy-done.15
  26.3 2.8 %dynamic-slice_add_fusion.1 = (f32[1280,128]{1,0:T(8,128)S(1)}, f32[1280,128]{1,0:T(8,128)}) fusion(f32[2560,128]{1,0:T(8,128)} %copy-done.15, s32[]{:T(128)S(6)} %select_n.47, f32[2560,128]{1,0:T(8,128)} %get-tuple-element.16, s32[]{:T(128)S(6)} %select_n.49), kind=kLoop, calls=%fused_computation.4 | loop fusion | flops 327680 | bytes 3932168 | tf_op jit(solution)/shard_map/add | solution.py:246
  29.1 3.4 %collective-permute-start.12 = (f32[1280,128]{1,0:T(8,128)}, f32[1280,128]{1,0:T(8,128)}, u32[]{:S(2)}, u32[]{:S(2)}) collective-permute-start(f32[1280,128]{1,0:T(8,128)} %get-tuple-element.19), channel_id=1, source_target_pairs={{0,2},{1,5},{2,0},{3,7},{4,6},{5,1},{6,4},{7,3},{8,10},{9,13},{10,... | collective-permute-start | bytes 1966088 | tf_op jit(solution)/shard_map/ppermute | solution.py:224
  32.5 0.0 copy-done.12
  32.5 0.0 collective-permute-start.2
  32.5 8.9 %collective-permute-done.12 = f32[1280,128]{1,0:T(8,128)} collective-permute-done((f32[1280,128]{1,0:T(8,128)}, f32[1280,128]{1,0:T(8,128)}, u32[]{:S(2)}, u32[]{:S(2)}) %collective-permute-start.12) | collective-permute-done | bytes 655392 | tf_op jit(solution)/shard_map/ppermute | solution.py:224
  41.4 1.7 %dynamic-slice_add_fusion.4 = f32[640,128]{1,0:T(8,128)} fusion(f32[1280,128]{1,0:T(8,128)} %collective-permute-done.12, s32[]{:T(128)S(6)} %select_n.50, f32[1280,128]{1,0:T(8,128)S(1)} %get-tuple-element.18), kind=kLoop, calls=%fused_computation.8 | loop fusion | flops 81920 | bytes 983044 | tf_op jit(solution)/shard_map/add | solution.py:244
  43.1 2.1 %collective-permute-start.13 = (f32[640,128]{1,0:T(8,128)}, f32[640,128]{1,0:T(8,128)}, u32[]{:S(2)}, u32[]{:S(2)}) collective-permute-start(f32[640,128]{1,0:T(8,128)} %dynamic-slice_add_fusion.4), channel_id=1, source_target_pairs={{0,4},{1,3},{2,6},{3,1},{4,0},{5,7},{6,2},{7,5},{8,12},{9,11},{10,... | collective-permute-start | bytes 983048 | tf_op jit(solution)/shard_map/ppermute | solution.py:224
  45.2 0.0 collective-permute-done.2
  45.2 0.0 copy-done.7
  45.2 0.1 dynamic-slice_add_fusion.3
  45.3 1.6 %collective-permute-start.3 = (f32[768,128]{1,0:T(8,128)S(1)}, f32[768,128]{1,0:T(8,128)S(1)}, u32[]{:S(2)}, u32[]{:S(2)}) collective-permute-start(f32[768,128]{1,0:T(8,128)S(1)} %get-tuple-element.21), channel_id=1, source_target_pairs={{0,2},{1,5},{2,0},{3,7},{4,6},{5,1},{6,4},{7,3},{8,10},{9,13},{10,... | collective-permute-start | bytes 1179656 | tf_op jit(solution)/shard_map/ppermute | solution.py:224
  46.9 7.2 %collective-permute-done.13 = f32[640,128]{1,0:T(8,128)} collective-permute-done((f32[640,128]{1,0:T(8,128)}, f32[640,128]{1,0:T(8,128)}, u32[]{:S(2)}, u32[]{:S(2)}) %collective-permute-start.13) | collective-permute-done | bytes 327712 | tf_op jit(solution)/shard_map/ppermute | solution.py:224
  54.1 1.2 add_add_fusion
  55.3 3.0 %collective-permute-start.14 = (f32[640,128]{1,0:T(8,128)S(1)}, f32[640,128]{1,0:T(8,128)S(1)}, u32[]{:S(2)}, u32[]{:S(2)}) collective-permute-start(f32[640,128]{1,0:T(8,128)S(1)} %add_add_fusion), channel_id=1, source_target_pairs={{0,8},{1,9},{2,10},{3,11},{4,12},{5,13},{6,14},{7,15},{8,0},{9,1},... | collective-permute-start | bytes 983048 | tf_op jit(solution)/shard_map/ppermute | solution.py:224
  58.3 0.0 collective-permute-done.3
  58.3 1.6 %collective-permute-start.4 = (f32[384,128]{1,0:T(8,128)S(1)}, f32[384,128]{1,0:T(8,128)S(1)}, u32[]{:S(2)}, u32[]{:S(2)}) collective-permute-start(f32[384,128]{1,0:T(8,128)S(1)} %dynamic-slice_add_fusion.5), channel_id=1, source_target_pairs={{0,4},{1,3},{2,6},{3,1},{4,0},{5,7},{6,2},{7,5},{8,12},{9,11},{10,... | collective-permute-start | bytes 589832 | tf_op jit(solution)/shard_map/ppermute | solution.py:224
  60.0 8.5 %collective-permute-done.14 = f32[640,128]{1,0:T(8,128)S(1)} collective-permute-done((f32[640,128]{1,0:T(8,128)S(1)}, f32[640,128]{1,0:T(8,128)S(1)}, u32[]{:S(2)}, u32[]{:S(2)}) %collective-permute-start.14) | collective-permute-done | bytes 327712 | tf_op jit(solution)/shard_map/ppermute | solution.py:224
  68.5 0.8 collective-permute-start.15
  69.3 0.0 collective-permute-done.4
  69.4 3.4 %collective-permute-start.5 = (f32[384,128]{1,0:T(8,128)S(1)}, f32[384,128]{1,0:T(8,128)S(1)}, u32[]{:S(2)}, u32[]{:S(2)}) collective-permute-start(f32[384,128]{1,0:T(8,128)S(1)} %add_add_fusion.1), channel_id=1, source_target_pairs={{0,8},{1,9},{2,10},{3,11},{4,12},{5,13},{6,14},{7,15},{8,0},{9,1},... | collective-permute-start | bytes 589832 | tf_op jit(solution)/shard_map/ppermute | solution.py:224
  72.8 4.8 %collective-permute-done.5 = f32[384,128]{1,0:T(8,128)S(1)} collective-permute-done((f32[384,128]{1,0:T(8,128)S(1)}, f32[384,128]{1,0:T(8,128)S(1)}, u32[]{:S(2)}, u32[]{:S(2)}) %collective-permute-start.5) | collective-permute-done | bytes 196640 | tf_op jit(solution)/shard_map/ppermute | solution.py:224
  77.6 4.6 %collective-permute-start.6 = (f32[384,128]{1,0:T(8,128)S(1)}, f32[384,128]{1,0:T(8,128)S(1)}, u32[]{:S(2)}, u32[]{:S(2)}) collective-permute-start(f32[384,128]{1,0:T(8,128)S(1)} %add.77), channel_id=1, source_target_pairs={{0,4},{1,3},{2,6},{3,1},{4,0},{5,7},{6,2},{7,5},{8,12},{9,11},{10,... | collective-permute-start | bytes 589832 | tf_op jit(solution)/shard_map/ppermute | solution.py:224
  82.2 0.0 collective-permute-done.15
  82.2 3.1 %collective-permute-start.16 = (f32[1280,128]{1,0:T(8,128)S(1)}, f32[1280,128]{1,0:T(8,128)S(1)}, u32[]{:S(2)}, u32[]{:S(2)}) collective-permute-start(f32[1280,128]{1,0:T(8,128)S(1)} %pad_maximum_fusion.2), channel_id=1, source_target_pairs={{0,2},{1,5},{2,0},{3,7},{4,6},{5,1},{6,4},{7,3},{8,10},{9,13},{10,... | collective-permute-start | bytes 1966088 | tf_op jit(solution)/shard_map/ppermute | solution.py:224
  85.4 2.6 %collective-permute-done.6 = f32[384,128]{1,0:T(8,128)S(1)} collective-permute-done((f32[384,128]{1,0:T(8,128)S(1)}, f32[384,128]{1,0:T(8,128)S(1)}, u32[]{:S(2)}, u32[]{:S(2)}) %collective-permute-start.6) | collective-permute-done | bytes 196640 | tf_op jit(solution)/shard_map/ppermute | solution.py:224
  88.0 3.1 %collective-permute-start.7 = (f32[768,128]{1,0:T(8,128)S(1)}, f32[768,128]{1,0:T(8,128)S(1)}, u32[]{:S(2)}, u32[]{:S(2)}) collective-permute-start(f32[768,128]{1,0:T(8,128)S(1)} %pad_maximum_fusion.3), channel_id=1, source_target_pairs={{0,2},{1,5},{2,0},{3,7},{4,6},{5,1},{6,4},{7,3},{8,10},{9,13},{10,... | collective-permute-start | bytes 1179656 | tf_op jit(solution)/shard_map/ppermute | solution.py:224
  91.2 7.0 %collective-permute-done.7 = f32[768,128]{1,0:T(8,128)S(1)} collective-permute-done((f32[768,128]{1,0:T(8,128)S(1)}, f32[768,128]{1,0:T(8,128)S(1)}, u32[]{:S(2)}, u32[]{:S(2)}) %collective-permute-start.7) | collective-permute-done | bytes 393248 | tf_op jit(solution)/shard_map/ppermute | solution.py:224
  98.2 0.1 pad_maximum_fusion.1.a_own
  98.2 1.6 %collective-permute-start.9 = (f32[1536,128]{1,0:T(8,128)S(1)}, f32[1536,128]{1,0:T(8,128)S(1)}, u32[]{:S(2)}, u32[]{:S(2)}) collective-permute-start(f32[1536,128]{1,0:T(8,128)S(1)} %pad_maximum_fusion.1.a_own), channel_id=1, source_target_pairs={{0,16},{16,0},{1,17},{17,1},{2,18},{18,2},{3,19},{19,3},{4,20},{20... | collective-permute-start | bytes 2359304 | tf_op jit(solution)/shard_map/ppermute | solution.py:447
  99.8 0.0 collective-permute-done.16
  99.8 0.1 pad_maximum_fusion.b_own
  99.9 0.1 collective-permute-start.17
  100.0 0.5 collective-permute-start.8
  100.5 11.4 %collective-permute-done.9.y_own = f32[1536,128]{1,0:T(8,128)S(1)} collective-permute-done((f32[1536,128]{1,0:T(8,128)S(1)}, f32[1536,128]{1,0:T(8,128)S(1)}, u32[]{:S(2)}, u32[]{:S(2)}) %collective-permute-start.9) | collective-permute-done | bytes 786464 | tf_op jit(solution)/shard_map/ppermute | solution.py:447
  111.9 0.0 collective-permute-start.10
  111.9 0.0 collective-permute-done.8.a_twin
  111.9 2.3 %collective-permute-done.10.y_twin = f32[1536,128]{1,0:T(8,128)S(1)} collective-permute-done((f32[1536,128]{1,0:T(8,128)S(1)}, f32[1536,128]{1,0:T(8,128)S(1)}, u32[]{:S(2)}, u32[]{:S(2)}) %collective-permute-start.10) | collective-permute-done | bytes 786464 | tf_op jit(solution)/shard_map/ppermute | solution.py:228
  114.2 0.0 collective-permute-done.17.b_twin
  114.2 1.1 copy-done.14
  115.3 32.9 %chain.1 = (f32[64,1024]{1,0:T(8,128)}, f32[64,1024]{1,0:T(8,128)}) custom-call(s32[3]{0:T(128)S(1)} %pad_add_fusion.place, f32[1536,128]{1,0:T(8,128)S(1)} %pad_maximum_fusion.1.a_own, f32[1536,128]{1,0:T(8,128)S(1)} %collective-permute-done.8.a_twin, f32[1536,128]{1,0:T(8,128)S(1)} %collective-permute-done.9.y_own, ...), custom_call_target="tpu_custom_call" | custom-call | tf_op jit(solution)/shard_map/chain/pallas_call | solution.py:455
  (21 shorter events, 0.2 us)
Async XLA Ops:
  0.7 0.7 copy-start.9
  1.4 0.7 copy-start.10
  2.0 10.1 %copy-start.8 = (bf16[64,2048]{1,0:T(8,128)(2,1)S(1)}, bf16[64,2048]{1,0:T(8,128)(2,1)}, u32[]{:S(2)}) copy-start(bf16[64,2048]{1,0:T(8,128)(2,1)} %start.1) | copy-start | bytes 786436
  6.3 1.0 copy-start
  7.3 3.9 %collective-permute-start.1 = (bf16[512,1024]{1,0:T(8,128)(2,1)}, bf16[512,1024]{1,0:T(8,128)(2,1)S(1)}, u32[]{:S(2)}, u32[]{:S(2)}) collective-permute-start(bf16[512,1024]{1,0:T(8,128)(2,1)} %get-tuple-element.13), channel_id=1, source_target_pairs={{0,1},{1,0},{2,3},{3,2},{4,5},{5,4},{6,7},{7,6},{8,9},{9,8},{10,11... | collective-permute-start | bytes 3145736 | tf_op jit(solution)/shard_map/ppermute | solution.py:228
  7.7 3.8 %collective-permute-start = (bf16[512,1024]{1,0:T(8,128)(2,1)S(1)}, bf16[512,1024]{1,0:T(8,128)(2,1)S(1)}, u32[]{:S(2)}, u32[]{:S(2)}) collective-permute-start(bf16[512,1024]{1,0:T(8,128)(2,1)S(1)} %get-tuple-element.11), channel_id=1, source_target_pairs={{0,1},{1,0},{2,3},{3,2},{4,5},{5,4},{6,7},{7,6},{8,9},{9,8},{10,11... | collective-permute-start | bytes 3145736 | tf_op jit(solution)/shard_map/ppermute | solution.py:228
  11.2 1.0 copy-start.2
  11.5 3.8 %copy-start.5 = (bf16[512,1024]{1,0:T(8,128)(2,1)}, bf16[512,1024]{1,0:T(8,128)(2,1)S(1)}, u32[]{:S(2)}) copy-start(bf16[512,1024]{1,0:T(8,128)(2,1)S(1)} %collective-permute-done.pr) | copy-start | bytes 3145732
  12.1 4.2 %copy-start.1 = (bf16[512,1024]{1,0:T(8,128)(2,1)S(1)}, bf16[512,1024]{1,0:T(8,128)(2,1)}, u32[]{:S(2)}) copy-start(bf16[512,1024]{1,0:T(8,128)(2,1)} %copy-done) | copy-start | bytes 3145732
  15.3 1.0 copy-start.4
  16.3 5.6 %copy-start.6 = (f32[1536,128]{1,0:T(8,128)}, f32[1536,128]{1,0:T(8,128)S(1)}, u32[]{:S(2)}) copy-start(f32[1536,128]{1,0:T(8,128)S(1)} %get-tuple-element.14.after) | copy-start | bytes 2359300
  16.3 5.6 %copy-start.11 = (f32[1536,128]{1,0:T(8,128)}, f32[1536,128]{1,0:T(8,128)S(1)}, u32[]{:S(2)}) copy-start(f32[1536,128]{1,0:T(8,128)S(1)} %get-tuple-element.15) | copy-start | bytes 2359300
  16.3 1.8 %copy-start.3 = (bf16[512,1024]{1,0:T(8,128)(2,1)S(1)}, bf16[512,1024]{1,0:T(8,128)(2,1)}, u32[]{:S(2)}) copy-start(bf16[512,1024]{1,0:T(8,128)(2,1)} %copy-done.2) | copy-start | bytes 3145732
  21.9 3.3 %collective-permute-start.11 = (f32[2560,128]{1,0:T(8,128)}, f32[2560,128]{1,0:T(8,128)S(1)}, u32[]{:S(2)}, u32[]{:S(2)}) collective-permute-start(f32[2560,128]{1,0:T(8,128)} %get-tuple-element.17), channel_id=1, source_target_pairs={{0,1},{1,0},{2,3},{3,2},{4,5},{5,4},{6,7},{7,6},{8,9},{9,8},{10,11... | collective-permute-start | bytes 3932168 | tf_op jit(solution)/shard_map/ppermute | solution.py:228
  25.2 1.1 copy-start.15
  26.3 6.2 %copy-start.12 = (f32[1536,128]{1,0:T(8,128)S(1)}, f32[1536,128]{1,0:T(8,128)}, u32[]{:S(2)}) copy-start(f32[1536,128]{1,0:T(8,128)} %copy-done.11) | copy-start | bytes 2359300
  29.1 16.1 %copy-start.7 = (f32[1536,128]{1,0:T(8,128)S(1)}, f32[1536,128]{1,0:T(8,128)}, u32[]{:S(2)}) copy-start(f32[1536,128]{1,0:T(8,128)} %copy-done.6) | copy-start | bytes 2359300
  29.1 12.3 %collective-permute-start.12 = (f32[1280,128]{1,0:T(8,128)}, f32[1280,128]{1,0:T(8,128)}, u32[]{:S(2)}, u32[]{:S(2)}) collective-permute-start(f32[1280,128]{1,0:T(8,128)} %get-tuple-element.19), channel_id=1, source_target_pairs={{0,2},{1,5},{2,0},{3,7},{4,6},{5,1},{6,4},{7,3},{8,10},{9,13},{10,... | collective-permute-start | bytes 1966088 | tf_op jit(solution)/shard_map/ppermute | solution.py:224
  32.5 12.7 %collective-permute-start.2 = (f32[1536,128]{1,0:T(8,128)S(1)}, f32[1536,128]{1,0:T(8,128)S(1)}, u32[]{:S(2)}, u32[]{:S(2)}) collective-permute-start(f32[1536,128]{1,0:T(8,128)S(1)} %copy-done.12), channel_id=1, source_target_pairs={{0,1},{1,0},{2,3},{3,2},{4,5},{5,4},{6,7},{7,6},{8,9},{9,8},{10,11... | collective-permute-start | bytes 2359304 | tf_op jit(solution)/shard_map/ppermute | solution.py:228
  43.1 11.0 %collective-permute-start.13 = (f32[640,128]{1,0:T(8,128)}, f32[640,128]{1,0:T(8,128)}, u32[]{:S(2)}, u32[]{:S(2)}) collective-permute-start(f32[640,128]{1,0:T(8,128)} %dynamic-slice_add_fusion.4), channel_id=1, source_target_pairs={{0,4},{1,3},{2,6},{3,1},{4,0},{5,7},{6,2},{7,5},{8,12},{9,11},{10,... | collective-permute-start | bytes 983048 | tf_op jit(solution)/shard_map/ppermute | solution.py:224
  45.3 13.0 %collective-permute-start.3 = (f32[768,128]{1,0:T(8,128)S(1)}, f32[768,128]{1,0:T(8,128)S(1)}, u32[]{:S(2)}, u32[]{:S(2)}) collective-permute-start(f32[768,128]{1,0:T(8,128)S(1)} %get-tuple-element.21), channel_id=1, source_target_pairs={{0,2},{1,5},{2,0},{3,7},{4,6},{5,1},{6,4},{7,3},{8,10},{9,13},{10,... | collective-permute-start | bytes 1179656 | tf_op jit(solution)/shard_map/ppermute | solution.py:224
  55.3 13.2 %collective-permute-start.14 = (f32[640,128]{1,0:T(8,128)S(1)}, f32[640,128]{1,0:T(8,128)S(1)}, u32[]{:S(2)}, u32[]{:S(2)}) collective-permute-start(f32[640,128]{1,0:T(8,128)S(1)} %add_add_fusion), channel_id=1, source_target_pairs={{0,8},{1,9},{2,10},{3,11},{4,12},{5,13},{6,14},{7,15},{8,0},{9,1},... | collective-permute-start | bytes 983048 | tf_op jit(solution)/shard_map/ppermute | solution.py:224
  58.3 11.0 %collective-permute-start.4 = (f32[384,128]{1,0:T(8,128)S(1)}, f32[384,128]{1,0:T(8,128)S(1)}, u32[]{:S(2)}, u32[]{:S(2)}) collective-permute-start(f32[384,128]{1,0:T(8,128)S(1)} %dynamic-slice_add_fusion.5), channel_id=1, source_target_pairs={{0,4},{1,3},{2,6},{3,1},{4,0},{5,7},{6,2},{7,5},{8,12},{9,11},{10,... | collective-permute-start | bytes 589832 | tf_op jit(solution)/shard_map/ppermute | solution.py:224
  68.5 13.7 %collective-permute-start.15 = (f32[640,128]{1,0:T(8,128)S(1)}, f32[640,128]{1,0:T(8,128)S(1)}, u32[]{:S(2)}, u32[]{:S(2)}) collective-permute-start(f32[640,128]{1,0:T(8,128)S(1)} %add.87), channel_id=1, source_target_pairs={{0,4},{1,3},{2,6},{3,1},{4,0},{5,7},{6,2},{7,5},{8,12},{9,11},{10,... | collective-permute-start | bytes 983048 | tf_op jit(solution)/shard_map/ppermute | solution.py:224
  69.4 8.2 %collective-permute-start.5 = (f32[384,128]{1,0:T(8,128)S(1)}, f32[384,128]{1,0:T(8,128)S(1)}, u32[]{:S(2)}, u32[]{:S(2)}) collective-permute-start(f32[384,128]{1,0:T(8,128)S(1)} %add_add_fusion.1), channel_id=1, source_target_pairs={{0,8},{1,9},{2,10},{3,11},{4,12},{5,13},{6,14},{7,15},{8,0},{9,1},... | collective-permute-start | bytes 589832 | tf_op jit(solution)/shard_map/ppermute | solution.py:224
  77.6 10.4 %collective-permute-start.6 = (f32[384,128]{1,0:T(8,128)S(1)}, f32[384,128]{1,0:T(8,128)S(1)}, u32[]{:S(2)}, u32[]{:S(2)}) collective-permute-start(f32[384,128]{1,0:T(8,128)S(1)} %add.77), channel_id=1, source_target_pairs={{0,4},{1,3},{2,6},{3,1},{4,0},{5,7},{6,2},{7,5},{8,12},{9,11},{10,... | collective-permute-start | bytes 589832 | tf_op jit(solution)/shard_map/ppermute | solution.py:224
  82.2 17.6 %collective-permute-start.16 = (f32[1280,128]{1,0:T(8,128)S(1)}, f32[1280,128]{1,0:T(8,128)S(1)}, u32[]{:S(2)}, u32[]{:S(2)}) collective-permute-start(f32[1280,128]{1,0:T(8,128)S(1)} %pad_maximum_fusion.2), channel_id=1, source_target_pairs={{0,2},{1,5},{2,0},{3,7},{4,6},{5,1},{6,4},{7,3},{8,10},{9,13},{10,... | collective-permute-start | bytes 1966088 | tf_op jit(solution)/shard_map/ppermute | solution.py:224
  88.0 10.1 %collective-permute-start.7 = (f32[768,128]{1,0:T(8,128)S(1)}, f32[768,128]{1,0:T(8,128)S(1)}, u32[]{:S(2)}, u32[]{:S(2)}) collective-permute-start(f32[768,128]{1,0:T(8,128)S(1)} %pad_maximum_fusion.3), channel_id=1, source_target_pairs={{0,2},{1,5},{2,0},{3,7},{4,6},{5,1},{6,4},{7,3},{8,10},{9,13},{10,... | collective-permute-start | bytes 1179656 | tf_op jit(solution)/shard_map/ppermute | solution.py:224
  98.2 13.7 %collective-permute-start.9 = (f32[1536,128]{1,0:T(8,128)S(1)}, f32[1536,128]{1,0:T(8,128)S(1)}, u32[]{:S(2)}, u32[]{:S(2)}) collective-permute-start(f32[1536,128]{1,0:T(8,128)S(1)} %pad_maximum_fusion.1.a_own), channel_id=1, source_target_pairs={{0,16},{16,0},{1,17},{17,1},{2,18},{18,2},{3,19},{19,3},{4,20},{20... | collective-permute-start | bytes 2359304 | tf_op jit(solution)/shard_map/ppermute | solution.py:447
  99.9 14.3 %copy-start.13 = (f32[2560,128]{1,0:T(8,128)}, f32[2560,128]{1,0:T(8,128)S(1)}, u32[]{:S(2)}) copy-start(f32[2560,128]{1,0:T(8,128)S(1)} %pad_maximum_fusion.b_own) | copy-start | bytes 3932164
  99.9 14.3 %collective-permute-start.17 = (f32[2560,128]{1,0:T(8,128)S(1)}, f32[2560,128]{1,0:T(8,128)S(1)}, u32[]{:S(2)}, u32[]{:S(2)}) collective-permute-start(f32[2560,128]{1,0:T(8,128)S(1)} %pad_maximum_fusion.b_own), channel_id=1, source_target_pairs={{0,1},{1,0},{2,3},{3,2},{4,5},{5,4},{6,7},{7,6},{8,9},{9,8},{10,11... | collective-permute-start | bytes 3932168 | tf_op jit(solution)/shard_map/ppermute | solution.py:228
  100.0 11.9 %collective-permute-start.8 = (f32[1536,128]{1,0:T(8,128)S(1)}, f32[1536,128]{1,0:T(8,128)S(1)}, u32[]{:S(2)}, u32[]{:S(2)}) collective-permute-start(f32[1536,128]{1,0:T(8,128)S(1)} %pad_maximum_fusion.1.a_own), channel_id=1, source_target_pairs={{0,1},{1,0},{2,3},{3,2},{4,5},{5,4},{6,7},{7,6},{8,9},{9,8},{10,11... | collective-permute-start | bytes 2359304 | tf_op jit(solution)/shard_map/ppermute | solution.py:228
  111.9 2.3 %collective-permute-start.10 = (f32[1536,128]{1,0:T(8,128)S(1)}, f32[1536,128]{1,0:T(8,128)S(1)}, u32[]{:S(2)}, u32[]{:S(2)}) collective-permute-start(f32[1536,128]{1,0:T(8,128)S(1)} %collective-permute-done.9.y_own), channel_id=1, source_target_pairs={{0,1},{1,0},{2,3},{3,2},{4,5},{5,4},{6,7},{7,6},{8,9},{9,8},{10,11... | collective-permute-start | bytes 2359304 | tf_op jit(solution)/shard_map/ppermute | solution.py:228
  114.2 1.1 copy-start.14

commit v4 on v0

v4 whole, which is shorter than its diff:
```python
import functools

import jax
import jax.numpy as jnp
from jax import lax
from jax.experimental import pallas as pl
from jax.experimental.pallas import tpu as pltpu
from jax.sharding import PartitionSpec as P

ITERS = 3
LANES = 128
UNIT = 128
SPLITS = 3
SUB = 8
F32 = jnp.float32
BF16 = jnp.bfloat16
NT = (((1,), (1,)), ((), ()))
VMEM_BYTES = 56 * 1024 * 1024


def own_blocks(count):
    return [(i, j) for i in range(count) for j in range(i, count)]


def shares(count):
    own = own_blocks(count)
    cross = [(i, j) for i in range(count) for j in range(count // 2)]
    return [
        (own[: len(own) // 2], cross[: len(cross) // 2]),
        (own[len(own) // 2 :], cross[len(cross) // 2 :]),
    ]


def padded(rows, bits):
    step = SUB << (bits - 1)
    return -(-rows // step) * step


def first_rows(count, height, bits):
    own, cross = shares(count)[0]
    return padded((len(own) + len(cross)) * UNIT + count * height, bits)


def second_rows(count, bits):
    return padded((len(own_blocks(count)) + count * (count // 2)) * UNIT, bits)


def any_spec():
    return pl.BlockSpec(memory_space=pl.ANY)


def smem_spec():
    return pl.BlockSpec(memory_space=pltpu.SMEM)


def params():
    return pltpu.CompilerParams(vmem_limit_bytes=VMEM_BYTES)


def start_all(copies):
    for copy in copies:
        copy.start()


def wait_all(copies):
    for copy in copies:
        copy.wait()


def load_days(keep, recv, whole, day, sems):
    rows = keep.shape[0]
    return [
        pltpu.make_async_copy(keep, whole.at[pl.ds(pl.multiple_of(day * rows, rows), rows), :], sems.at[0]),
        pltpu.make_async_copy(recv, whole.at[pl.ds(pl.multiple_of((1 - day) * rows, rows), rows), :], sems.at[1]),
    ]


def first_bit(orders, day, cell):
    return jnp.where(day == 0, (cell >> orders[0][0]) & 1, (cell >> orders[1][0]) & 1)


def flush(scr, home, away, bit, sems):
    rows = home.shape[0]
    copies = [
        pltpu.make_async_copy(scr.at[pl.ds(pl.multiple_of((1 - bit) * rows, SUB), rows), :], away, sems.at[0]),
        pltpu.make_async_copy(scr.at[pl.ds(pl.multiple_of(bit * rows, SUB), rows), :], home, sems.at[1]),
    ]
    start_all(copies)
    wait_all(copies)


def rows_at(whole, block):
    return whole[pl.ds(pl.multiple_of(block * UNIT, UNIT), UNIT), :]


def first_gram_kernel(orders, place, cell_map, pred_own, pred_recv, cell_own, start, home, away,
                      pred, cell, panel, scr, sems, tile_sems, outs):
    day, group, index = place[0], place[1], place[2]
    number = cell_map.shape[0]
    height = panel.shape[0]
    tiles = []
    for t in range(number):
        slot = pl.multiple_of(lax.rem(cell_map[t], number) * LANES, LANES)
        tiles.append(
            pltpu.make_async_copy(
                start.at[:, pl.ds(slot, LANES)], panel.at[:, pl.ds(t * LANES, LANES)], tile_sems.at[t]
            )
        )
    data = load_days(pred_own, pred_recv, pred, day, sems)
    field = pltpu.make_async_copy(cell_own, cell, sems.at[2])
    start_all(data)
    field.start()
    start_all(tiles)
    count = cell.shape[0] // UNIT
    (own0, cross0), (own1, cross1) = shares(count)
    row = 0
    wait_all(data)
    for (i0, j0), (i1, j1) in zip(own0, own1):
        left = rows_at(pred, day * count + i0 + group * (i1 - i0))
        right = rows_at(pred, day * count + j0 + group * (j1 - j0))
        scr[row : row + UNIT, :] = lax.dot_general(left, right, NT, preferred_element_type=F32)
        row += UNIT
    for (i0, j0), (i1, j1) in zip(cross0, cross1):
        left = rows_at(pred, i0 + group * (i1 - i0))
        right = rows_at(pred, count + day * (count // 2) + j0 + group * (j1 - j0))
        scr[row : row + UNIT, :] = lax.dot_general(left, right, NT, preferred_element_type=F32)
        row += UNIT
    field.wait()
    wait_all(tiles)
    scores = lax.dot_general(panel[...], cell[...], NT, preferred_element_type=F32)
    for c in range(count):
        scr[row : row + height, :] = scores[:, c * LANES : (c + 1) * LANES]
        row += height
    flush(scr, home, away, first_bit(orders, day, index), outs)


def second_gram_kernel(orders, place, cell_own, cell_recv, after, home, away, cell, scr, sems, outs):
    day, index = place[0], place[2]
    data = load_days(cell_own, cell_recv, cell, day, sems)
    start_all(data)
    wait_all(data)
    rows = cell_own.shape[0]
    count = rows // UNIT
    row = 0
    base = pl.multiple_of(day * rows, rows)
    for i in range(count):
        width = (count - i) * UNIT
        right = cell[pl.ds(base + i * UNIT, width), :]
        value = lax.dot_general(right[:UNIT, :], right, NT, preferred_element_type=F32)
        for c in range(count - i):
            scr[row : row + UNIT, :] = value[:, c * UNIT : (c + 1) * UNIT]
            row += UNIT
    side = rows // 2
    right = cell[pl.ds(rows + pl.multiple_of(day * side, side), side), :]
    value = lax.dot_general(cell[:rows, :], right, NT, preferred_element_type=F32)
    for i in range(count):
        for j in range(count // 2):
            scr[row : row + UNIT, :] = value[i * UNIT : (i + 1) * UNIT, j * UNIT : (j + 1) * UNIT]
            row += UNIT
    flush(scr, home, away, first_bit(orders, day, index), outs)


def first_gram(orders, bits, place, cell_map, pred_own, pred_recv, cell_own, start):
    rows, width = pred_own.shape
    height = start.shape[0]
    total = first_rows(rows // UNIT, height, bits)
    out = jax.ShapeDtypeStruct((total // 2, LANES), F32)
    return pl.pallas_call(
        functools.partial(first_gram_kernel, orders),
        out_shape=(out, out),
        in_specs=[smem_spec()] * 2 + [any_spec()] * 4,
        out_specs=(any_spec(), any_spec()),
        scratch_shapes=[
            pltpu.VMEM((2 * rows, width), BF16),
            pltpu.VMEM((rows, width), BF16),
            pltpu.VMEM((height, width), BF16),
            pltpu.VMEM((total, LANES), F32),
            pltpu.SemaphoreType.DMA((3,)),
            pltpu.SemaphoreType.DMA((cell_map.shape[0],)),
            pltpu.SemaphoreType.DMA((2,)),
        ],
        compiler_params=params(),
        name="first_gram",
    )(place, cell_map, pred_own, pred_recv, cell_own, start)


def second_gram(orders, bits, place, cell_own, cell_recv, after):
    rows, width = cell_own.shape
    total = second_rows(rows // UNIT, bits)
    out = jax.ShapeDtypeStruct((total // 2, LANES), F32)
    return pl.pallas_call(
        functools.partial(second_gram_kernel, orders),
        out_shape=(out, out),
        in_specs=[smem_spec()] + [any_spec()] * 3,
        out_specs=(any_spec(), any_spec()),
        scratch_shapes=[
            pltpu.VMEM((2 * rows, width), BF16),
            pltpu.VMEM((total, LANES), F32),
            pltpu.SemaphoreType.DMA((2,)),
            pltpu.SemaphoreType.DMA((2,)),
        ],
        compiler_params=params(),
        name="second_gram",
    )(place, cell_own, cell_recv, after)


def bit_orders(bits):
    plain = list(range(bits))
    swapped = plain[:]
    if bits > 2:
        swapped[0], swapped[1] = 1, 0
    return plain, swapped


def cell_exchange(value, orders, stage, cells):
    pairs = []
    for c in range(cells):
        for d in range(2):
            pairs.append((2 * c + d, 2 * (c ^ (1 << orders[d][stage])) + d))
    return lax.ppermute(value, ("cell", "day"), pairs)


def other_core(value):
    return lax.ppermute(value, "day", [(0, 1), (1, 0)])


def halve(orders, stage, mine, recv):
    bit = jnp.where(lax.axis_index("day") == 0, orders[0][stage], orders[1][stage])
    own = (lax.axis_index("cell") >> bit) & 1
    half = mine.shape[0] // 2
    away = lax.dynamic_slice_in_dim(mine, (1 - own) * half, half, 0)
    away = away + lax.dynamic_slice_in_dim(recv, (1 - own) * half, half, 0)
    home = lax.dynamic_slice_in_dim(mine, own * half, half, 0)
    home = home + lax.dynamic_slice_in_dim(recv, own * half, half, 0)
    return home, away


def finish_sum(orders, bits, cells, home, recv):
    for stage in range(1, bits - 1):
        home, away = halve(orders, stage, home, recv)
        recv = cell_exchange(away, orders, stage, cells)
    part = home + recv
    part = part + cell_exchange(part, orders, bits - 1, cells)
    for stage in reversed(range(bits - 1)):
        part = jnp.concatenate([part, cell_exchange(part, orders, stage, cells)], axis=0)
    return part


def placed_copies(source, target, half, bits, order, cell, sem):
    pieces = 1 << (bits - 1)
    rows = source.shape[0] // pieces
    copies = []
    for p in range(pieces):
        to = 0
        for stage in range(bits - 1):
            digit = (p >> (bits - 2 - stage)) & 1
            own = (cell >> order[stage]) & 1
            to = 2 * to + (own ^ digit)
        begin = pl.multiple_of(to * rows, SUB)
        copies.append(
            pltpu.make_async_copy(
                source.at[pl.ds(p * rows, rows), :], target.at[half, pl.ds(begin, rows), :], sem.at[p]
            )
        )
    return copies


def collect(day, cell, bits, orders, arrays, sems):
    def run(core):
        copies = []
        for n, (own, twin, target) in enumerate(arrays):
            copies += placed_copies(own, target, core, bits, orders[core], cell, sems.at[2 * n])
            copies += placed_copies(twin, target, 1 - core, bits, orders[1 - core], cell, sems.at[2 * n + 1])
        start_all(copies)
        wait_all(copies)

    @pl.when(day == 0)
    def _():
        run(0)

    @pl.when(day == 1)
    def _():
        run(1)


def split3(value):
    first = value.astype(BF16)
    rest = value - first.astype(F32)
    second = rest.astype(BF16)
    third = (rest - second.astype(F32)).astype(BF16)
    return first, second, third


def assemble(value, i, j, gram):
    rows, cols = pl.ds(i * UNIT, UNIT), pl.ds(j * UNIT, UNIT)
    for s, piece in enumerate(split3(value)):
        gram[s, rows, cols] = piece
    if i != j:
        for s, piece in enumerate(split3(value.T)):
            gram[s, cols, rows] = piece


def assemble_list(packed, core, count, own, cross, gram):
    row = 0
    for i, j in own:
        assemble(packed[core, row : row + UNIT, :], core * count + i, core * count + j, gram)
        row += UNIT
    for i, j in cross:
        assemble(packed[core, row : row + UNIT, :], i, count + core * (count // 2) + j, gram)
        row += UNIT
    return row


def exact_dot(left, right):
    return jnp.dot(left, right, precision=lax.Precision.HIGHEST, preferred_element_type=F32)


def inverse_factor(moments):
    size = moments.shape[0]
    row_ids = lax.broadcasted_iota(jnp.int32, (size, size), 0)
    col_ids = lax.broadcasted_iota(jnp.int32, (size, size), 1)
    work = jnp.concatenate([(row_ids == col_ids).astype(F32), moments], axis=1)
    shape = (SUB, 2 * size)
    sub = lax.broadcasted_iota(jnp.int32, shape, 0)
    rows = [work[SUB * i : SUB * i + SUB, :] for i in range(size // SUB)]
    out = []
    for b in range(size // SUB):
        lane = size + SUB * b
        head = rows[b]
        cols = [jnp.broadcast_to(head[:, lane + c : lane + c + 1], shape) for c in range(SUB)]
        entry = [[jnp.broadcast_to(cols[c][r : r + 1, :], shape) for c in range(r + 1)] for r in range(SUB)]
        y = [jnp.broadcast_to(head[r : r + 1, :], shape) for r in range(SUB)]
        inverse = []
        factor = [[None] * SUB for _ in range(SUB)]
        for k in range(SUB):
            inverse.append(1.0 / entry[k][k])
            for i in range(k + 1, SUB):
                factor[i][k] = entry[i][k] * inverse[k]
                for j in range(k + 1, i + 1):
                    entry[i][j] = entry[i][j] - factor[i][k] * entry[j][k]
                y[i] = y[i] - factor[i][k] * y[k]
        p = [y[k] * inverse[k] for k in range(SUB)]
        for i in reversed(range(SUB)):
            for k in range(i):
                p[k] = p[k] - factor[i][k] * p[i]
        for i in range(b + 1, size // SUB):
            terms = [jnp.broadcast_to(rows[i][:, lane + k : lane + k + 1], shape) * p[k] for k in range(SUB)]
            while len(terms) > 1:
                terms = [terms[t] + terms[t + 1] for t in range(0, len(terms), 2)]
            rows[i] = rows[i] - terms[0]
        result, pivot = y[0], entry[0][0]
        for k in range(1, SUB):
            result = jnp.where(sub == k, y[k], result)
            pivot = jnp.where(sub == k, entry[k][k], pivot)
        out.append(result * (1.0 / jnp.sqrt(pivot)))
    return jnp.concatenate(out, axis=0)[:, :size]


def half_step(scores, gram, cells):
    value = jnp.dot(scores, gram[0], preferred_element_type=F32)
    for s in range(1, SPLITS):
        value = value + jnp.dot(scores, gram[s], preferred_element_type=F32)
    moments = sum(
        lax.dot_general(piece, scores, NT, preferred_element_type=F32) for piece in split3(value)
    )
    return inverse_factor(moments / cells), value


def next_scores(inverse, value):
    return exact_dot(inverse, value).astype(BF16)


def first_chain_kernel(bits, orders, counts, place, a_own, a_twin, y_own, y_twin,
                       gram_out, scores_out, loadings_out, alpha, other, gram, sems, out_sem):
    day, group, index = place[0], place[1], place[2]
    collect(day, index, bits, orders, ((a_own, a_twin, alpha), (y_own, y_twin, other)), sems)
    days = gram.shape[1]
    count = days // UNIT // 2
    height = scores_out.shape[0]

    def assemble_all(packs):
        for packed, (own, cross) in zip(packs, shares(count)):
            for core in range(2):
                assemble_list(packed, core, count, own, cross, gram)

    @pl.when(group == 0)
    def _():
        assemble_all((alpha, other))

    @pl.when(group == 1)
    def _():
        assemble_all((other, alpha))

    save = pltpu.make_async_copy(gram, gram_out, out_sem)
    save.start()
    own, cross = shares(count)[0]
    begin = (len(own) + len(cross)) * UNIT
    tiles = [
        alpha[core, begin + c * height : begin + (c + 1) * height, :] for core in range(2) for c in range(count)
    ]
    scores = jnp.concatenate(tiles, axis=1).astype(BF16)
    scores_out[...] = scores
    inverse, value = half_step(scores, gram, counts[0])
    loadings_out[...] = next_scores(inverse, value)
    save.wait()


def first_chain(bits, orders, counts, days, height, place, a_own, a_twin, y_own, y_twin):
    pieces = 1 << (bits - 1)
    vmem = pl.BlockSpec(memory_space=pltpu.VMEM)
    panel = jax.ShapeDtypeStruct((height, days), BF16)
    return pl.pallas_call(
        functools.partial(first_chain_kernel, bits, orders, counts),
        out_shape=(jax.ShapeDtypeStruct((SPLITS, days, days), BF16), panel, panel),
        in_specs=[smem_spec()] + [any_spec()] * 4,
        out_specs=(any_spec(), vmem, vmem),
        scratch_shapes=[
            pltpu.VMEM((2,) + a_own.shape, F32),
            pltpu.VMEM((2,) + a_own.shape, F32),
            pltpu.VMEM((SPLITS, days, days), BF16),
            pltpu.SemaphoreType.DMA((4, pieces)),
            pltpu.SemaphoreType.DMA,
        ],
        compiler_params=params(),
        name="first_chain",
    )(place, a_own, a_twin, y_own, y_twin)


def load_tiles(tile_map, own, recv, whole, day, sems):
    number = tile_map.shape[0]
    half = number // 2
    rows = own.shape[0]
    mine = pl.ds(pl.multiple_of(day * rows, rows), rows)
    theirs = pl.ds(pl.multiple_of((1 - day) * rows, rows), rows)
    for t in range(number):
        slot = lax.rem(tile_map[t], number)
        place = lax.rem(slot, half)
        to = pl.ds(pl.multiple_of(place * LANES, LANES), LANES)
        source = pl.ds(t * LANES, LANES)

        @pl.when(lax.div(slot, half) == day)
        def _():
            pltpu.make_async_copy(own.at[:, source], whole.at[mine, to], sems.at[0, place]).start()
            pltpu.make_async_copy(recv.at[:, source], whole.at[theirs, to], sems.at[1, place]).start()


def wait_tiles(tile_map, own, whole, sems):
    rows = own.shape[0]
    part = pl.ds(0, LANES)
    for place in range(tile_map.shape[0] // 2):
        for n in range(2):
            pltpu.make_async_copy(own.at[:, part], whole.at[pl.ds(0, rows), part], sems.at[n, place]).wait()


def second_chain_kernel(bits, orders, counts, place, pred_map, cell_map, b_own, b_twin, gram_in, scores_in,
                        loadings_in, pred_own, pred_recv, cell_own, cell_recv, pred_out, cell_out,
                        beta, pred, cell, pred_gram, cell_gram, sems, gram_sem, pred_sems, cell_sems):
    day, index = place[0], place[2]
    restore = pltpu.make_async_copy(gram_in, pred_gram, gram_sem)
    collect(day, index, bits, orders, ((b_own, b_twin, beta),), sems)
    restore.start()
    load_tiles(pred_map, pred_own, pred_recv, pred, day, pred_sems)
    load_tiles(cell_map, cell_own, cell_recv, cell, day, cell_sems)
    days = pred.shape[0]
    count = days // UNIT // 2
    own = own_blocks(count)
    cross = [(i, j) for i in range(count) for j in range(count // 2)]
    for core in range(2):
        assemble_list(beta, core, count, own, cross, cell_gram)
    pred_scores, loadings = scores_in[...], loadings_in[...]
    pred_inverse = pred_value = None
    for iteration in range(ITERS):
        if iteration > 0 or ITERS == 1:
            pred_inverse, pred_value = half_step(pred_scores, pred_gram, counts[0])
            loadings = next_scores(pred_inverse, pred_value)
        cell_inverse, cell_value = half_step(loadings, cell_gram, counts[1])
        if iteration == 0:
            restore.wait()
            wait_tiles(pred_map, pred_own, pred, pred_sems)
            wait_tiles(cell_map, cell_own, cell, cell_sems)
        if iteration < ITERS - 1:
            pred_scores = next_scores(cell_inverse, cell_value)
    raw = jnp.dot(pred_scores, pred[...], preferred_element_type=F32)
    pred_out[...] = exact_dot(pred_inverse, raw)
    raw = jnp.dot(loadings, cell[...], preferred_element_type=F32)
    cell_out[...] = exact_dot(cell_inverse, raw)


def second_chain(bits, orders, counts, place, pred_map, cell_map, b_own, b_twin, gram, scores, loadings, fields):
    pieces = 1 << (bits - 1)
    height, days = scores.shape
    width = fields[0].shape[1] // 2
    tiles = pred_map.shape[0] // 2
    vmem = pl.BlockSpec(memory_space=pltpu.VMEM)
    out = jax.ShapeDtypeStruct((height, width), F32)
    return pl.pallas_call(
        functools.partial(second_chain_kernel, bits, orders, counts),
        out_shape=(out, out),
        in_specs=[smem_spec()] * 3 + [any_spec()] * 3 + [vmem] * 2 + [any_spec()] * 4,
        out_specs=(vmem, vmem),
        scratch_shapes=[
            pltpu.VMEM((2,) + b_own.shape, F32),
            pltpu.VMEM((days, width), BF16),
            pltpu.VMEM((days, width), BF16),
            pltpu.VMEM((SPLITS, days, days), BF16),
            pltpu.VMEM((SPLITS, days, days), BF16),
            pltpu.SemaphoreType.DMA((2, pieces)),
            pltpu.SemaphoreType.DMA,
            pltpu.SemaphoreType.DMA((2, tiles)),
            pltpu.SemaphoreType.DMA((2, tiles)),
        ],
        compiler_params=params(),
        name="second_chain",
    )(place, pred_map, cell_map, b_own, b_twin, gram, scores, loadings, *fields)


def local(predictors, predictand, pred_map, cell_map, start_panel):
    cells = lax.axis_size("cell")
    bits = cells.bit_length() - 1
    orders = bit_orders(bits)
    days = predictors.shape[0] * 2
    height = start_panel.shape[0]
    counts = (float(predictors.shape[1] * cells), float(predictand.shape[1] * cells))
    place = jnp.stack([lax.axis_index("day"), lax.axis_index("group"), lax.axis_index("cell")])
    place = place.astype(jnp.int32)

    pred_recv = other_core(predictors)
    cell_recv = other_core(predictand)
    a_home, a_away = first_gram(orders, bits, place, cell_map, predictors, pred_recv, predictand, start_panel)
    b_home, b_away = second_gram(orders, bits, place, predictand, cell_recv, a_away)
    a_recv = cell_exchange(a_away, orders, 0, cells)
    b_away, a_recv = lax.optimization_barrier((b_away, a_recv))
    a_own = finish_sum(orders, bits, cells, a_home, a_recv)
    b_recv = cell_exchange(b_away, orders, 0, cells)
    b_own = finish_sum(orders, bits, cells, b_home, b_recv)
    y_own = lax.ppermute(a_own, "group", [(0, 1), (1, 0)])
    a_twin = other_core(a_own)
    y_twin = other_core(y_own)
    b_twin = other_core(b_own)
    gram, scores, loadings = first_chain(
        bits, orders, counts, days, height, place, a_own, a_twin, y_own, y_twin
    )
    return second_chain(
        bits, orders, counts, place, pred_map, cell_map, b_own, b_twin, gram, scores, loadings,
        (predictors, pred_recv, predictand, cell_recv),
    )


def solution(mesh):
    in_specs = (
        P("day", "cell"),
        P("day", ("group", "cell")),
        P("cell"),
        P(("group", "cell")),
        P(None, ("group", "cell")),
    )
    out_specs = (P(None, ("group", "cell", "day")), P(None, ("group", "cell", "day")))
    return jax.shard_map(local, mesh=mesh, in_specs=in_specs, out_specs=out_specs, check_vma=False)
```

time: 705 us -> 140 us (0.20)
  blocking collectives: 435 us -> 0 us
  other arithmetic: 78.9 us -> 1.97 us
  Pallas kernels: 0 us -> 52.3 us
  waiting for transfers between devices: 104 us -> 61.1 us
  matrix products: 42.4 us -> 0 us
  local copies, waits for them, and re-layouts: 28.1 us -> 3.33 us
  starting transfers between devices: 0.25 us -> 19.7 us
  between operations: 14.5 us -> 1.01 us
    psum x12 -> x0, blocking collectives: 435 us -> none  [the longest x6 224 us: moments_over_cells(): return lax.psum(partial_value, 'cell')]
    psum x6 -> x0, waiting for transfers between devices: 104 us -> none  [loads_whole(): return lax.psum(partial_value, 'day')]
    another operation x30 -> x1, other arithmetic: 72.4 us -> 0.64 us  [local(): jnp.stack([lax.axis_index('day'), lax.axis_index('group'), lax.axis_index...]
    ppermute x0 -> x16, waiting for transfers between devices: none -> 61.1 us  [the longest x10 44.1 us: cell_exchange(): return lax.ppermute(value, ('cell', 'day'), pairs)]
    pallas_call x0 -> x4, Pallas kernels: none -> 52.3 us  [the longest x1 28.3 us: second_chain(): pl.pallas_call(functools.partial(second_chain_kernel, bits, orders, count...]
    dot_general x18 -> x0, matrix products: 32.3 us -> none  [the longest x6 14.2 us: half_step(): jnp.dot(scores, second_field, preferred_element_type=jnp.float32)]
    ppermute x0 -> x16, starting transfers between devices: none -> 19.7 us  [the longest x10 16.9 us: cell_exchange(): return lax.ppermute(value, ('cell', 'day'), pairs)]
    another operation x6 -> x0, matrix products: 10.1 us -> none  [half_step(): lax.linalg.triangular_solve(factor, unscaled, left_side=True, lower=True)]
  transfers between devices with their start and end apart: 6 -> 16, of which waited for: 6 -> 10; matrix products, arithmetic and copies ran while one was open for 0% -> 1% of each run, Pallas kernels for 0% -> 17%
where the time goes in v4:
time: 140 us; the launch traced here: 139 us
  waiting for transfers between devices  61.1 us (44%)
  Pallas kernels  52.3 us (37%)
  starting transfers between devices  19.7 us (14%)
  local copies, waits for them, and re-layouts  3.33 us (2%)
  other arithmetic  1.97 us (1%)
    ppermute x10, waiting for transfers between devices, cell_exchange(): return lax.ppermute(value, ('cell', 'day'), pairs)  44.1 us
    pallas_call x1, Pallas kernels, second_chain(): pl.pallas_call(functools.partial(second_chain_kernel, bits, orders, count...  28.3 us
    ppermute x10, starting transfers between devices, cell_exchange(): return lax.ppermute(value, ('cell', 'day'), pairs)  16.9 us
    pallas_call x1, Pallas kernels, first_chain(): pl.pallas_call(functools.partial(first_chain_kernel, bits, orders, counts...  11.1 us
    ppermute x1, waiting for transfers between devices, local(): y_own = lax.ppermute(a_own, 'group', [(0, 1), (1, 0)])  9.27 us
    ppermute x5, waiting for transfers between devices, other_core(): return lax.ppermute(value, 'day', [(0, 1), (1, 0)])  7.76 us
    pallas_call x1, Pallas kernels, first_gram(): pl.pallas_call(functools.partial(first_gram_kernel, orders), out_shape=(o...  6.56 us
    pallas_call x1, Pallas kernels, second_gram(): pl.pallas_call(functools.partial(second_gram_kernel, orders), out_shape=(...  6.34 us
  transfers between devices with their start and end apart: 16, of which 10 were waited for; matrix products, arithmetic and copies ran while one was open for 1% of the time, Pallas kernels for 17%

profile of v4, /device:TPU:0, one launch (start us, length us, event | category | flops | bytes accessed | tf_op | source)
XLA Modules:
  0.0 139.4 jit_solution(17553263783070481563)
XLA Ops:
  0.6 0.5 collective-permute-start.1
  1.1 0.1 collective-permute-start
  1.2 0.6 pad_add_fusion.place
  1.9 5.6 %collective-permute-done.1.pred_recv = bf16[512,2048]{1,0:T(8,128)(2,1)} collective-permute-done((bf16[512,2048]{1,0:T(8,128)(2,1)}, bf16[512,2048]{1,0:T(8,128)(2,1)}, u32[]{:S(2)}, u32[]{:S(2)}) %collective-permute-start.1) | collective-permute-done | bytes 2097184 | tf_op jit(solution)/shard_map/ppermute | solution.py:224
  7.4 6.6 %first_gram.1 = (f32[704,128]{1,0:T(8,128)}, f32[704,128]{1,0:T(8,128)}) custom-call(s32[3]{0:T(128)} %pad_add_fusion.place, s32[16]{0:T(128)} %cell_map.3, bf16[512,2048]{1,0:T(8,128)(2,1)} %pred_own.3, bf16[512,2048]{1,0:T(8,128)(2,1)} %collective-permute-done.1.pred_recv, bf16[512,2048]{1,0:T(8,128)(2,1)} %cell_own.5, bf16[64,2048]{1,0:T(8,128)(2,1)} %start.1), custom_call_target="tpu_custom_call" | custom-call | tf_op jit(solution)/shard_map/first_gram/pallas_call | solution.py:168
  14.0 0.0 copy-start.8
  14.0 2.9 %collective-permute-start.2 = (f32[704,128]{1,0:T(8,128)}, f32[704,128]{1,0:T(8,128)S(1)}, u32[]{:S(2)}, u32[]{:S(2)}) collective-permute-start(f32[704,128]{1,0:T(8,128)} %get-tuple-element.11.after), channel_id=1, source_target_pairs={{0,2},{1,5},{2,0},{3,7},{4,6},{5,1},{6,4},{7,3},{8,10},{9,13},{10,... | collective-permute-start | bytes 1081352 | tf_op jit(solution)/shard_map/ppermute | solution.py:220
  17.0 0.0 collective-permute-done.cell_recv
  17.0 0.0 copy-start
  17.0 1.4 copy-done
  18.4 6.3 %second_gram.1 = (f32[1152,128]{1,0:T(8,128)}, f32[1152,128]{1,0:T(8,128)}) custom-call(s32[3]{0:T(128)} %pad_add_fusion.place, bf16[512,2048]{1,0:T(8,128)(2,1)} %cell_own.5, bf16[512,2048]{1,0:T(8,128)(2,1)} %copy-done, f32[704,128]{1,0:T(8,128)} %get-tuple-element.11.after), custom_call_target="tpu_custom_call" | custom-call | tf_op jit(solution)/shard_map/second_gram/pallas_call | solution.py:191
  24.7 0.0 copy-start.7
  24.7 0.0 collective-permute-done.2
  24.7 0.1 collective-permute-start.3
  24.8 10.1 %collective-permute-done.3 = f32[1152,128]{1,0:T(8,128)S(1)} collective-permute-done((f32[1152,128]{1,0:T(8,128)}, f32[1152,128]{1,0:T(8,128)S(1)}, u32[]{:S(2)}, u32[]{:S(2)}) %collective-permute-start.3) | collective-permute-done | bytes 589856 | tf_op jit(solution)/shard_map/ppermute | solution.py:220
  34.9 1.0 dynamic-slice_add_fusion
  35.9 1.6 %collective-permute-start.4 = (f32[576,128]{1,0:T(8,128)S(1)}, f32[576,128]{1,0:T(8,128)S(1)}, u32[]{:S(2)}, u32[]{:S(2)}) collective-permute-start(f32[576,128]{1,0:T(8,128)S(1)} %dynamic-slice_add_fusion), channel_id=1, source_target_pairs={{0,4},{1,3},{2,6},{3,1},{4,0},{5,7},{6,2},{7,5},{8,12},{9,11},{10,... | collective-permute-start | bytes 884744 | tf_op jit(solution)/shard_map/ppermute | solution.py:220
  37.5 0.0 copy-done.8
  37.5 0.5 collective-permute-start.9
  38.1 4.6 %collective-permute-done.4 = f32[576,128]{1,0:T(8,128)S(1)} collective-permute-done((f32[576,128]{1,0:T(8,128)S(1)}, f32[576,128]{1,0:T(8,128)S(1)}, u32[]{:S(2)}, u32[]{:S(2)}) %collective-permute-start.4) | collective-permute-done | bytes 294944 | tf_op jit(solution)/shard_map/ppermute | solution.py:220
  42.7 0.0 copy-done.7
  42.7 3.0 %collective-permute-start.5 = (f32[576,128]{1,0:T(8,128)S(1)}, f32[576,128]{1,0:T(8,128)S(1)}, u32[]{:S(2)}, u32[]{:S(2)}) collective-permute-start(f32[576,128]{1,0:T(8,128)S(1)} %add_add_fusion), channel_id=1, source_target_pairs={{0,8},{1,9},{2,10},{3,11},{4,12},{5,13},{6,14},{7,15},{8,0},{9,1},... | collective-permute-start | bytes 884744 | tf_op jit(solution)/shard_map/ppermute | solution.py:220
  45.7 0.0 collective-permute-done.9
  45.7 3.8 %collective-permute-start.10 = (f32[352,128]{1,0:T(8,128)S(1)}, f32[352,128]{1,0:T(8,128)S(1)}, u32[]{:S(2)}, u32[]{:S(2)}) collective-permute-start(f32[352,128]{1,0:T(8,128)S(1)} %add_add_fusion.1), channel_id=1, source_target_pairs={{0,8},{1,9},{2,10},{3,11},{4,12},{5,13},{6,14},{7,15},{8,0},{9,1},... | collective-permute-start | bytes 540680 | tf_op jit(solution)/shard_map/ppermute | solution.py:220
  49.5 15.3 %collective-permute-done.10 = f32[352,128]{1,0:T(8,128)S(1)} collective-permute-done((f32[352,128]{1,0:T(8,128)S(1)}, f32[352,128]{1,0:T(8,128)S(1)}, u32[]{:S(2)}, u32[]{:S(2)}) %collective-permute-start.10) | collective-permute-done | bytes 180256 | tf_op jit(solution)/shard_map/ppermute | solution.py:220
  64.8 0.1 collective-permute-start.11
  64.9 0.0 collective-permute-done.5
  65.0 2.1 %collective-permute-start.6 = (f32[576,128]{1,0:T(8,128)S(1)}, f32[576,128]{1,0:T(8,128)S(1)}, u32[]{:S(2)}, u32[]{:S(2)}) collective-permute-start(f32[576,128]{1,0:T(8,128)S(1)} %add.45), channel_id=1, source_target_pairs={{0,4},{1,3},{2,6},{3,1},{4,0},{5,7},{6,2},{7,5},{8,12},{9,11},{10,... | collective-permute-start | bytes 884744 | tf_op jit(solution)/shard_map/ppermute | solution.py:220
  67.0 3.4 %collective-permute-done.11 = f32[352,128]{1,0:T(8,128)S(1)} collective-permute-done((f32[352,128]{1,0:T(8,128)S(1)}, f32[352,128]{1,0:T(8,128)S(1)}, u32[]{:S(2)}, u32[]{:S(2)}) %collective-permute-start.11) | collective-permute-done | bytes 180256 | tf_op jit(solution)/shard_map/ppermute | solution.py:220
  70.4 1.6 %collective-permute-start.12 = (f32[704,128]{1,0:T(8,128)S(1)}, f32[704,128]{1,0:T(8,128)S(1)}, u32[]{:S(2)}, u32[]{:S(2)}) collective-permute-start(f32[704,128]{1,0:T(8,128)S(1)} %pad_maximum_fusion.3), channel_id=1, source_target_pairs={{0,2},{1,5},{2,0},{3,7},{4,6},{5,1},{6,4},{7,3},{8,10},{9,13},{10,... | collective-permute-start | bytes 1081352 | tf_op jit(solution)/shard_map/ppermute | solution.py:220
  72.0 3.8 %collective-permute-done.6 = f32[576,128]{1,0:T(8,128)S(1)} collective-permute-done((f32[576,128]{1,0:T(8,128)S(1)}, f32[576,128]{1,0:T(8,128)S(1)}, u32[]{:S(2)}, u32[]{:S(2)}) %collective-permute-start.6) | collective-permute-done | bytes 294944 | tf_op jit(solution)/shard_map/ppermute | solution.py:220
  75.8 1.3 collective-permute-start.7
  77.1 0.8 collective-permute-done.12
  78.0 0.0 copy-start.2
  78.0 1.6 %collective-permute-start.14 = (f32[1408,128]{1,0:T(8,128)S(1)}, f32[1408,128]{1,0:T(8,128)S(1)}, u32[]{:S(2)}, u32[]{:S(2)}) collective-permute-start(f32[1408,128]{1,0:T(8,128)S(1)} %pad_maximum_fusion.1.a_own), channel_id=1, source_target_pairs={{0,16},{16,0},{1,17},{17,1},{2,18},{18,2},{3,19},{19,3},{4,20},{20... | collective-permute-start | bytes 2162696 | tf_op jit(solution)/shard_map/ppermute | solution.py:536
  79.6 6.2 %collective-permute-done.7 = f32[1152,128]{1,0:T(8,128)S(1)} collective-permute-done((f32[1152,128]{1,0:T(8,128)S(1)}, f32[1152,128]{1,0:T(8,128)S(1)}, u32[]{:S(2)}, u32[]{:S(2)}) %collective-permute-start.7) | collective-permute-done | bytes 589856 | tf_op jit(solution)/shard_map/ppermute | solution.py:220
  85.8 0.1 pad_maximum_fusion.b_own
  85.8 0.0 copy-start.1
  85.8 0.1 collective-permute-start.8
  85.9 0.0 copy-done.2
  85.9 0.5 collective-permute-start.13
  86.4 9.3 %collective-permute-done.14.y_own = f32[1408,128]{1,0:T(8,128)S(1)} collective-permute-done((f32[1408,128]{1,0:T(8,128)S(1)}, f32[1408,128]{1,0:T(8,128)S(1)}, u32[]{:S(2)}, u32[]{:S(2)}) %collective-permute-start.14) | collective-permute-done | bytes 720928 | tf_op jit(solution)/shard_map/ppermute | solution.py:536
  95.7 0.0 copy-start.4
  95.7 0.0 collective-permute-start.15
  95.7 0.0 collective-permute-done.13.a_twin
  95.7 0.0 copy-start.5
  95.7 2.2 %collective-permute-done.15.y_twin = f32[1408,128]{1,0:T(8,128)S(1)} collective-permute-done((f32[1408,128]{1,0:T(8,128)S(1)}, f32[1408,128]{1,0:T(8,128)S(1)}, u32[]{:S(2)}, u32[]{:S(2)}) %collective-permute-start.15) | collective-permute-done | bytes 720928 | tf_op jit(solution)/shard_map/ppermute | solution.py:224
  97.9 0.0 copy-done.4
  97.9 0.0 copy-done.5
  97.9 0.0 copy-start.6
  97.9 0.9 copy-done.6
  98.8 11.1 %first_chain.1 = (bf16[3,1024,1024]{2,1,0:T(8,128)(2,1)}, bf16[64,1024]{1,0:T(8,128)(2,1)}, bf16[64,1024]{1,0:T(8,128)(2,1)}) custom-call(s32[3]{0:T(128)} %pad_add_fusion.place, f32[1408,128]{1,0:T(8,128)} %copy-done.2, f32[1408,128]{1,0:T(8,128)} %copy-done.5, f32[1408,128]{1,0:T(8,128)} %copy-done.4, f32[1408,128]{1,0:T(8,128)} %copy-done.6), custom_call_target="tpu_custom_call" | custom-call | tf_op jit(solution)/shard_map/first_chain/pallas_call | solution.py:412
  109.9 0.0 copy-done.1
  109.9 0.0 collective-permute-done.8.b_twin
  109.9 0.0 copy-start.3
  109.9 1.0 copy-done.3
  111.0 28.3 %second_chain.1 = (f32[64,1024]{1,0:T(8,128)}, f32[64,1024]{1,0:T(8,128)}) custom-call(s32[3]{0:T(128)} %pad_add_fusion.place, s32[16]{0:T(128)} %pred_map.1, s32[16]{0:T(128)} %cell_map.3, f32[2304,128]{1,0:T(8,128)} %copy-done.1, f32[2304,128]{1,0:T(8,128)} %copy-done.3, bf16[3,1024,1024]{2,1,0:T(8,128)(2,1)} %get-tuple-element.17.gram_in, ...), custom_call_target="tpu_custom_call" | custom-call | tf_op jit(solution)/shard_map/second_chain/pallas_call | solution.py:496
  (8 shorter events, 0.3 us)
Async XLA Ops:
  0.6 6.8 %collective-permute-start.1 = (bf16[512,2048]{1,0:T(8,128)(2,1)}, bf16[512,2048]{1,0:T(8,128)(2,1)}, u32[]{:S(2)}, u32[]{:S(2)}) collective-permute-start(bf16[512,2048]{1,0:T(8,128)(2,1)} %pred_own.3), channel_id=1, source_target_pairs={{0,1},{1,0},{2,3},{3,2},{4,5},{5,4},{6,7},{7,6},{8,9},{9,8},{10,11... | collective-permute-start | bytes 6291464 | tf_op jit(solution)/shard_map/ppermute | solution.py:224
  1.1 15.8 %collective-permute-start = (bf16[512,2048]{1,0:T(8,128)(2,1)}, bf16[512,2048]{1,0:T(8,128)(2,1)S(1)}, u32[]{:S(2)}, u32[]{:S(2)}) collective-permute-start(bf16[512,2048]{1,0:T(8,128)(2,1)} %cell_own.5), channel_id=1, source_target_pairs={{0,1},{1,0},{2,3},{3,2},{4,5},{5,4},{6,7},{7,6},{8,9},{9,8},{10,11... | collective-permute-start | bytes 6291464 | tf_op jit(solution)/shard_map/ppermute | solution.py:224
  14.0 23.5 %copy-start.8 = (f32[704,128]{1,0:T(8,128)S(1)}, f32[704,128]{1,0:T(8,128)}, u32[]{:S(2)}) copy-start(f32[704,128]{1,0:T(8,128)} %get-tuple-element.15) | copy-start | bytes 1081348
  14.0 10.7 %collective-permute-start.2 = (f32[704,128]{1,0:T(8,128)}, f32[704,128]{1,0:T(8,128)S(1)}, u32[]{:S(2)}, u32[]{:S(2)}) collective-permute-start(f32[704,128]{1,0:T(8,128)} %get-tuple-element.11.after), channel_id=1, source_target_pairs={{0,2},{1,5},{2,0},{3,7},{4,6},{5,1},{6,4},{7,3},{8,10},{9,13},{10,... | collective-permute-start | bytes 1081352 | tf_op jit(solution)/shard_map/ppermute | solution.py:220
  17.0 1.4 copy-start
  24.7 18.0 %copy-start.7 = (f32[1152,128]{1,0:T(8,128)S(1)}, f32[1152,128]{1,0:T(8,128)}, u32[]{:S(2)}) copy-start(f32[1152,128]{1,0:T(8,128)} %get-tuple-element.12) | copy-start | bytes 1769476
  24.7 10.2 %collective-permute-start.3 = (f32[1152,128]{1,0:T(8,128)}, f32[1152,128]{1,0:T(8,128)S(1)}, u32[]{:S(2)}, u32[]{:S(2)}) collective-permute-start(f32[1152,128]{1,0:T(8,128)} %get-tuple-element.14), channel_id=1, source_target_pairs={{0,2},{1,5},{2,0},{3,7},{4,6},{5,1},{6,4},{7,3},{8,10},{9,13},{10,... | collective-permute-start | bytes 1769480 | tf_op jit(solution)/shard_map/ppermute | solution.py:220
  35.9 6.8 %collective-permute-start.4 = (f32[576,128]{1,0:T(8,128)S(1)}, f32[576,128]{1,0:T(8,128)S(1)}, u32[]{:S(2)}, u32[]{:S(2)}) collective-permute-start(f32[576,128]{1,0:T(8,128)S(1)} %dynamic-slice_add_fusion), channel_id=1, source_target_pairs={{0,4},{1,3},{2,6},{3,1},{4,0},{5,7},{6,2},{7,5},{8,12},{9,11},{10,... | collective-permute-start | bytes 884744 | tf_op jit(solution)/shard_map/ppermute | solution.py:220
  37.5 8.1 %collective-permute-start.9 = (f32[352,128]{1,0:T(8,128)S(1)}, f32[352,128]{1,0:T(8,128)S(1)}, u32[]{:S(2)}, u32[]{:S(2)}) collective-permute-start(f32[352,128]{1,0:T(8,128)S(1)} %dynamic-slice_add_fusion.1), channel_id=1, source_target_pairs={{0,4},{1,3},{2,6},{3,1},{4,0},{5,7},{6,2},{7,5},{8,12},{9,11},{10,... | collective-permute-start | bytes 540680 | tf_op jit(solution)/shard_map/ppermute | solution.py:220
  42.7 22.2 %collective-permute-start.5 = (f32[576,128]{1,0:T(8,128)S(1)}, f32[576,128]{1,0:T(8,128)S(1)}, u32[]{:S(2)}, u32[]{:S(2)}) collective-permute-start(f32[576,128]{1,0:T(8,128)S(1)} %add_add_fusion), channel_id=1, source_target_pairs={{0,8},{1,9},{2,10},{3,11},{4,12},{5,13},{6,14},{7,15},{8,0},{9,1},... | collective-permute-start | bytes 884744 | tf_op jit(solution)/shard_map/ppermute | solution.py:220
  45.7 19.1 %collective-permute-start.10 = (f32[352,128]{1,0:T(8,128)S(1)}, f32[352,128]{1,0:T(8,128)S(1)}, u32[]{:S(2)}, u32[]{:S(2)}) collective-permute-start(f32[352,128]{1,0:T(8,128)S(1)} %add_add_fusion.1), channel_id=1, source_target_pairs={{0,8},{1,9},{2,10},{3,11},{4,12},{5,13},{6,14},{7,15},{8,0},{9,1},... | collective-permute-start | bytes 540680 | tf_op jit(solution)/shard_map/ppermute | solution.py:220
  64.8 5.6 %collective-permute-start.11 = (f32[352,128]{1,0:T(8,128)S(1)}, f32[352,128]{1,0:T(8,128)S(1)}, u32[]{:S(2)}, u32[]{:S(2)}) collective-permute-start(f32[352,128]{1,0:T(8,128)S(1)} %add.51), channel_id=1, source_target_pairs={{0,4},{1,3},{2,6},{3,1},{4,0},{5,7},{6,2},{7,5},{8,12},{9,11},{10,... | collective-permute-start | bytes 540680 | tf_op jit(solution)/shard_map/ppermute | solution.py:220
  65.0 10.8 %collective-permute-start.6 = (f32[576,128]{1,0:T(8,128)S(1)}, f32[576,128]{1,0:T(8,128)S(1)}, u32[]{:S(2)}, u32[]{:S(2)}) collective-permute-start(f32[576,128]{1,0:T(8,128)S(1)} %add.45), channel_id=1, source_target_pairs={{0,4},{1,3},{2,6},{3,1},{4,0},{5,7},{6,2},{7,5},{8,12},{9,11},{10,... | collective-permute-start | bytes 884744 | tf_op jit(solution)/shard_map/ppermute | solution.py:220
  70.4 7.5 %collective-permute-start.12 = (f32[704,128]{1,0:T(8,128)S(1)}, f32[704,128]{1,0:T(8,128)S(1)}, u32[]{:S(2)}, u32[]{:S(2)}) collective-permute-start(f32[704,128]{1,0:T(8,128)S(1)} %pad_maximum_fusion.3), channel_id=1, source_target_pairs={{0,2},{1,5},{2,0},{3,7},{4,6},{5,1},{6,4},{7,3},{8,10},{9,13},{10,... | collective-permute-start | bytes 1081352 | tf_op jit(solution)/shard_map/ppermute | solution.py:220
  75.8 9.9 %collective-permute-start.7 = (f32[1152,128]{1,0:T(8,128)S(1)}, f32[1152,128]{1,0:T(8,128)S(1)}, u32[]{:S(2)}, u32[]{:S(2)}) collective-permute-start(f32[1152,128]{1,0:T(8,128)S(1)} %pad_maximum_fusion.2), channel_id=1, source_target_pairs={{0,2},{1,5},{2,0},{3,7},{4,6},{5,1},{6,4},{7,3},{8,10},{9,13},{10,... | collective-permute-start | bytes 1769480 | tf_op jit(solution)/shard_map/ppermute | solution.py:220
  78.0 8.0 %copy-start.2 = (f32[1408,128]{1,0:T(8,128)}, f32[1408,128]{1,0:T(8,128)S(1)}, u32[]{:S(2)}) copy-start(f32[1408,128]{1,0:T(8,128)S(1)} %pad_maximum_fusion.1.a_own) | copy-start | bytes 2162692
  78.0 17.7 %collective-permute-start.14 = (f32[1408,128]{1,0:T(8,128)S(1)}, f32[1408,128]{1,0:T(8,128)S(1)}, u32[]{:S(2)}, u32[]{:S(2)}) collective-permute-start(f32[1408,128]{1,0:T(8,128)S(1)} %pad_maximum_fusion.1.a_own), channel_id=1, source_target_pairs={{0,16},{16,0},{1,17},{17,1},{2,18},{18,2},{3,19},{19,3},{4,20},{20... | collective-permute-start | bytes 2162696 | tf_op jit(solution)/shard_map/ppermute | solution.py:536
  85.8 24.1 %copy-start.1 = (f32[2304,128]{1,0:T(8,128)}, f32[2304,128]{1,0:T(8,128)S(1)}, u32[]{:S(2)}) copy-start(f32[2304,128]{1,0:T(8,128)S(1)} %pad_maximum_fusion.b_own) | copy-start | bytes 3538948
  85.8 24.1 %collective-permute-start.8 = (f32[2304,128]{1,0:T(8,128)S(1)}, f32[2304,128]{1,0:T(8,128)S(1)}, u32[]{:S(2)}, u32[]{:S(2)}) collective-permute-start(f32[2304,128]{1,0:T(8,128)S(1)} %pad_maximum_fusion.b_own), channel_id=1, source_target_pairs={{0,1},{1,0},{2,3},{3,2},{4,5},{5,4},{6,7},{7,6},{8,9},{9,8},{10,11... | collective-permute-start | bytes 3538952 | tf_op jit(solution)/shard_map/ppermute | solution.py:224
  85.9 9.8 %collective-permute-start.13 = (f32[1408,128]{1,0:T(8,128)S(1)}, f32[1408,128]{1,0:T(8,128)S(1)}, u32[]{:S(2)}, u32[]{:S(2)}) collective-permute-start(f32[1408,128]{1,0:T(8,128)S(1)} %pad_maximum_fusion.1.a_own), channel_id=1, source_target_pairs={{0,1},{1,0},{2,3},{3,2},{4,5},{5,4},{6,7},{7,6},{8,9},{9,8},{10,11... | collective-permute-start | bytes 2162696 | tf_op jit(solution)/shard_map/ppermute | solution.py:224
  95.7 2.2 %copy-start.4 = (f32[1408,128]{1,0:T(8,128)}, f32[1408,128]{1,0:T(8,128)S(1)}, u32[]{:S(2)}) copy-start(f32[1408,128]{1,0:T(8,128)S(1)} %collective-permute-done.14.y_own) | copy-start | bytes 2162692
  95.7 2.2 %collective-permute-start.15 = (f32[1408,128]{1,0:T(8,128)S(1)}, f32[1408,128]{1,0:T(8,128)S(1)}, u32[]{:S(2)}, u32[]{:S(2)}) collective-permute-start(f32[1408,128]{1,0:T(8,128)S(1)} %collective-permute-done.14.y_own), channel_id=1, source_target_pairs={{0,1},{1,0},{2,3},{3,2},{4,5},{5,4},{6,7},{7,6},{8,9},{9,8},{10,11... | collective-permute-start | bytes 2162696 | tf_op jit(solution)/shard_map/ppermute | solution.py:224
  95.7 2.2 %copy-start.5 = (f32[1408,128]{1,0:T(8,128)}, f32[1408,128]{1,0:T(8,128)S(1)}, u32[]{:S(2)}) copy-start(f32[1408,128]{1,0:T(8,128)S(1)} %collective-permute-done.13.a_twin) | copy-start | bytes 2162692
  97.9 0.9 copy-start.6
  109.9 1.1 copy-start.3

commit v5 on v4

--- a/solution.py
+++ b/solution.py
@@ -67,14 +67,6 @@
         copy.wait()
 
 
-def load_days(keep, recv, whole, day, sems):
-    rows = keep.shape[0]
-    return [
-        pltpu.make_async_copy(keep, whole.at[pl.ds(pl.multiple_of(day * rows, rows), rows), :], sems.at[0]),
-        pltpu.make_async_copy(recv, whole.at[pl.ds(pl.multiple_of((1 - day) * rows, rows), rows), :], sems.at[1]),
-    ]
-
-
 def first_bit(orders, day, cell):
     return jnp.where(day == 0, (cell >> orders[0][0]) & 1, (cell >> orders[1][0]) & 1)
 
@@ -89,15 +81,12 @@
     wait_all(copies)
 
 
-def rows_at(whole, block):
-    return whole[pl.ds(pl.multiple_of(block * UNIT, UNIT), UNIT), :]
-
-
-def first_gram_kernel(orders, place, cell_map, pred_own, pred_recv, cell_own, start, home, away,
-                      pred, cell, panel, scr, sems, tile_sems, outs):
-    day, group, index = place[0], place[1], place[2]
+def own_gram_kernel(place, cell_map, pred_own, cell_own, start, first_out, second_out,
+                    pred, cell, panel, first, second, sems, tile_sems, outs):
+    group = place[1]
     number = cell_map.shape[0]
     height = panel.shape[0]
+    loads = [pltpu.make_async_copy(cell_own, cell, sems.at[0]), pltpu.make_async_copy(pred_own, pred, sems.at[1])]
     tiles = []
     for t in range(number):
         slot = pl.multiple_of(lax.rem(cell_map[t], number) * LANES, LANES)
@@ -106,102 +95,122 @@
                 start.at[:, pl.ds(slot, LANES)], panel.at[:, pl.ds(t * LANES, LANES)], tile_sems.at[t]
             )
         )
-    data = load_days(pred_own, pred_recv, pred, day, sems)
-    field = pltpu.make_async_copy(cell_own, cell, sems.at[2])
-    start_all(data)
-    field.start()
     start_all(tiles)
+    start_all(loads)
     count = cell.shape[0] // UNIT
-    (own0, cross0), (own1, cross1) = shares(count)
+    loads[0].wait()
     row = 0
-    wait_all(data)
-    for (i0, j0), (i1, j1) in zip(own0, own1):
-        left = rows_at(pred, day * count + i0 + group * (i1 - i0))
-        right = rows_at(pred, day * count + j0 + group * (j1 - j0))
-        scr[row : row + UNIT, :] = lax.dot_general(left, right, NT, preferred_element_type=F32)
-        row += UNIT
-    for (i0, j0), (i1, j1) in zip(cross0, cross1):
-        left = rows_at(pred, i0 + group * (i1 - i0))
-        right = rows_at(pred, count + day * (count // 2) + j0 + group * (j1 - j0))
-        scr[row : row + UNIT, :] = lax.dot_general(left, right, NT, preferred_element_type=F32)
-        row += UNIT
-    field.wait()
+    for i in range(count):
+        right = cell[i * UNIT :, :]
+        value = lax.dot_general(right[:UNIT, :], right, NT, preferred_element_type=F32)
+        for c in range(count - i):
+            second[row : row + UNIT, :] = value[:, c * UNIT : (c + 1) * UNIT]
+            row += UNIT
+    save = pltpu.make_async_copy(second, second_out, outs.at[1])
+    save.start()
     wait_all(tiles)
+    row = 0
     scores = lax.dot_general(panel[...], cell[...], NT, preferred_element_type=F32)
     for c in range(count):
-        scr[row : row + height, :] = scores[:, c * LANES : (c + 1) * LANES]
+        first[row : row + height, :] = scores[:, c * LANES : (c + 1) * LANES]
         row += height
-    flush(scr, home, away, first_bit(orders, day, index), outs)
-
-
-def second_gram_kernel(orders, place, cell_own, cell_recv, after, home, away, cell, scr, sems, outs):
-    day, index = place[0], place[2]
-    data = load_days(cell_own, cell_recv, cell, day, sems)
-    start_all(data)
-    wait_all(data)
-    rows = cell_own.shape[0]
-    count = rows // UNIT
-    row = 0
-    base = pl.multiple_of(day * rows, rows)
-    for i in range(count):
-        width = (count - i) * UNIT
-        right = cell[pl.ds(base + i * UNIT, width), :]
-        value = lax.dot_general(right[:UNIT, :], right, NT, preferred_element_type=F32)
-        for c in range(count - i):
-            scr[row : row + UNIT, :] = value[:, c * UNIT : (c + 1) * UNIT]
-            row += UNIT
-    side = rows // 2
-    right = cell[pl.ds(rows + pl.multiple_of(day * side, side), side), :]
-    value = lax.dot_general(cell[:rows, :], right, NT, preferred_element_type=F32)
-    for i in range(count):
-        for j in range(count // 2):
-            scr[row : row + UNIT, :] = value[i * UNIT : (i + 1) * UNIT, j * UNIT : (j + 1) * UNIT]
-            row += UNIT
-    flush(scr, home, away, first_bit(orders, day, index), outs)
-
-
-def first_gram(orders, bits, place, cell_map, pred_own, pred_recv, cell_own, start):
+    loads[1].wait()
+    for (i0, j0), (i1, j1) in zip(shares(count)[0][0], shares(count)[1][0]):
+        left = rows_at(pred, i0 + group * (i1 - i0))
+        right = rows_at(pred, j0 + group * (j1 - j0))
+        first[row : row + UNIT, :] = lax.dot_general(left, right, NT, preferred_element_type=F32)
+        row += UNIT
+    last = pltpu.make_async_copy(first, first_out, outs.at[0])
+    last.start()
+    last.wait()
+    save.wait()
+
+
+def rows_at(whole, block):
+    return whole[pl.ds(pl.multiple_of(block * UNIT, UNIT), UNIT), :]
+
+
+def own_gram(place, cell_map, pred_own, cell_own, start):
     rows, width = pred_own.shape
     height = start.shape[0]
-    total = first_rows(rows // UNIT, height, bits)
-    out = jax.ShapeDtypeStruct((total // 2, LANES), F32)
+    count = rows // UNIT
+    number = len(own_blocks(count))
+    first = number // 2 * UNIT + count * height
+    second = number * UNIT
     return pl.pallas_call(
-        functools.partial(first_gram_kernel, orders),
-        out_shape=(out, out),
-        in_specs=[smem_spec()] * 2 + [any_spec()] * 4,
+        own_gram_kernel,
+        out_shape=(jax.ShapeDtypeStruct((first, LANES), F32), jax.ShapeDtypeStruct((second, LANES), F32)),
+        in_specs=[smem_spec()] * 2 + [any_spec()] * 3,
         out_specs=(any_spec(), any_spec()),
         scratch_shapes=[
-            pltpu.VMEM((2 * rows, width), BF16),
+            pltpu.VMEM((rows, width), BF16),
             pltpu.VMEM((rows, width), BF16),
             pltpu.VMEM((height, width), BF16),
-            pltpu.VMEM((total, LANES), F32),
-            pltpu.SemaphoreType.DMA((3,)),
+            pltpu.VMEM((first, LANES), F32),
+            pltpu.VMEM((second, LANES), F32),
+            pltpu.SemaphoreType.DMA((2,)),
             pltpu.SemaphoreType.DMA((cell_map.shape[0],)),
             pltpu.SemaphoreType.DMA((2,)),
         ],
         compiler_params=params(),
-        name="first_gram",
-    )(place, cell_map, pred_own, pred_recv, cell_own, start)
-
-
-def second_gram(orders, bits, place, cell_own, cell_recv, after):
-    rows, width = cell_own.shape
-    total = second_rows(rows // UNIT, bits)
+        name="own_gram",
+    )(place, cell_map, pred_own, cell_own, start)
+
+
+def cross_gram_kernel(orders, shared, place, own, recv, part, home, away, left, right, scr, sems, outs):
+    day, group, index = place[0], place[1], place[2]
+    height, side = left.shape[0], right.shape[0]
+    at_left = pl.ds(pl.multiple_of(group * height, height), height) if shared else pl.ds(0, height)
+    at_right = pl.ds(pl.multiple_of(day * side, side), side)
+    keep = pltpu.make_async_copy(part, scr.at[pl.ds(0, part.shape[0]), :], sems.at[2])
+    keep.start()
+
+    @pl.when(day == 0)
+    def _():
+        pltpu.make_async_copy(own.at[at_left, :], left, sems.at[0]).start()
+        pltpu.make_async_copy(recv.at[at_right, :], right, sems.at[1]).start()
+
+    @pl.when(day == 1)
+    def _():
+        pltpu.make_async_copy(recv.at[at_left, :], left, sems.at[0]).start()
+        pltpu.make_async_copy(own.at[at_right, :], right, sems.at[1]).start()
+
+    pltpu.make_async_copy(own.at[at_left, :], left, sems.at[0]).wait()
+    pltpu.make_async_copy(own.at[at_right, :], right, sems.at[1]).wait()
+    row = part.shape[0]
+    for i in range(height // UNIT):
+        value = lax.dot_general(
+            left[i * UNIT : (i + 1) * UNIT, :], right[...], NT, preferred_element_type=F32
+        )
+        for j in range(side // UNIT):
+            scr[row : row + UNIT, :] = value[:, j * UNIT : (j + 1) * UNIT]
+            row += UNIT
+    keep.wait()
+    flush(scr, home, away, first_bit(orders, day, index), outs)
+
+
+def cross_gram(orders, shared, total, name, place, own, recv, part):
+    rows, width = own.shape
     out = jax.ShapeDtypeStruct((total // 2, LANES), F32)
     return pl.pallas_call(
-        functools.partial(second_gram_kernel, orders),
+        functools.partial(cross_gram_kernel, orders, shared),
         out_shape=(out, out),
         in_specs=[smem_spec()] + [any_spec()] * 3,
         out_specs=(any_spec(), any_spec()),
         scratch_shapes=[
-            pltpu.VMEM((2 * rows, width), BF16),
+            pltpu.VMEM((rows // 2 if shared else rows, width), BF16),
+            pltpu.VMEM((rows // 2, width), BF16),
             pltpu.VMEM((total, LANES), F32),
-            pltpu.SemaphoreType.DMA((2,)),
+            pltpu.SemaphoreType.DMA((3,)),
             pltpu.SemaphoreType.DMA((2,)),
         ],
         compiler_params=params(),
-        name="second_gram",
-    )(place, cell_own, cell_recv, after)
+        name=name,
+    )(place, own, recv, part)
+
+
+def after(value, gate):
+    return lax.optimization_barrier((value, gate))[0]
 
 
 def bit_orders(bits):
@@ -222,6 +231,10 @@
 
 def other_core(value):
     return lax.ppermute(value, "day", [(0, 1), (1, 0)])
+
+
+def other_group(value):
+    return lax.ppermute(value, "group", [(0, 1), (1, 0)])
 
 
 def halve(orders, stage, mine, recv):
@@ -235,20 +248,44 @@
     return home, away
 
 
-def finish_sum(orders, bits, cells, home, recv):
-    for stage in range(1, bits - 1):
+def sum_chunks(orders, bits, cells, first, second):
+    home, away = first
+    late_home, late_away = second
+    last = bits - 1
+    recv = cell_exchange(away, orders, 0, cells)
+    home, away = halve(orders, 1, home, recv)
+    late_away = after(late_away, away)
+    recv = cell_exchange(away, orders, 1, cells)
+    late = cell_exchange(late_away, orders, 0, cells)
+    for stage in range(2, last):
         home, away = halve(orders, stage, home, recv)
         recv = cell_exchange(away, orders, stage, cells)
     part = home + recv
-    part = part + cell_exchange(part, orders, bits - 1, cells)
-    for stage in reversed(range(bits - 1)):
+    middle = cell_exchange(part, orders, last, cells)
+    late_home, late_away = halve(orders, 1, late_home, after(late, part))
+    late = cell_exchange(late_away, orders, 1, cells)
+    for stage in range(2, last):
+        late_home, late_away = halve(orders, stage, late_home, late)
+        late = cell_exchange(late_away, orders, stage, cells)
+    part = part + after(middle, late_away)
+    late_part = after(late_home + late, part)
+    for stage in reversed(range(1, last)):
         part = jnp.concatenate([part, cell_exchange(part, orders, stage, cells)], axis=0)
-    return part
-
-
-def placed_copies(source, target, half, bits, order, cell, sem):
+    late_middle = cell_exchange(late_part, orders, last, cells)
+    other = other_group(part)
+    rest = after(cell_exchange(part, orders, 0, cells), late_part)
+    other_rest = other_group(rest)
+    late_part = late_part + after(after(late_middle, rest), other)
+    for stage in reversed(range(1, last)):
+        recv = cell_exchange(late_part, orders, stage, cells)
+        late_part = jnp.concatenate([late_part, recv if stage > 1 else after(recv, other_rest)], axis=0)
+    late_rest = cell_exchange(late_part, orders, 0, cells)
+    return (part, rest), (other, other_rest), (late_part, late_rest)
+
+
+def placed_copies(sources, target, half, bits, order, cell, sem):
     pieces = 1 << (bits - 1)
-    rows = source.shape[0] // pieces
+    rows = target.shape[1] // pieces
     copies = []
     for p in range(pieces):
         to = 0
@@ -257,9 +294,11 @@
             own = (cell >> order[stage]) & 1
             to = 2 * to + (own ^ digit)
         begin = pl.multiple_of(to * rows, SUB)
+        source = sources[p // (pieces // 2)]
+        at = p % (pieces // 2) * rows
         copies.append(
             pltpu.make_async_copy(
-                source.at[pl.ds(p * rows, rows), :], target.at[half, pl.ds(begin, rows), :], sem.at[p]
+                source.at[pl.ds(at, rows), :], target.at[half, pl.ds(begin, rows), :], sem.at[p]
             )
         )
     return copies
@@ -300,15 +339,13 @@
             gram[s, cols, rows] = piece
 
 
-def assemble_list(packed, core, count, own, cross, gram):
-    row = 0
+def assemble_list(packed, core, row, count, own, cross, gram):
     for i, j in own:
         assemble(packed[core, row : row + UNIT, :], core * count + i, core * count + j, gram)
         row += UNIT
     for i, j in cross:
         assemble(packed[core, row : row + UNIT, :], i, count + core * (count // 2) + j, gram)
         row += UNIT
-    return row
 
 
 def exact_dot(left, right):
@@ -370,10 +407,11 @@
     return exact_dot(inverse, value).astype(BF16)
 
 
-def first_chain_kernel(bits, orders, counts, place, a_own, a_twin, y_own, y_twin,
+def first_chain_kernel(bits, orders, counts, place, a0, a1, y0, y1, a0_twin, a1_twin, y0_twin, y1_twin,
                        gram_out, scores_out, loadings_out, alpha, other, gram, sems, out_sem):
     day, group, index = place[0], place[1], place[2]
-    collect(day, index, bits, orders, ((a_own, a_twin, alpha), (y_own, y_twin, other)), sems)
+    arrays = (((a0, a1), (a0_twin, a1_twin), alpha), ((y0, y1), (y0_twin, y1_twin), other))
+    collect(day, index, bits, orders, arrays, sems)
     days = gram.shape[1]
     count = days // UNIT // 2
     height = scores_out.shape[0]
@@ -381,7 +419,7 @@
     def assemble_all(packs):
         for packed, (own, cross) in zip(packs, shares(count)):
             for core in range(2):
-                assemble_list(packed, core, count, own, cross, gram)
+                assemble_list(packed, core, count * height, count, own, cross, gram)
 
     @pl.when(group == 0)
     def _():
@@ -393,11 +431,7 @@
 
     save = pltpu.make_async_copy(gram, gram_out, out_sem)
     save.start()
-    own, cross = shares(count)[0]
-    begin = (len(own) + len(cross)) * UNIT
-    tiles = [
-        alpha[core, begin + c * height : begin + (c + 1) * height, :] for core in range(2) for c in range(count)
-    ]
+    tiles = [alpha[core, c * height : (c + 1) * height, :] for core in range(2) for c in range(count)]
     scores = jnp.concatenate(tiles, axis=1).astype(BF16)
     scores_out[...] = scores
     inverse, value = half_step(scores, gram, counts[0])
@@ -405,25 +439,25 @@
     save.wait()
 
 
-def first_chain(bits, orders, counts, days, height, place, a_own, a_twin, y_own, y_twin):
+def first_chain(bits, orders, counts, days, height, place, sums):
     pieces = 1 << (bits - 1)
     vmem = pl.BlockSpec(memory_space=pltpu.VMEM)
     panel = jax.ShapeDtypeStruct((height, days), BF16)
     return pl.pallas_call(
         functools.partial(first_chain_kernel, bits, orders, counts),
         out_shape=(jax.ShapeDtypeStruct((SPLITS, days, days), BF16), panel, panel),
-        in_specs=[smem_spec()] + [any_spec()] * 4,
+        in_specs=[smem_spec()] + [any_spec()] * 8,
         out_specs=(any_spec(), vmem, vmem),
         scratch_shapes=[
-            pltpu.VMEM((2,) + a_own.shape, F32),
-            pltpu.VMEM((2,) + a_own.shape, F32),
+            pltpu.VMEM((2, 2 * sums[0].shape[0], LANES), F32),
+            pltpu.VMEM((2, 2 * sums[0].shape[0], LANES), F32),
             pltpu.VMEM((SPLITS, days, days), BF16),
             pltpu.SemaphoreType.DMA((4, pieces)),
             pltpu.SemaphoreType.DMA,
         ],
         compiler_params=params(),
         name="first_chain",
-    )(place, a_own, a_twin, y_own, y_twin)
+    )(place, *sums)
 
 
 def load_tiles(tile_map, own, recv, whole, day, sems):
@@ -452,12 +486,12 @@
             pltpu.make_async_copy(own.at[:, part], whole.at[pl.ds(0, rows), part], sems.at[n, place]).wait()
 
 
-def second_chain_kernel(bits, orders, counts, place, pred_map, cell_map, b_own, b_twin, gram_in, scores_in,
+def second_chain_kernel(bits, orders, counts, place, pred_map, cell_map, b0, b1, b0_twin, b1_twin, gram_in, scores_in,
                         loadings_in, pred_own, pred_recv, cell_own, cell_recv, pred_out, cell_out,
                         beta, pred, cell, pred_gram, cell_gram, sems, gram_sem, pred_sems, cell_sems):
     day, index = place[0], place[2]
     restore = pltpu.make_async_copy(gram_in, pred_gram, gram_sem)
-    collect(day, index, bits, orders, ((b_own, b_twin, beta),), sems)
+    collect(day, index, bits, orders, (((b0, b1), (b0_twin, b1_twin), beta),), sems)
     restore.start()
     load_tiles(pred_map, pred_own, pred_recv, pred, day, pred_sems)
     load_tiles(cell_map, cell_own, cell_recv, cell, day, cell_sems)
@@ -466,7 +500,7 @@
     own = own_blocks(count)
     cross = [(i, j) for i in range(count) for j in range(count // 2)]
     for core in range(2):
-        assemble_list(beta, core, count, own, cross, cell_gram)
+        assemble_list(beta, core, 0, count, own, cross, cell_gram)
     pred_scores, loadings = scores_in[...], loadings_in[...]
     pred_inverse = pred_value = None
     for iteration in range(ITERS):
@@ -486,7 +520,7 @@
     cell_out[...] = exact_dot(cell_inverse, raw)
 
 
-def second_chain(bits, orders, counts, place, pred_map, cell_map, b_own, b_twin, gram, scores, loadings, fields):
+def second_chain(bits, orders, counts, place, pred_map, cell_map, sums, gram, scores, loadings, fields):
     pieces = 1 << (bits - 1)
     height, days = scores.shape
     width = fields[0].shape[1] // 2
@@ -496,10 +530,10 @@
     return pl.pallas_call(
         functools.partial(second_chain_kernel, bits, orders, counts),
         out_shape=(out, out),
-        in_specs=[smem_spec()] * 3 + [any_spec()] * 3 + [vmem] * 2 + [any_spec()] * 4,
+        in_specs=[smem_spec()] * 3 + [any_spec()] * 5 + [vmem] * 2 + [any_spec()] * 4,
         out_specs=(vmem, vmem),
         scratch_shapes=[
-            pltpu.VMEM((2,) + b_own.shape, F32),
+            pltpu.VMEM((2, 2 * sums[0].shape[0], LANES), F32),
             pltpu.VMEM((days, width), BF16),
             pltpu.VMEM((days, width), BF16),
             pltpu.VMEM((SPLITS, days, days), BF16),
@@ -511,7 +545,7 @@
         ],
         compiler_params=params(),
         name="second_chain",
-    )(place, pred_map, cell_map, b_own, b_twin, gram, scores, loadings, *fields)
+    )(place, pred_map, cell_map, *sums, gram, scores, loadings, *fields)
 
 
 def local(predictors, predictand, pred_map, cell_map, start_panel):
@@ -526,22 +560,23 @@
 
     pred_recv = other_core(predictors)
     cell_recv = other_core(predictand)
-    a_home, a_away = first_gram(orders, bits, place, cell_map, predictors, pred_recv, predictand, start_panel)
-    b_home, b_away = second_gram(orders, bits, place, predictand, cell_recv, a_away)
-    a_recv = cell_exchange(a_away, orders, 0, cells)
-    b_away, a_recv = lax.optimization_barrier((b_away, a_recv))
-    a_own = finish_sum(orders, bits, cells, a_home, a_recv)
-    b_recv = cell_exchange(b_away, orders, 0, cells)
-    b_own = finish_sum(orders, bits, cells, b_home, b_recv)
-    y_own = lax.ppermute(a_own, "group", [(0, 1), (1, 0)])
-    a_twin = other_core(a_own)
-    y_twin = other_core(y_own)
-    b_twin = other_core(b_own)
+    count = predictors.shape[0] // UNIT
+    first_part, second_part = own_gram(place, cell_map, predictors, predictand, start_panel)
+    first = cross_gram(
+        orders, True, first_rows(count, height, bits), "first_cross", place, predictors, pred_recv, first_part
+    )
+    second = cross_gram(
+        orders, False, second_rows(count, bits), "second_cross", place, predictand, after(cell_recv, first[1]), second_part
+    )
+    mine, other, late = sum_chunks(orders, bits, cells, first, second)
+    sums = mine + other
     gram, scores, loadings = first_chain(
-        bits, orders, counts, days, height, place, a_own, a_twin, y_own, y_twin
+        bits, orders, counts, days, height, place, sums + tuple(other_core(part) for part in sums)
     )
+    late = (late[0], after(late[1], loadings))
+    late = late + tuple(other_core(part) for part in late)
     return second_chain(
-        bits, orders, counts, place, pred_map, cell_map, b_own, b_twin, gram, scores, loadings,
+        bits, orders, counts, place, pred_map, cell_map, late, gram, scores, loadings,
         (predictors, pred_recv, predictand, cell_recv),
     )
 

time: 140 us -> 125 us (0.89)
  waiting for transfers between devices: 61.1 us -> 39.5 us
  starting transfers between devices: 19.7 us -> 23.4 us
  Pallas kernels: 52.3 us -> 55.9 us
    ppermute x1 -> x2, waiting for transfers between devices: 9.27 us -> 0.01 us  [other_group(): return lax.ppermute(value, 'group', [(0, 1), (1, 0)])]
    ppermute x10, waiting for transfers between devices: 44.1 us -> 35.6 us  [cell_exchange(): return lax.ppermute(value, ('cell', 'day'), pairs)]
    ppermute x5 -> x8, waiting for transfers between devices: 7.76 us -> 3.88 us  [other_core(): return lax.ppermute(value, 'day', [(0, 1), (1, 0)])]
    pallas_call x2 -> x3, Pallas kernels: 12.9 us -> 16.6 us  [the longest x2 9.53 us: cross_gram(): pl.pallas_call(functools.partial(cross_gram_kernel, orders, shared), out_...]
    ppermute x1 -> x2, starting transfers between devices: 1.6 us -> 3.19 us  [other_group(): return lax.ppermute(value, 'group', [(0, 1), (1, 0)])]
    unnamed x18 -> x30, local copies, waits for them, and re-layouts: 3.33 us -> 3.2 us
  transfers between devices with their start and end apart: 16 -> 20, of which waited for: 10 -> 13; matrix products, arithmetic and copies ran while one was open for 1% -> 1% of each run, Pallas kernels for 17% -> 22%
where the time goes in v5:
time: 125 us
  Pallas kernels  55.9 us (45%)
  waiting for transfers between devices  39.5 us (32%)
  starting transfers between devices  23.4 us (19%)
  local copies, waits for them, and re-layouts  3.2 us (3%)
  other arithmetic  1.78 us (1%)
    ppermute x10, waiting for transfers between devices, cell_exchange(): return lax.ppermute(value, ('cell', 'day'), pairs)  35.6 us
    pallas_call x1, Pallas kernels, second_chain(): pl.pallas_call(functools.partial(second_chain_kernel, bits, orders, count...  28.3 us
    ppermute x10, starting transfers between devices, cell_exchange(): return lax.ppermute(value, ('cell', 'day'), pairs)  18.3 us
    pallas_call x1, Pallas kernels, first_chain(): pl.pallas_call(functools.partial(first_chain_kernel, bits, orders, counts...  11.1 us
    pallas_call x2, Pallas kernels, cross_gram(): pl.pallas_call(functools.partial(cross_gram_kernel, orders, shared), out_...  9.53 us
    pallas_call x1, Pallas kernels, own_gram(): pl.pallas_call(own_gram_kernel, out_shape=(jax.ShapeDtypeStruct((first, L...  7.03 us
    ppermute x8, waiting for transfers between devices, other_core(): return lax.ppermute(value, 'day', [(0, 1), (1, 0)])  3.88 us
    unnamed x30, local copies, waits for them, and re-layouts  3.2 us
  transfers between devices with their start and end apart: 20, of which 13 were waited for; matrix products, arithmetic and copies ran while one was open for 1% of the time, Pallas kernels for 22%

profile of v5, /device:TPU:0, one launch (start us, length us, event | category | flops | bytes accessed | tf_op | source)
XLA Modules:
  0.0 124.8 jit_solution(1351963777224381138)
XLA Ops:
  0.6 0.5 collective-permute-start.1
  1.1 0.1 collective-permute-start
  1.2 0.6 pad_add_fusion.place
  1.8 7.0 %own_gram.1 = (f32[896,128]{1,0:T(8,128)}, f32[1280,128]{1,0:T(8,128)}) custom-call(s32[3]{0:T(128)} %pad_add_fusion.place, s32[16]{0:T(128)} %cell_map.3, bf16[512,2048]{1,0:T(8,128)(2,1)} %pred_own.3, bf16[512,2048]{1,0:T(8,128)(2,1)} %cell_own.3, bf16[64,2048]{1,0:T(8,128)(2,1)} %start.1), custom_call_target="tpu_custom_call" | custom-call | tf_op jit(solution)/shard_map/own_gram/pallas_call | solution.py:140
  8.8 0.0 collective-permute-done.1.recv.pred_recv
  8.8 0.0 copy-start
  8.9 1.4 %copy-done = bf16[512,2048]{1,0:T(8,128)(2,1)} copy-done((bf16[512,2048]{1,0:T(8,128)(2,1)}, bf16[512,2048]{1,0:T(8,128)(2,1)S(1)}, u32[]{:S(2)}) %copy-start) | copy-done | bytes 2097176
  10.2 4.1 %first_cross.1 = (f32[704,128]{1,0:T(8,128)}, f32[704,128]{1,0:T(8,128)}) custom-call(s32[3]{0:T(128)} %pad_add_fusion.place, bf16[512,2048]{1,0:T(8,128)(2,1)} %pred_own.3, bf16[512,2048]{1,0:T(8,128)(2,1)} %copy-done, f32[896,128]{1,0:T(8,128)} %get-tuple-element.21.part), custom_call_target="tpu_custom_call" | custom-call | tf_op jit(solution)/shard_map/first_cross/pallas_call | solution.py:195
  14.3 3.0 %collective-permute-start.2 = (f32[704,128]{1,0:T(8,128)}, f32[704,128]{1,0:T(8,128)S(1)}, u32[]{:S(2)}, u32[]{:S(2)}) collective-permute-start(f32[704,128]{1,0:T(8,128)} %get-tuple-element.22), channel_id=1, source_target_pairs={{0,2},{1,5},{2,0},{3,7},{4,6},{5,1},{6,4},{7,3},{8,10},{9,13},{10,... | collective-permute-start | bytes 1081352 | tf_op jit(solution)/shard_map/ppermute | solution.py:229
  17.3 0.0 collective-permute-done.recv.cell_recv
  17.3 5.4 %second_cross.1 = (f32[1152,128]{1,0:T(8,128)}, f32[1152,128]{1,0:T(8,128)}) custom-call(s32[3]{0:T(128)} %pad_add_fusion.place, bf16[512,2048]{1,0:T(8,128)(2,1)} %cell_own.3, bf16[512,2048]{1,0:T(8,128)(2,1)} %collective-permute-done.recv.cell_recv, f32[1280,128]{1,0:T(8,128)} %get-tuple-element.24.part), custom_call_target="tpu_custom_call" | custom-call | tf_op jit(solution)/shard_map/second_cross/pallas_call | solution.py:195
  22.8 0.0 copy-start.3
  22.8 0.2 collective-permute-done.2
  22.9 0.0 copy-done.14
  23.0 2.1 %collective-permute-start.3 = (f32[1152,128]{1,0:T(8,128)}, f32[1152,128]{1,0:T(8,128)S(1)}, u32[]{:S(2)}, u32[]{:S(2)}) collective-permute-start(f32[1152,128]{1,0:T(8,128)} %get-tuple-element.28), channel_id=1, source_target_pairs={{0,2},{1,5},{2,0},{3,7},{4,6},{5,1},{6,4},{7,3},{8,10},{9,13},{10,... | collective-permute-start | bytes 1769480 | tf_op jit(solution)/shard_map/ppermute | solution.py:229
  25.1 1.6 %collective-permute-start.4 = (f32[352,128]{1,0:T(8,128)S(1)}, f32[352,128]{1,0:T(8,128)S(1)}, u32[]{:S(2)}, u32[]{:S(2)}) collective-permute-start(f32[352,128]{1,0:T(8,128)S(1)} %dynamic-slice_add_fusion.1), channel_id=1, source_target_pairs={{0,4},{1,3},{2,6},{3,1},{4,0},{5,7},{6,2},{7,5},{8,12},{9,11},{10,... | collective-permute-start | bytes 540680 | tf_op jit(solution)/shard_map/ppermute | solution.py:229
  26.6 5.9 %collective-permute-done.4 = f32[352,128]{1,0:T(8,128)S(1)} collective-permute-done((f32[352,128]{1,0:T(8,128)S(1)}, f32[352,128]{1,0:T(8,128)S(1)}, u32[]{:S(2)}, u32[]{:S(2)}) %collective-permute-start.4) | collective-permute-done | bytes 180256 | tf_op jit(solution)/shard_map/ppermute | solution.py:229
  32.6 3.7 %collective-permute-start.6 = (f32[352,128]{1,0:T(8,128)S(1)}, f32[352,128]{1,0:T(8,128)S(1)}, u32[]{:S(2)}, u32[]{:S(2)}) collective-permute-start(f32[352,128]{1,0:T(8,128)S(1)} %add_add_fusion.1), channel_id=1, source_target_pairs={{0,8},{1,9},{2,10},{3,11},{4,12},{5,13},{6,14},{7,15},{8,0},{9,1},... | collective-permute-start | bytes 540680 | tf_op jit(solution)/shard_map/ppermute | solution.py:229
  36.3 0.0 collective-permute-done.3
  36.3 1.0 dynamic-slice_add_fusion
  37.3 4.6 %collective-permute-done.6 = f32[352,128]{1,0:T(8,128)S(1)} collective-permute-done((f32[352,128]{1,0:T(8,128)S(1)}, f32[352,128]{1,0:T(8,128)S(1)}, u32[]{:S(2)}, u32[]{:S(2)}) %collective-permute-start.6) | collective-permute-done | bytes 180256 | tf_op jit(solution)/shard_map/ppermute | solution.py:229
  41.9 0.9 collective-permute-start.8
  42.8 1.2 collective-permute-start.5
  44.0 5.3 %collective-permute-done.8 = f32[352,128]{1,0:T(8,128)S(1)} collective-permute-done((f32[352,128]{1,0:T(8,128)S(1)}, f32[352,128]{1,0:T(8,128)S(1)}, u32[]{:S(2)}, u32[]{:S(2)}) %collective-permute-start.8) | collective-permute-done | bytes 180256 | tf_op jit(solution)/shard_map/ppermute | solution.py:229
  49.3 0.0 copy-start.2
  49.3 4.6 %collective-permute-start.9 = (f32[704,128]{1,0:T(8,128)S(1)}, f32[704,128]{1,0:T(8,128)S(1)}, u32[]{:S(2)}, u32[]{:S(2)}) collective-permute-start(f32[704,128]{1,0:T(8,128)S(1)} %pad_maximum_fusion.1.a0), channel_id=1, source_target_pairs={{0,2},{1,5},{2,0},{3,7},{4,6},{5,1},{6,4},{7,3},{8,10},{9,13},{10,... | collective-permute-start | bytes 1081352 | tf_op jit(solution)/shard_map/ppermute | solution.py:229
  53.9 1.6 %collective-permute-start.10 = (f32[704,128]{1,0:T(8,128)S(1)}, f32[704,128]{1,0:T(8,128)S(1)}, u32[]{:S(2)}, u32[]{:S(2)}) collective-permute-start(f32[704,128]{1,0:T(8,128)S(1)} %pad_maximum_fusion.1.a0), channel_id=1, source_target_pairs={{0,16},{16,0},{1,17},{17,1},{2,18},{18,2},{3,19},{19,3},{4,20},{20... | collective-permute-start | bytes 1081352 | tf_op jit(solution)/shard_map/ppermute | solution.py:237
  55.5 1.6 %collective-permute-done.5 = f32[576,128]{1,0:T(8,128)S(1)} collective-permute-done((f32[576,128]{1,0:T(8,128)S(1)}, f32[576,128]{1,0:T(8,128)S(1)}, u32[]{:S(2)}, u32[]{:S(2)}) %collective-permute-start.5) | collective-permute-done | bytes 294944 | tf_op jit(solution)/shard_map/ppermute | solution.py:229
  57.1 0.0 copy-done.3
  57.1 0.9 collective-permute-start.7
  58.0 2.9 %collective-permute-done.9.a1 = f32[704,128]{1,0:T(8,128)S(1)} collective-permute-done((f32[704,128]{1,0:T(8,128)S(1)}, f32[704,128]{1,0:T(8,128)S(1)}, u32[]{:S(2)}, u32[]{:S(2)}) %collective-permute-start.9) | collective-permute-done | bytes 360480 | tf_op jit(solution)/shard_map/ppermute | solution.py:229
  60.9 1.6 %collective-permute-start.12 = (f32[704,128]{1,0:T(8,128)S(1)}, f32[704,128]{1,0:T(8,128)S(1)}, u32[]{:S(2)}, u32[]{:S(2)}) collective-permute-start(f32[704,128]{1,0:T(8,128)S(1)} %collective-permute-done.9.a1), channel_id=1, source_target_pairs={{0,16},{16,0},{1,17},{17,1},{2,18},{18,2},{3,19},{19,3},{4,20},{20... | collective-permute-start | bytes 1081352 | tf_op jit(solution)/shard_map/ppermute | solution.py:237
  62.5 5.2 %collective-permute-done.7 = f32[576,128]{1,0:T(8,128)S(1)} collective-permute-done((f32[576,128]{1,0:T(8,128)S(1)}, f32[576,128]{1,0:T(8,128)S(1)}, u32[]{:S(2)}, u32[]{:S(2)}) %collective-permute-start.7) | collective-permute-done | bytes 294944 | tf_op jit(solution)/shard_map/ppermute | solution.py:229
  67.7 0.0 collective-permute-done.10.y0
  67.8 0.1 collective-permute-start.11
  67.9 9.9 %collective-permute-done.11 = f32[576,128]{1,0:T(8,128)S(1)} collective-permute-done((f32[576,128]{1,0:T(8,128)S(1)}, f32[576,128]{1,0:T(8,128)S(1)}, u32[]{:S(2)}, u32[]{:S(2)}) %collective-permute-start.11) | collective-permute-done | bytes 294944 | tf_op jit(solution)/shard_map/ppermute | solution.py:229
  77.8 0.0 collective-permute-done.12.y1
  77.8 0.0 copy-start.1
  77.8 0.3 collective-permute-start.13
  78.2 0.0 collective-permute-start.14
  78.2 0.5 collective-permute-start.15
  78.7 0.0 collective-permute-start.16
  78.7 0.5 collective-permute-start.17
  79.2 0.7 collective-permute-done.14.a0_twin
  79.8 0.1 collective-permute-start.18
  80.0 0.4 collective-permute-done.15.a1_twin
  80.3 0.5 collective-permute-done.16.y0_twin
  80.9 0.5 collective-permute-done.17.y1_twin
  81.4 0.0 copy-done.2
  81.4 0.0 copy-done.7
  81.4 0.0 copy-done.8
  81.4 0.0 copy-done.9
  81.4 0.0 copy-done.10
  81.4 0.0 copy-done.11
  81.4 0.2 copy-done.12
  81.6 0.7 copy-done.13
  82.3 11.1 %first_chain.1 = (bf16[3,1024,1024]{2,1,0:T(8,128)(2,1)}, bf16[64,1024]{1,0:T(8,128)(2,1)}, bf16[64,1024]{1,0:T(8,128)(2,1)}) custom-call(s32[3]{0:T(128)} %pad_add_fusion.place, f32[704,128]{1,0:T(8,128)} %copy-done.2, f32[704,128]{1,0:T(8,128)} %copy-done.7, f32[704,128]{1,0:T(8,128)} %copy-done.8, f32[704,128]{1,0:T(8,128)} %copy-done.9, ...), custom_call_target="tpu_custom_call" | custom-call | tf_op jit(solution)/shard_map/first_chain/pallas_call | solution.py:446
  93.4 0.0 collective-permute-done.13.b1
  93.4 0.0 copy-start.4
  93.4 0.2 collective-permute-start.19
  93.7 0.0 collective-permute-done.18.b0_twin
  93.7 1.8 %collective-permute-done.19.b1_twin = f32[1152,128]{1,0:T(8,128)S(1)} collective-permute-done((f32[1152,128]{1,0:T(8,128)S(1)}, f32[1152,128]{1,0:T(8,128)S(1)}, u32[]{:S(2)}, u32[]{:S(2)}) %collective-permute-start.19) | collective-permute-done | bytes 589856 | tf_op jit(solution)/shard_map/ppermute | solution.py:233
  95.5 0.9 copy-done.6
  96.4 28.3 %second_chain.1 = (f32[64,1024]{1,0:T(8,128)}, f32[64,1024]{1,0:T(8,128)}) custom-call(s32[3]{0:T(128)} %pad_add_fusion.place, s32[16]{0:T(128)} %pred_map.1, s32[16]{0:T(128)} %cell_map.3, f32[1152,128]{1,0:T(8,128)} %copy-done.1, f32[1152,128]{1,0:T(8,128)} %copy-done.4, f32[1152,128]{1,0:T(8,128)} %copy-done.5, f32[1152,128]{1,0:T(8,128)} %copy-done.6, ...), custom_call_target="tpu_custom_call" | custom-call | tf_op jit(solution)/shard_map/second_chain/pallas_call | solution.py:530
  (20 shorter events, 0.2 us)
Async XLA Ops:
  0.6 8.2 %collective-permute-start.1 = (bf16[512,2048]{1,0:T(8,128)(2,1)}, bf16[512,2048]{1,0:T(8,128)(2,1)S(1)}, u32[]{:S(2)}, u32[]{:S(2)}) collective-permute-start(bf16[512,2048]{1,0:T(8,128)(2,1)} %pred_own.3), channel_id=1, source_target_pairs={{0,1},{1,0},{2,3},{3,2},{4,5},{5,4},{6,7},{7,6},{8,9},{9,8},{10,11... | collective-permute-start | bytes 6291464 | tf_op jit(solution)/shard_map/ppermute | solution.py:233
  1.1 16.2 %collective-permute-start = (bf16[512,2048]{1,0:T(8,128)(2,1)}, bf16[512,2048]{1,0:T(8,128)(2,1)}, u32[]{:S(2)}, u32[]{:S(2)}) collective-permute-start(bf16[512,2048]{1,0:T(8,128)(2,1)} %cell_own.3), channel_id=1, source_target_pairs={{0,1},{1,0},{2,3},{3,2},{4,5},{5,4},{6,7},{7,6},{8,9},{9,8},{10,11... | collective-permute-start | bytes 6291464 | tf_op jit(solution)/shard_map/ppermute | solution.py:233
  8.8 1.4 %copy-start = (bf16[512,2048]{1,0:T(8,128)(2,1)}, bf16[512,2048]{1,0:T(8,128)(2,1)S(1)}, u32[]{:S(2)}) copy-start(bf16[512,2048]{1,0:T(8,128)(2,1)S(1)} %collective-permute-done.1.recv.pred_recv) | copy-start | bytes 6291460
  14.3 8.6 %collective-permute-start.2 = (f32[704,128]{1,0:T(8,128)}, f32[704,128]{1,0:T(8,128)S(1)}, u32[]{:S(2)}, u32[]{:S(2)}) collective-permute-start(f32[704,128]{1,0:T(8,128)} %get-tuple-element.22), channel_id=1, source_target_pairs={{0,2},{1,5},{2,0},{3,7},{4,6},{5,1},{6,4},{7,3},{8,10},{9,13},{10,... | collective-permute-start | bytes 1081352 | tf_op jit(solution)/shard_map/ppermute | solution.py:229
  17.3 5.6 %copy-start.14 = (f32[704,128]{1,0:T(8,128)S(1)}, f32[704,128]{1,0:T(8,128)}, u32[]{:S(2)}) copy-start(f32[704,128]{1,0:T(8,128)} %get-tuple-element.27) | copy-start | bytes 1081348
  22.8 34.3 %copy-start.3 = (f32[1152,128]{1,0:T(8,128)S(1)}, f32[1152,128]{1,0:T(8,128)}, u32[]{:S(2)}) copy-start(f32[1152,128]{1,0:T(8,128)} %get-tuple-element.25) | copy-start | bytes 1769476
  23.0 13.3 %collective-permute-start.3 = (f32[1152,128]{1,0:T(8,128)}, f32[1152,128]{1,0:T(8,128)S(1)}, u32[]{:S(2)}, u32[]{:S(2)}) collective-permute-start(f32[1152,128]{1,0:T(8,128)} %get-tuple-element.28), channel_id=1, source_target_pairs={{0,2},{1,5},{2,0},{3,7},{4,6},{5,1},{6,4},{7,3},{8,10},{9,13},{10,... | collective-permute-start | bytes 1769480 | tf_op jit(solution)/shard_map/ppermute | solution.py:229
  25.1 7.5 %collective-permute-start.4 = (f32[352,128]{1,0:T(8,128)S(1)}, f32[352,128]{1,0:T(8,128)S(1)}, u32[]{:S(2)}, u32[]{:S(2)}) collective-permute-start(f32[352,128]{1,0:T(8,128)S(1)} %dynamic-slice_add_fusion.1), channel_id=1, source_target_pairs={{0,4},{1,3},{2,6},{3,1},{4,0},{5,7},{6,2},{7,5},{8,12},{9,11},{10,... | collective-permute-start | bytes 540680 | tf_op jit(solution)/shard_map/ppermute | solution.py:229
  32.6 9.3 %collective-permute-start.6 = (f32[352,128]{1,0:T(8,128)S(1)}, f32[352,128]{1,0:T(8,128)S(1)}, u32[]{:S(2)}, u32[]{:S(2)}) collective-permute-start(f32[352,128]{1,0:T(8,128)S(1)} %add_add_fusion.1), channel_id=1, source_target_pairs={{0,8},{1,9},{2,10},{3,11},{4,12},{5,13},{6,14},{7,15},{8,0},{9,1},... | collective-permute-start | bytes 540680 | tf_op jit(solution)/shard_map/ppermute | solution.py:229
  41.9 7.4 %collective-permute-start.8 = (f32[352,128]{1,0:T(8,128)S(1)}, f32[352,128]{1,0:T(8,128)S(1)}, u32[]{:S(2)}, u32[]{:S(2)}) collective-permute-start(f32[352,128]{1,0:T(8,128)S(1)} %add.50), channel_id=1, source_target_pairs={{0,4},{1,3},{2,6},{3,1},{4,0},{5,7},{6,2},{7,5},{8,12},{9,11},{10,... | collective-permute-start | bytes 540680 | tf_op jit(solution)/shard_map/ppermute | solution.py:229
  42.8 14.3 %collective-permute-start.5 = (f32[576,128]{1,0:T(8,128)S(1)}, f32[576,128]{1,0:T(8,128)S(1)}, u32[]{:S(2)}, u32[]{:S(2)}) collective-permute-start(f32[576,128]{1,0:T(8,128)S(1)} %dynamic-slice_add_fusion), channel_id=1, source_target_pairs={{0,4},{1,3},{2,6},{3,1},{4,0},{5,7},{6,2},{7,5},{8,12},{9,11},{10,... | collective-permute-start | bytes 884744 | tf_op jit(solution)/shard_map/ppermute | solution.py:229
  49.3 32.1 %copy-start.2 = (f32[704,128]{1,0:T(8,128)}, f32[704,128]{1,0:T(8,128)S(1)}, u32[]{:S(2)}) copy-start(f32[704,128]{1,0:T(8,128)S(1)} %pad_maximum_fusion.1.a0) | copy-start | bytes 1081348
  49.3 11.6 %collective-permute-start.9 = (f32[704,128]{1,0:T(8,128)S(1)}, f32[704,128]{1,0:T(8,128)S(1)}, u32[]{:S(2)}, u32[]{:S(2)}) collective-permute-start(f32[704,128]{1,0:T(8,128)S(1)} %pad_maximum_fusion.1.a0), channel_id=1, source_target_pairs={{0,2},{1,5},{2,0},{3,7},{4,6},{5,1},{6,4},{7,3},{8,10},{9,13},{10,... | collective-permute-start | bytes 1081352 | tf_op jit(solution)/shard_map/ppermute | solution.py:229
  53.9 13.8 %collective-permute-start.10 = (f32[704,128]{1,0:T(8,128)S(1)}, f32[704,128]{1,0:T(8,128)S(1)}, u32[]{:S(2)}, u32[]{:S(2)}) collective-permute-start(f32[704,128]{1,0:T(8,128)S(1)} %pad_maximum_fusion.1.a0), channel_id=1, source_target_pairs={{0,16},{16,0},{1,17},{17,1},{2,18},{18,2},{3,19},{19,3},{4,20},{20... | collective-permute-start | bytes 1081352 | tf_op jit(solution)/shard_map/ppermute | solution.py:237
  57.1 10.6 %collective-permute-start.7 = (f32[576,128]{1,0:T(8,128)S(1)}, f32[576,128]{1,0:T(8,128)S(1)}, u32[]{:S(2)}, u32[]{:S(2)}) collective-permute-start(f32[576,128]{1,0:T(8,128)S(1)} %add_add_fusion), channel_id=1, source_target_pairs={{0,8},{1,9},{2,10},{3,11},{4,12},{5,13},{6,14},{7,15},{8,0},{9,1},... | collective-permute-start | bytes 884744 | tf_op jit(solution)/shard_map/ppermute | solution.py:229
  60.9 20.5 %copy-start.7 = (f32[704,128]{1,0:T(8,128)}, f32[704,128]{1,0:T(8,128)S(1)}, u32[]{:S(2)}) copy-start(f32[704,128]{1,0:T(8,128)S(1)} %collective-permute-done.9.a1) | copy-start | bytes 1081348
  60.9 16.9 %collective-permute-start.12 = (f32[704,128]{1,0:T(8,128)S(1)}, f32[704,128]{1,0:T(8,128)S(1)}, u32[]{:S(2)}, u32[]{:S(2)}) collective-permute-start(f32[704,128]{1,0:T(8,128)S(1)} %collective-permute-done.9.a1), channel_id=1, source_target_pairs={{0,16},{16,0},{1,17},{17,1},{2,18},{18,2},{3,19},{19,3},{4,20},{20... | collective-permute-start | bytes 1081352 | tf_op jit(solution)/shard_map/ppermute | solution.py:237
  67.7 13.6 %copy-start.8 = (f32[704,128]{1,0:T(8,128)}, f32[704,128]{1,0:T(8,128)S(1)}, u32[]{:S(2)}) copy-start(f32[704,128]{1,0:T(8,128)S(1)} %collective-permute-done.10.y0) | copy-start | bytes 1081348
  67.8 10.0 %collective-permute-start.11 = (f32[576,128]{1,0:T(8,128)S(1)}, f32[576,128]{1,0:T(8,128)S(1)}, u32[]{:S(2)}, u32[]{:S(2)}) collective-permute-start(f32[576,128]{1,0:T(8,128)S(1)} %add.51), channel_id=1, source_target_pairs={{0,4},{1,3},{2,6},{3,1},{4,0},{5,7},{6,2},{7,5},{8,12},{9,11},{10,... | collective-permute-start | bytes 884744 | tf_op jit(solution)/shard_map/ppermute | solution.py:229
  77.8 3.6 %copy-start.9 = (f32[704,128]{1,0:T(8,128)}, f32[704,128]{1,0:T(8,128)S(1)}, u32[]{:S(2)}) copy-start(f32[704,128]{1,0:T(8,128)S(1)} %collective-permute-done.12.y1) | copy-start | bytes 1081348
  77.8 17.7 %copy-start.1 = (f32[1152,128]{1,0:T(8,128)}, f32[1152,128]{1,0:T(8,128)S(1)}, u32[]{:S(2)}) copy-start(f32[1152,128]{1,0:T(8,128)S(1)} %pad_maximum_fusion.b0) | copy-start | bytes 1769476
  77.8 15.6 %collective-permute-start.13 = (f32[1152,128]{1,0:T(8,128)S(1)}, f32[1152,128]{1,0:T(8,128)S(1)}, u32[]{:S(2)}, u32[]{:S(2)}) collective-permute-start(f32[1152,128]{1,0:T(8,128)S(1)} %pad_maximum_fusion.b0), channel_id=1, source_target_pairs={{0,2},{1,5},{2,0},{3,7},{4,6},{5,1},{6,4},{7,3},{8,10},{9,13},{10,... | collective-permute-start | bytes 1769480 | tf_op jit(solution)/shard_map/ppermute | solution.py:229
  78.2 1.7 %collective-permute-start.14 = (f32[704,128]{1,0:T(8,128)S(1)}, f32[704,128]{1,0:T(8,128)S(1)}, u32[]{:S(2)}, u32[]{:S(2)}) collective-permute-start(f32[704,128]{1,0:T(8,128)S(1)} %pad_maximum_fusion.1.a0), channel_id=1, source_target_pairs={{0,1},{1,0},{2,3},{3,2},{4,5},{5,4},{6,7},{7,6},{8,9},{9,8},{10,11... | collective-permute-start | bytes 1081352 | tf_op jit(solution)/shard_map/ppermute | solution.py:233
  78.2 2.2 %collective-permute-start.15 = (f32[704,128]{1,0:T(8,128)S(1)}, f32[704,128]{1,0:T(8,128)S(1)}, u32[]{:S(2)}, u32[]{:S(2)}) collective-permute-start(f32[704,128]{1,0:T(8,128)S(1)} %collective-permute-done.9.a1), channel_id=1, source_target_pairs={{0,1},{1,0},{2,3},{3,2},{4,5},{5,4},{6,7},{7,6},{8,9},{9,8},{10,11... | collective-permute-start | bytes 1081352 | tf_op jit(solution)/shard_map/ppermute | solution.py:233
  78.7 2.2 %collective-permute-start.16 = (f32[704,128]{1,0:T(8,128)S(1)}, f32[704,128]{1,0:T(8,128)S(1)}, u32[]{:S(2)}, u32[]{:S(2)}) collective-permute-start(f32[704,128]{1,0:T(8,128)S(1)} %collective-permute-done.10.y0), channel_id=1, source_target_pairs={{0,1},{1,0},{2,3},{3,2},{4,5},{5,4},{6,7},{7,6},{8,9},{9,8},{10,11... | collective-permute-start | bytes 1081352 | tf_op jit(solution)/shard_map/ppermute | solution.py:233
  78.7 2.7 %collective-permute-start.17 = (f32[704,128]{1,0:T(8,128)S(1)}, f32[704,128]{1,0:T(8,128)S(1)}, u32[]{:S(2)}, u32[]{:S(2)}) collective-permute-start(f32[704,128]{1,0:T(8,128)S(1)} %collective-permute-done.12.y1), channel_id=1, source_target_pairs={{0,1},{1,0},{2,3},{3,2},{4,5},{5,4},{6,7},{7,6},{8,9},{9,8},{10,11... | collective-permute-start | bytes 1081352 | tf_op jit(solution)/shard_map/ppermute | solution.py:233
  79.8 1.6 %copy-start.10 = (f32[704,128]{1,0:T(8,128)}, f32[704,128]{1,0:T(8,128)S(1)}, u32[]{:S(2)}) copy-start(f32[704,128]{1,0:T(8,128)S(1)} %collective-permute-done.14.a0_twin) | copy-start | bytes 1081348
  79.8 13.9 %collective-permute-start.18 = (f32[1152,128]{1,0:T(8,128)S(1)}, f32[1152,128]{1,0:T(8,128)S(1)}, u32[]{:S(2)}, u32[]{:S(2)}) collective-permute-start(f32[1152,128]{1,0:T(8,128)S(1)} %pad_maximum_fusion.b0), channel_id=1, source_target_pairs={{0,1},{1,0},{2,3},{3,2},{4,5},{5,4},{6,7},{7,6},{8,9},{9,8},{10,11... | collective-permute-start | bytes 1769480 | tf_op jit(solution)/shard_map/ppermute | solution.py:233
  80.3 1.1 copy-start.11
  80.9 0.7 copy-start.12
  81.6 0.7 copy-start.13
  93.4 2.1 %copy-start.4 = (f32[1152,128]{1,0:T(8,128)}, f32[1152,128]{1,0:T(8,128)S(1)}, u32[]{:S(2)}) copy-start(f32[1152,128]{1,0:T(8,128)S(1)} %collective-permute-done.13.b1) | copy-start | bytes 1769476
  93.4 2.1 %collective-permute-start.19 = (f32[1152,128]{1,0:T(8,128)S(1)}, f32[1152,128]{1,0:T(8,128)S(1)}, u32[]{:S(2)}, u32[]{:S(2)}) collective-permute-start(f32[1152,128]{1,0:T(8,128)S(1)} %collective-permute-done.13.b1), channel_id=1, source_target_pairs={{0,1},{1,0},{2,3},{3,2},{4,5},{5,4},{6,7},{7,6},{8,9},{9,8},{10,11... | collective-permute-start | bytes 1769480 | tf_op jit(solution)/shard_map/ppermute | solution.py:233
  93.7 1.8 %copy-start.5 = (f32[1152,128]{1,0:T(8,128)}, f32[1152,128]{1,0:T(8,128)S(1)}, u32[]{:S(2)}) copy-start(f32[1152,128]{1,0:T(8,128)S(1)} %collective-permute-done.18.b0_twin) | copy-start | bytes 1769476
  95.5 0.9 copy-start.6

commit v6 on v5

v6 whole, which is shorter than its diff:
```python
import functools

import jax
import jax.numpy as jnp
from jax import lax
from jax.experimental import pallas as pl
from jax.experimental.pallas import tpu as pltpu
from jax.sharding import PartitionSpec as P

ITERS = 3
LANES = 128
UNIT = 128
SPLITS = 3
SUB = 8
F32 = jnp.float32
BF16 = jnp.bfloat16
NT = (((1,), (1,)), ((), ()))
MIB = 1024 * 1024


def own_blocks(count):
    return [(i, j) for i in range(count) for j in range(i, count)]


def shares(count):
    own = own_blocks(count)
    cross = [(i, j) for i in range(count) for j in range(count // 2)]
    return [
        (own[: len(own) // 2], cross[: len(cross) // 2]),
        (own[len(own) // 2 :], cross[len(cross) // 2 :]),
    ]


def padded(rows, bits):
    step = SUB << (bits - 1)
    return -(-rows // step) * step


def first_rows(count, height, bits):
    own, cross = shares(count)[0]
    return padded((len(own) + len(cross)) * UNIT + count * height, bits)


def second_rows(count, bits):
    return padded((len(own_blocks(count)) + count * (count // 2)) * UNIT, bits)


def smem_spec():
    return pl.BlockSpec(memory_space=pltpu.SMEM)


def vmem_spec():
    return pl.BlockSpec(memory_space=pltpu.VMEM)


def params(mebibytes):
    return pltpu.CompilerParams(vmem_limit_bytes=mebibytes * MIB)


def first_bit(orders, day, cell):
    return jnp.where(day == 0, (cell >> orders[0][0]) & 1, (cell >> orders[1][0]) & 1)


def own_gram_kernel(place, cell_map, pred, cell, start, first, second, panel):
    group = place[1]
    number = cell_map.shape[0]
    height = panel.shape[0]
    for t in range(number):
        slot = pl.multiple_of(lax.rem(cell_map[t], number) * LANES, LANES)
        panel[:, t * LANES : (t + 1) * LANES] = start[:, pl.ds(slot, LANES)]
    count = cell.shape[0] // UNIT
    row = 0
    scores = lax.dot_general(panel[...], cell[...], NT, preferred_element_type=F32)
    for c in range(count):
        first[row : row + height, :] = scores[:, c * LANES : (c + 1) * LANES]
        row += height
    for (i0, j0), (i1, j1) in zip(shares(count)[0][0], shares(count)[1][0]):
        left = rows_at(pred, i0 + group * (i1 - i0))
        right = rows_at(pred, j0 + group * (j1 - j0))
        first[row : row + UNIT, :] = lax.dot_general(left, right, NT, preferred_element_type=F32)
        row += UNIT
    row = 0
    for i in range(0, count, 2):
        right = cell[i * UNIT :, :]
        value = lax.dot_general(right[: 2 * UNIT, :], right, NT, preferred_element_type=F32)
        for r in range(2):
            for c in range(r, count - i):
                second[row : row + UNIT, :] = value[r * UNIT : (r + 1) * UNIT, c * UNIT : (c + 1) * UNIT]
                row += UNIT


def rows_at(whole, block):
    return whole[pl.ds(pl.multiple_of(block * UNIT, UNIT), UNIT), :]


def own_gram(place, cell_map, pred_own, cell_own, start):
    rows, width = pred_own.shape
    height = start.shape[0]
    count = rows // UNIT
    number = len(own_blocks(count))
    first = number // 2 * UNIT + count * height
    second = number * UNIT
    return pl.pallas_call(
        own_gram_kernel,
        out_shape=(jax.ShapeDtypeStruct((first, LANES), F32), jax.ShapeDtypeStruct((second, LANES), F32)),
        in_specs=[smem_spec()] * 2 + [vmem_spec()] * 3,
        out_specs=(vmem_spec(), vmem_spec()),
        scratch_shapes=[pltpu.VMEM((height, width), BF16)],
        compiler_params=params(16),
        name="own_gram",
    )(place, cell_map, pred_own, cell_own, start)


def own_tiles(tile_map, own, recv, whole, day):
    number = tile_map.shape[0]
    half = number // 2
    rows = own.shape[0]
    mine = pl.ds(pl.multiple_of(day * rows, rows), rows)
    theirs = pl.ds(pl.multiple_of((1 - day) * rows, rows), rows)
    for t in range(number):
        slot = lax.rem(tile_map[t], number)
        to = pl.ds(pl.multiple_of(lax.rem(slot, half) * LANES, LANES), LANES)

        @pl.when(lax.div(slot, half) == day)
        def _():
            whole[mine, to] = own[:, t * LANES : (t + 1) * LANES]
            whole[theirs, to] = recv[:, t * LANES : (t + 1) * LANES]


def cross_blocks(orders, shared, place, own, recv, part, home, away, left, right, scr):
    day, group, index = place[0], place[1], place[2]
    height, side = left.shape[0], right.shape[0]
    at_left = pl.ds(pl.multiple_of(group * height, height), height) if shared else pl.ds(0, height)
    at_right = pl.ds(pl.multiple_of(day * side, side), side)

    @pl.when(day == 0)
    def _():
        left[...] = own[at_left, :]
        right[...] = recv[at_right, :]

    @pl.when(day == 1)
    def _():
        left[...] = recv[at_left, :]
        right[...] = own[at_right, :]

    row = part.shape[0]
    scr[:row, :] = part[...]
    value = lax.dot_general(left[...], right[...], NT, preferred_element_type=F32)
    for i in range(height // UNIT):
        for j in range(side // UNIT):
            scr[row : row + UNIT, :] = value[i * UNIT : (i + 1) * UNIT, j * UNIT : (j + 1) * UNIT]
            row += UNIT
    if row < scr.shape[0]:
        scr[row:, :] = jnp.zeros((scr.shape[0] - row, LANES), F32)
    bit = first_bit(orders, day, index)
    rows = home.shape[0]
    home[...] = scr[pl.ds(pl.multiple_of(bit * rows, SUB), rows), :]
    away[...] = scr[pl.ds(pl.multiple_of((1 - bit) * rows, SUB), rows), :]


def first_cross_kernel(orders, place, own, recv, part, home, away, left, right, scr):
    cross_blocks(orders, True, place, own, recv, part, home, away, left, right, scr)


def second_cross_kernel(orders, place, pred_map, cell_map, pred_own, pred_recv, cell_own, cell_recv, part,
                        home, away, pred_tiles, cell_tiles, left, right, scr):
    cross_blocks(orders, False, place, cell_own, cell_recv, part, home, away, left, right, scr)
    own_tiles(pred_map, pred_own, pred_recv, pred_tiles, place[0])
    own_tiles(cell_map, cell_own, cell_recv, cell_tiles, place[0])


def first_cross(orders, total, place, own, recv, part):
    rows, width = own.shape
    out = jax.ShapeDtypeStruct((total // 2, LANES), F32)
    side = pltpu.VMEM((rows // 2, width), BF16)
    return pl.pallas_call(
        functools.partial(first_cross_kernel, orders),
        out_shape=(out, out),
        in_specs=[smem_spec()] + [vmem_spec()] * 3,
        out_specs=(vmem_spec(),) * 2,
        scratch_shapes=[side, side, pltpu.VMEM((total, LANES), F32)],
        compiler_params=params(12),
        name="first_cross",
    )(place, own, recv, part)


def second_cross(orders, total, place, pred_map, cell_map, pred_own, pred_recv, cell_own, cell_recv, part):
    rows, width = cell_own.shape
    out = jax.ShapeDtypeStruct((total // 2, LANES), F32)
    tiles = jax.ShapeDtypeStruct((2 * rows, width // 2), BF16)
    return pl.pallas_call(
        functools.partial(second_cross_kernel, orders),
        out_shape=(out, out, tiles, tiles),
        in_specs=[smem_spec()] * 3 + [vmem_spec()] * 5,
        out_specs=(vmem_spec(),) * 4,
        scratch_shapes=[
            pltpu.VMEM((rows, width), BF16),
            pltpu.VMEM((rows // 2, width), BF16),
            pltpu.VMEM((total, LANES), F32),
        ],
        compiler_params=params(12),
        name="second_cross",
    )(place, pred_map, cell_map, pred_own, pred_recv, cell_own, cell_recv, part)


def after(value, gate):
    return lax.optimization_barrier((value, gate))[0]


def bit_orders(bits):
    plain = list(range(bits))
    swapped = plain[:]
    if bits > 2:
        swapped[0], swapped[1] = 1, 0
    return plain, swapped


def cell_exchange(value, orders, stage, cells):
    pairs = []
    for c in range(cells):
        for d in range(2):
            pairs.append((2 * c + d, 2 * (c ^ (1 << orders[d][stage])) + d))
    return lax.ppermute(value, ("cell", "day"), pairs)


def other_core(value):
    return lax.ppermute(value, "day", [(0, 1), (1, 0)])


def other_group(value):
    return lax.ppermute(value, "group", [(0, 1), (1, 0)])


def halve(orders, stage, mine, recv):
    bit = jnp.where(lax.axis_index("day") == 0, orders[0][stage], orders[1][stage])
    own = (lax.axis_index("cell") >> bit) & 1
    half = mine.shape[0] // 2
    away = lax.dynamic_slice_in_dim(mine, (1 - own) * half, half, 0)
    away = away + lax.dynamic_slice_in_dim(recv, (1 - own) * half, half, 0)
    home = lax.dynamic_slice_in_dim(mine, own * half, half, 0)
    home = home + lax.dynamic_slice_in_dim(recv, own * half, half, 0)
    return home, away


def sum_chunks(orders, bits, cells, first, second):
    home, away = first
    late_home, late_away = second
    last = bits - 1
    recv = cell_exchange(away, orders, 0, cells)
    home, away = halve(orders, 1, home, recv)
    late_away = after(late_away, away)
    recv = cell_exchange(away, orders, 1, cells)
    late = cell_exchange(late_away, orders, 0, cells)
    for stage in range(2, last):
        home, away = halve(orders, stage, home, recv)
        recv = cell_exchange(away, orders, stage, cells)
    part = home + recv
    middle = cell_exchange(part, orders, last, cells)
    late_home, late_away = halve(orders, 1, late_home, after(late, part))
    late = cell_exchange(late_away, orders, 1, cells)
    for stage in range(2, last):
        late_home, late_away = halve(orders, stage, late_home, late)
        late = cell_exchange(late_away, orders, stage, cells)
    part = part + after(middle, late_away)
    late_part = after(late_home + late, part)
    for stage in reversed(range(1, last)):
        part = jnp.concatenate([part, cell_exchange(part, orders, stage, cells)], axis=0)
    late_middle = cell_exchange(late_part, orders, last, cells)
    other = other_group(part)
    rest = after(cell_exchange(part, orders, 0, cells), late_part)
    other_rest = other_group(rest)
    late_part = late_part + after(after(late_middle, rest), other)
    for stage in reversed(range(1, last)):
        recv = cell_exchange(late_part, orders, stage, cells)
        late_part = jnp.concatenate([late_part, recv if stage > 1 else after(recv, other_rest)], axis=0)
    late_rest = cell_exchange(late_part, orders, 0, cells)
    return (part, rest), (other, other_rest), (late_part, late_rest)


def place_sums(sources, target, core, bits, orders, cell):
    pieces = 1 << (bits - 1)
    rows = target.shape[1] // pieces
    for p in range(pieces):
        to = 0
        for stage in range(bits - 1):
            digit = (p >> (bits - 2 - stage)) & 1
            own = jnp.where(core == 0, (cell >> orders[0][stage]) & 1, (cell >> orders[1][stage]) & 1)
            to = 2 * to + (own ^ digit)
        begin = pl.multiple_of(to * rows, SUB)
        at = p % (pieces // 2) * rows
        target[core, pl.ds(begin, rows), :] = sources[p // (pieces // 2)][at : at + rows, :]


def split3(value):
    first = value.astype(BF16)
    rest = value - first.astype(F32)
    second = rest.astype(BF16)
    third = (rest - second.astype(F32)).astype(BF16)
    return first, second, third


def assemble(value, i, j, gram):
    rows, cols = pl.ds(i * UNIT, UNIT), pl.ds(j * UNIT, UNIT)
    for s, piece in enumerate(split3(value)):
        gram[s, rows, cols] = piece
    if i != j:
        for s, piece in enumerate(split3(value.T)):
            gram[s, cols, rows] = piece


def assemble_list(packed, core, row, count, own, cross, gram):
    for i, j in own:
        assemble(packed[core, row : row + UNIT, :], core * count + i, core * count + j, gram)
        row += UNIT
    for i, j in cross:
        assemble(packed[core, row : row + UNIT, :], i, count + core * (count // 2) + j, gram)
        row += UNIT


def exact_dot(left, right):
    return jnp.dot(left, right, precision=lax.Precision.HIGHEST, preferred_element_type=F32)


def inverse_factor(moments):
    size = moments.shape[0]
    row_ids = lax.broadcasted_iota(jnp.int32, (size, size), 0)
    col_ids = lax.broadcasted_iota(jnp.int32, (size, size), 1)
    work = jnp.concatenate([(row_ids == col_ids).astype(F32), moments], axis=1)
    shape = (SUB, 2 * size)
    sub = lax.broadcasted_iota(jnp.int32, shape, 0)
    rows = [work[SUB * i : SUB * i + SUB, :] for i in range(size // SUB)]
    out = []
    for b in range(size // SUB):
        lane = size + SUB * b
        head = rows[b]
        cols = [jnp.broadcast_to(head[:, lane + c : lane + c + 1], shape) for c in range(SUB)]
        entry = [[jnp.broadcast_to(cols[c][r : r + 1, :], shape) for c in range(r + 1)] for r in range(SUB)]
        y = [jnp.broadcast_to(head[r : r + 1, :], shape) for r in range(SUB)]
        inverse = []
        factor = [[None] * SUB for _ in range(SUB)]
        for k in range(SUB):
            inverse.append(1.0 / entry[k][k])
            for i in range(k + 1, SUB):
                factor[i][k] = entry[i][k] * inverse[k]
                for j in range(k + 1, i + 1):
                    entry[i][j] = entry[i][j] - factor[i][k] * entry[j][k]
                y[i] = y[i] - factor[i][k] * y[k]
        p = [y[k] * inverse[k] for k in range(SUB)]
        for i in reversed(range(SUB)):
            for k in range(i):
                p[k] = p[k] - factor[i][k] * p[i]
        for i in range(b + 1, size // SUB):
            terms = [jnp.broadcast_to(rows[i][:, lane + k : lane + k + 1], shape) * p[k] for k in range(SUB)]
            while len(terms) > 1:
                terms = [terms[t] + terms[t + 1] for t in range(0, len(terms), 2)]
            rows[i] = rows[i] - terms[0]
        result, pivot = y[0], entry[0][0]
        for k in range(1, SUB):
            result = jnp.where(sub == k, y[k], result)
            pivot = jnp.where(sub == k, entry[k][k], pivot)
        out.append(result * (1.0 / jnp.sqrt(pivot)))
    return jnp.concatenate(out, axis=0)[:, :size]


def half_step(scores, gram, cells):
    value = jnp.dot(scores, gram[0], preferred_element_type=F32)
    for s in range(1, SPLITS):
        value = value + jnp.dot(scores, gram[s], preferred_element_type=F32)
    moments = sum(
        lax.dot_general(piece, scores, NT, preferred_element_type=F32) for piece in split3(value)
    )
    return inverse_factor(moments / cells), value


def next_scores(inverse, value):
    return exact_dot(inverse, value).astype(BF16)


def first_chain_kernel(bits, orders, counts, place, a0, a1, y0, y1, a0_twin, a1_twin, y0_twin, y1_twin,
                       gram, scores_out, loadings_out, alpha, other):
    day, group, index = place[0], place[1], place[2]
    place_sums((a0, a1), alpha, day, bits, orders, index)
    place_sums((a0_twin, a1_twin), alpha, 1 - day, bits, orders, index)
    place_sums((y0, y1), other, day, bits, orders, index)
    place_sums((y0_twin, y1_twin), other, 1 - day, bits, orders, index)
    days = gram.shape[1]
    count = days // UNIT // 2
    height = scores_out.shape[0]

    def assemble_all(packs):
        for packed, (own, cross) in zip(packs, shares(count)):
            for core in range(2):
                assemble_list(packed, core, count * height, count, own, cross, gram)

    @pl.when(group == 0)
    def _():
        assemble_all((alpha, other))

    @pl.when(group == 1)
    def _():
        assemble_all((other, alpha))

    tiles = [alpha[core, c * height : (c + 1) * height, :] for core in range(2) for c in range(count)]
    scores = jnp.concatenate(tiles, axis=1).astype(BF16)
    scores_out[...] = scores
    inverse, value = half_step(scores, gram, counts[0])
    loadings_out[...] = next_scores(inverse, value)


def first_chain(bits, orders, counts, days, height, place, sums):
    panel = jax.ShapeDtypeStruct((height, days), BF16)
    packed = pltpu.VMEM((2, 2 * sums[0].shape[0], LANES), F32)
    return pl.pallas_call(
        functools.partial(first_chain_kernel, bits, orders, counts),
        out_shape=(jax.ShapeDtypeStruct((SPLITS, days, days), BF16), panel, panel),
        in_specs=[smem_spec()] + [vmem_spec()] * 8,
        out_specs=(vmem_spec(),) * 3,
        scratch_shapes=[packed, packed],
        compiler_params=params(20),
        name="first_chain",
    )(place, *sums)


def second_chain_kernel(bits, orders, counts, place, b0, b1, b0_twin, b1_twin, pred_gram,
                        scores_in, loadings_in, pred, cell, pred_out, cell_out, beta, cell_gram):
    day, index = place[0], place[2]
    place_sums((b0, b1), beta, day, bits, orders, index)
    place_sums((b0_twin, b1_twin), beta, 1 - day, bits, orders, index)
    days = pred.shape[0]
    count = days // UNIT // 2
    own = own_blocks(count)
    cross = [(i, j) for i in range(count) for j in range(count // 2)]
    for core in range(2):
        assemble_list(beta, core, 0, count, own, cross, cell_gram)
    pred_scores, loadings = scores_in[...], loadings_in[...]
    pred_inverse = pred_value = None
    for iteration in range(ITERS):
        if iteration > 0 or ITERS == 1:
            pred_inverse, pred_value = half_step(pred_scores, pred_gram, counts[0])
            loadings = next_scores(pred_inverse, pred_value)
        cell_inverse, cell_value = half_step(loadings, cell_gram, counts[1])
        if iteration < ITERS - 1:
            pred_scores = next_scores(cell_inverse, cell_value)
    raw = jnp.dot(pred_scores, pred[...], preferred_element_type=F32)
    pred_out[...] = exact_dot(pred_inverse, raw)
    raw = jnp.dot(loadings, cell[...], preferred_element_type=F32)
    cell_out[...] = exact_dot(cell_inverse, raw)


def second_chain(bits, orders, counts, place, sums, gram, scores, loadings, pred, cell):
    height, days = scores.shape
    out = jax.ShapeDtypeStruct((height, pred.shape[1]), F32)
    return pl.pallas_call(
        functools.partial(second_chain_kernel, bits, orders, counts),
        out_shape=(out, out),
        in_specs=[smem_spec()] + [vmem_spec()] * 9,
        out_specs=(vmem_spec(), vmem_spec()),
        scratch_shapes=[
            pltpu.VMEM((2, 2 * sums[0].shape[0], LANES), F32),
            pltpu.VMEM((SPLITS, days, days), BF16),
        ],
        compiler_params=params(24),
        name="second_chain",
    )(place, *sums, gram, scores, loadings, pred, cell)


def local(predictors, predictand, pred_map, cell_map, start_panel):
    cells = lax.axis_size("cell")
    bits = cells.bit_length() - 1
    orders = bit_orders(bits)
    days = predictors.shape[0] * 2
    height = start_panel.shape[0]
    counts = (float(predictors.shape[1] * cells), float(predictand.shape[1] * cells))
    place = jnp.stack([lax.axis_index("day"), lax.axis_index("group"), lax.axis_index("cell")])
    place = place.astype(jnp.int32)

    pred_recv = other_core(predictors)
    cell_recv = other_core(predictand)
    count = predictors.shape[0] // UNIT
    first_part, second_part = own_gram(place, cell_map, predictors, predictand, start_panel)
    first = first_cross(orders, first_rows(count, height, bits), place, predictors, pred_recv, first_part)
    home, away, pred, cell = second_cross(
        orders, second_rows(count, bits), place, pred_map, cell_map,
        predictors, pred_recv, predictand, after(cell_recv, first[1]), second_part,
    )
    second = (home, away)
    mine, other, late = sum_chunks(orders, bits, cells, first, second)
    sums = mine + other
    gram, scores, loadings = first_chain(
        bits, orders, counts, days, height, place, sums + tuple(other_core(part) for part in sums)
    )
    late = (late[0], after(late[1], loadings))
    late = late + tuple(other_core(part) for part in late)
    return second_chain(bits, orders, counts, place, late, gram, scores, loadings, pred, cell)


def solution(mesh):
    in_specs = (
        P("day", "cell"),
        P("day", ("group", "cell")),
        P("cell"),
        P(("group", "cell")),
        P(None, ("group", "cell")),
    )
    out_specs = (P(None, ("group", "cell", "day")), P(None, ("group", "cell", "day")))
    return jax.shard_map(local, mesh=mesh, in_specs=in_specs, out_specs=out_specs, check_vma=False)
```

time: 125 us -> 115 us (0.920)
  Pallas kernels: 55.9 us -> 39.6 us
  local copies, waits for them, and re-layouts: 3.2 us -> 9.82 us
  starting transfers between devices: 23.4 us -> 18.5 us
  waiting for transfers between devices: 39.5 us -> 43.2 us
    unnamed x30 -> x28, local copies, waits for them, and re-layouts: 3.2 us -> 9.82 us
    pallas_call x1, Pallas kernels: 28.3 us -> 21.7 us  [second_chain(): pl.pallas_call(functools.partial(second_chain_kernel, bits, orders, count...]
    pallas_call x1, Pallas kernels: 11.1 us -> 6.36 us  [first_chain(): pl.pallas_call(functools.partial(first_chain_kernel, bits, orders, counts...]
    ppermute x10, starting transfers between devices: 18.3 us -> 13.8 us  [cell_exchange(): return lax.ppermute(value, ('cell', 'day'), pairs)]
    pallas_call x1, Pallas kernels: 7.03 us -> 2.85 us  [own_gram(): pl.pallas_call(own_gram_kernel, out_shape=(jax.ShapeDtypeStruct((first, L...]
    ppermute x10, waiting for transfers between devices: 35.6 us -> 39.3 us  [cell_exchange(): return lax.ppermute(value, ('cell', 'day'), pairs)]
  transfers between devices with their start and end apart: 20 -> 20, of which waited for: 13 -> 11; matrix products, arithmetic and copies ran while one was open for 1% -> 1% of each run, Pallas kernels for 22% -> 16%
where the time goes in v6:
time: 115 us; the launch traced here: 114 us
  waiting for transfers between devices  43.2 us (38%)
  Pallas kernels  39.6 us (34%)
  starting transfers between devices  18.5 us (16%)
  local copies, waits for them, and re-layouts  9.82 us (9%)
  other arithmetic  2.25 us (2%)
    ppermute x10, waiting for transfers between devices, cell_exchange(): return lax.ppermute(value, ('cell', 'day'), pairs)  39.3 us
    pallas_call x1, Pallas kernels, second_chain(): pl.pallas_call(functools.partial(second_chain_kernel, bits, orders, count...  21.7 us
    ppermute x10, starting transfers between devices, cell_exchange(): return lax.ppermute(value, ('cell', 'day'), pairs)  13.8 us
    unnamed x28, local copies, waits for them, and re-layouts  9.82 us
    pallas_call x1, Pallas kernels, first_chain(): pl.pallas_call(functools.partial(first_chain_kernel, bits, orders, counts...  6.36 us
    pallas_call x1, Pallas kernels, second_cross(): pl.pallas_call(functools.partial(second_cross_kernel, orders), out_shape=...  5.69 us
    ppermute x8, waiting for transfers between devices, other_core(): return lax.ppermute(value, 'day', [(0, 1), (1, 0)])  3.93 us
    pallas_call x1, Pallas kernels, first_cross(): pl.pallas_call(functools.partial(first_cross_kernel, orders), out_shape=(...  3.06 us
  transfers between devices with their start and end apart: 20, of which 11 were waited for; matrix products, arithmetic and copies ran while one was open for 1% of the time, Pallas kernels for 16%

profile of v6, /device:TPU:0, one launch (start us, length us, event | category | flops | bytes accessed | tf_op | source)
XLA Modules:
  0.0 114.3 jit_solution(8930164977890371589)
XLA Ops:
  0.6 0.5 collective-permute-start
  1.1 0.1 collective-permute-start.1
  1.2 0.1 pad_add_fusion.place
  1.3 1.6 %copy-done = bf16[512,2048]{1,0:T(8,128)(2,1)S(1)} copy-done((bf16[512,2048]{1,0:T(8,128)(2,1)S(1)}, bf16[512,2048]{1,0:T(8,128)(2,1)}, u32[]{:S(2)}) %copy-start) | copy-done | bytes 2097176
  2.9 1.6 %copy-done.2 = bf16[512,2048]{1,0:T(8,128)(2,1)S(1)} copy-done((bf16[512,2048]{1,0:T(8,128)(2,1)S(1)}, bf16[512,2048]{1,0:T(8,128)(2,1)}, u32[]{:S(2)}) %copy-start.2) | copy-done | bytes 2097176
  4.5 0.9 copy-done.10
  5.4 0.7 copy-done.11
  6.1 2.8 %own_gram.1 = (f32[896,128]{1,0:T(8,128)S(1)}, f32[1280,128]{1,0:T(8,128)S(1)}) custom-call(s32[3]{0:T(128)S(1)} %pad_add_fusion.place, s32[16]{0:T(128)S(1)} %copy-done.11, bf16[512,2048]{1,0:T(8,128)(2,1)S(1)} %copy-done, bf16[512,2048]{1,0:T(8,128)(2,1)S(1)} %copy-done.2, bf16[64,2048]{1,0:T(8,128)(2,1)S(1)} %copy-done.10), custom_call_target="tpu_custom_call" | custom-call | tf_op jit(solution)/shard_map/own_gram/pallas_call | solution.py:103
  9.0 0.0 collective-permute-done.recv.pred_recv
  9.0 0.0 copy-done.1
  9.0 0.0 copy-start.12
  9.0 0.0 copy-start.13
  9.0 3.1 %first_cross.1 = (f32[704,128]{1,0:T(8,128)S(1)}, f32[704,128]{1,0:T(8,128)}) custom-call(s32[3]{0:T(128)S(1)} %pad_add_fusion.place, bf16[512,2048]{1,0:T(8,128)(2,1)S(1)} %copy-done.1, bf16[512,2048]{1,0:T(8,128)(2,1)} %collective-permute-done.recv.pred_recv, f32[896,128]{1,0:T(8,128)S(1)} %get-tuple-element.23.part), custom_call_target="tpu_custom_call" | custom-call | tf_op jit(solution)/shard_map/first_cross/pallas_call | solution.py:176
  12.1 0.7 copy-done.8
  12.8 2.9 %collective-permute-start.2 = (f32[704,128]{1,0:T(8,128)}, f32[704,128]{1,0:T(8,128)}, u32[]{:S(2)}, u32[]{:S(2)}) collective-permute-start(f32[704,128]{1,0:T(8,128)} %get-tuple-element.24), channel_id=1, source_target_pairs={{0,2},{1,5},{2,0},{3,7},{4,6},{5,1},{6,4},{7,3},{8,10},{9,13},{10,... | collective-permute-start | bytes 1081352 | tf_op jit(solution)/shard_map/ppermute | solution.py:223
  15.7 0.0 collective-permute-done.1.cell_recv
  15.7 0.0 copy-done.12
  15.7 0.0 copy-done.13
  15.7 0.0 copy-start.3
  15.7 1.6 %copy-done.3 = bf16[512,2048]{1,0:T(8,128)(2,1)S(1)} copy-done((bf16[512,2048]{1,0:T(8,128)(2,1)S(1)}, bf16[512,2048]{1,0:T(8,128)(2,1)}, u32[]{:S(2)}) %copy-start.3) | copy-done | bytes 2097176
  17.3 5.7 %second_cross.1 = (f32[1152,128]{1,0:T(8,128)S(1)}, f32[1152,128]{1,0:T(8,128)}, bf16[1024,1024]{1,0:T(8,128)(2,1)S(1)}, bf16[1024,1024]{1,0:T(8,128)(2,1)S(1)}) custom-call(s32[3]{0:T(128)S(1)} %pad_add_fusion.place, s32[16]{0:T(128)S(1)} %copy-done.13, s32[16]{0:T(128)S(1)} %copy-done.12, bf16[512,2048]{1,0:T(8,128)(2,1)S(1)} %copy-done.1, ...), custom_call_target="tpu_custom_call" | custom-call | tf_op jit(solution)/shard_map/second_cross/pallas_call | solution.py:191
  23.0 1.4 %copy-done.4 = bf16[1024,1024]{1,0:T(8,128)(2,1)} copy-done((bf16[1024,1024]{1,0:T(8,128)(2,1)}, bf16[1024,1024]{1,0:T(8,128)(2,1)S(1)}, u32[]{:S(2)}) %copy-start.4) | copy-done | bytes 2097176
  24.4 1.3 %copy-done.6 = bf16[1024,1024]{1,0:T(8,128)(2,1)} copy-done((bf16[1024,1024]{1,0:T(8,128)(2,1)}, bf16[1024,1024]{1,0:T(8,128)(2,1)S(1)}, u32[]{:S(2)}) %copy-start.6) | copy-done | bytes 2097176
  25.7 0.0 collective-permute-done.2
  25.7 0.0 copy-done.9
  25.7 1.0 dynamic-slice_add_fusion.1
  26.7 0.1 collective-permute-start.3
  26.7 2.1 %collective-permute-start.4 = (f32[352,128]{1,0:T(8,128)S(1)}, f32[352,128]{1,0:T(8,128)S(1)}, u32[]{:S(2)}, u32[]{:S(2)}) collective-permute-start(f32[352,128]{1,0:T(8,128)S(1)} %dynamic-slice_add_fusion.1), channel_id=1, source_target_pairs={{0,4},{1,3},{2,6},{3,1},{4,0},{5,7},{6,2},{7,5},{8,12},{9,11},{10,... | collective-permute-start | bytes 540680 | tf_op jit(solution)/shard_map/ppermute | solution.py:223
  28.8 5.4 %collective-permute-done.4 = f32[352,128]{1,0:T(8,128)S(1)} collective-permute-done((f32[352,128]{1,0:T(8,128)S(1)}, f32[352,128]{1,0:T(8,128)S(1)}, u32[]{:S(2)}, u32[]{:S(2)}) %collective-permute-start.4) | collective-permute-done | bytes 180256 | tf_op jit(solution)/shard_map/ppermute | solution.py:223
  34.2 1.0 add_add_fusion.1
  35.3 3.2 %collective-permute-start.6 = (f32[352,128]{1,0:T(8,128)S(1)}, f32[352,128]{1,0:T(8,128)S(1)}, u32[]{:S(2)}, u32[]{:S(2)}) collective-permute-start(f32[352,128]{1,0:T(8,128)S(1)} %add_add_fusion.1), channel_id=1, source_target_pairs={{0,8},{1,9},{2,10},{3,11},{4,12},{5,13},{6,14},{7,15},{8,0},{9,1},... | collective-permute-start | bytes 540680 | tf_op jit(solution)/shard_map/ppermute | solution.py:223
  38.5 0.0 collective-permute-done.3
  38.5 7.0 %collective-permute-done.6 = f32[352,128]{1,0:T(8,128)S(1)} collective-permute-done((f32[352,128]{1,0:T(8,128)S(1)}, f32[352,128]{1,0:T(8,128)S(1)}, u32[]{:S(2)}, u32[]{:S(2)}) %collective-permute-start.6) | collective-permute-done | bytes 180256 | tf_op jit(solution)/shard_map/ppermute | solution.py:223
  45.5 0.1 collective-permute-start.8
  45.6 2.0 %collective-permute-start.5 = (f32[576,128]{1,0:T(8,128)S(1)}, f32[576,128]{1,0:T(8,128)S(1)}, u32[]{:S(2)}, u32[]{:S(2)}) collective-permute-start(f32[576,128]{1,0:T(8,128)S(1)} %dynamic-slice_add_fusion), channel_id=1, source_target_pairs={{0,4},{1,3},{2,6},{3,1},{4,0},{5,7},{6,2},{7,5},{8,12},{9,11},{10,... | collective-permute-start | bytes 884744 | tf_op jit(solution)/shard_map/ppermute | solution.py:223
  47.6 3.5 %collective-permute-done.8 = f32[352,128]{1,0:T(8,128)S(1)} collective-permute-done((f32[352,128]{1,0:T(8,128)S(1)}, f32[352,128]{1,0:T(8,128)S(1)}, u32[]{:S(2)}, u32[]{:S(2)}) %collective-permute-start.8) | collective-permute-done | bytes 180256 | tf_op jit(solution)/shard_map/ppermute | solution.py:223
  51.1 1.7 %collective-permute-start.9 = (f32[704,128]{1,0:T(8,128)S(1)}, f32[704,128]{1,0:T(8,128)S(1)}, u32[]{:S(2)}, u32[]{:S(2)}) collective-permute-start(f32[704,128]{1,0:T(8,128)S(1)} %pad_maximum_fusion.1.a0), channel_id=1, source_target_pairs={{0,2},{1,5},{2,0},{3,7},{4,6},{5,1},{6,4},{7,3},{8,10},{9,13},{10,... | collective-permute-start | bytes 1081352 | tf_op jit(solution)/shard_map/ppermute | solution.py:223
  52.8 1.4 %collective-permute-start.10 = (f32[704,128]{1,0:T(8,128)S(1)}, f32[704,128]{1,0:T(8,128)S(1)}, u32[]{:S(2)}, u32[]{:S(2)}) collective-permute-start(f32[704,128]{1,0:T(8,128)S(1)} %pad_maximum_fusion.1.a0), channel_id=1, source_target_pairs={{0,16},{16,0},{1,17},{17,1},{2,18},{18,2},{3,19},{19,3},{4,20},{20... | collective-permute-start | bytes 1081352 | tf_op jit(solution)/shard_map/ppermute | solution.py:231
  54.2 6.3 %collective-permute-done.5 = f32[576,128]{1,0:T(8,128)S(1)} collective-permute-done((f32[576,128]{1,0:T(8,128)S(1)}, f32[576,128]{1,0:T(8,128)S(1)}, u32[]{:S(2)}, u32[]{:S(2)}) %collective-permute-start.5) | collective-permute-done | bytes 294944 | tf_op jit(solution)/shard_map/ppermute | solution.py:223
  60.6 0.1 collective-permute-start.7
  60.6 0.0 collective-permute-done.9.a1
  60.7 1.4 %collective-permute-start.12 = (f32[704,128]{1,0:T(8,128)S(1)}, f32[704,128]{1,0:T(8,128)S(1)}, u32[]{:S(2)}, u32[]{:S(2)}) collective-permute-start(f32[704,128]{1,0:T(8,128)S(1)} %collective-permute-done.9.a1), channel_id=1, source_target_pairs={{0,16},{16,0},{1,17},{17,1},{2,18},{18,2},{3,19},{19,3},{4,20},{20... | collective-permute-start | bytes 1081352 | tf_op jit(solution)/shard_map/ppermute | solution.py:231
  62.0 8.3 %collective-permute-done.7 = f32[576,128]{1,0:T(8,128)S(1)} collective-permute-done((f32[576,128]{1,0:T(8,128)S(1)}, f32[576,128]{1,0:T(8,128)S(1)}, u32[]{:S(2)}, u32[]{:S(2)}) %collective-permute-start.7) | collective-permute-done | bytes 294944 | tf_op jit(solution)/shard_map/ppermute | solution.py:223
  70.4 0.0 collective-permute-done.10.y0
  70.4 0.1 collective-permute-start.11
  70.5 8.8 %collective-permute-done.11 = f32[576,128]{1,0:T(8,128)S(1)} collective-permute-done((f32[576,128]{1,0:T(8,128)S(1)}, f32[576,128]{1,0:T(8,128)S(1)}, u32[]{:S(2)}, u32[]{:S(2)}) %collective-permute-start.11) | collective-permute-done | bytes 294944 | tf_op jit(solution)/shard_map/ppermute | solution.py:223
  79.3 0.0 collective-permute-done.12.y1
  79.3 1.6 %collective-permute-start.13 = (f32[1152,128]{1,0:T(8,128)S(1)}, f32[1152,128]{1,0:T(8,128)S(1)}, u32[]{:S(2)}, u32[]{:S(2)}) collective-permute-start(f32[1152,128]{1,0:T(8,128)S(1)} %pad_maximum_fusion.b0), channel_id=1, source_target_pairs={{0,2},{1,5},{2,0},{3,7},{4,6},{5,1},{6,4},{7,3},{8,10},{9,13},{10,... | collective-permute-start | bytes 1769480 | tf_op jit(solution)/shard_map/ppermute | solution.py:223
  80.9 0.0 collective-permute-start.14
  80.9 0.5 collective-permute-start.15
  81.4 0.0 collective-permute-start.16
  81.4 0.5 collective-permute-start.17
  81.9 0.7 collective-permute-done.14.a0_twin
  82.6 0.1 collective-permute-start.18
  82.7 0.4 collective-permute-done.15.a1_twin
  83.1 0.5 collective-permute-done.16.y0_twin
  83.6 0.5 collective-permute-done.17.y1_twin
  84.1 6.4 %first_chain.1 = (bf16[3,1024,1024]{2,1,0:T(8,128)(2,1)S(1)}, bf16[64,1024]{1,0:T(8,128)(2,1)S(1)}, bf16[64,1024]{1,0:T(8,128)(2,1)S(1)}) custom-call(s32[3]{0:T(128)S(1)} %pad_add_fusion.place, f32[704,128]{1,0:T(8,128)S(1)} %pad_maximum_fusion.1.a0, f32[704,128]{1,0:T(8,128)S(1)} %collective-permute-done.9.a1, f32[704,128]{1,0:T(8,128)S(1)} %collective-permute-done.10.y0, ...), custom_call_target="tpu_custom_call" | custom-call | tf_op jit(solution)/shard_map/first_chain/pallas_call | solution.py:413
  90.5 0.0 collective-permute-done.13.b1
  90.5 0.2 collective-permute-start.19
  90.7 0.0 collective-permute-done.18.b0_twin
  90.7 1.9 %collective-permute-done.19.b1_twin = f32[1152,128]{1,0:T(8,128)S(1)} collective-permute-done((f32[1152,128]{1,0:T(8,128)S(1)}, f32[1152,128]{1,0:T(8,128)S(1)}, u32[]{:S(2)}, u32[]{:S(2)}) %collective-permute-start.19) | collective-permute-done | bytes 589856 | tf_op jit(solution)/shard_map/ppermute | solution.py:227
  92.6 0.0 copy-done.7
  92.6 21.7 %second_chain.1 = (f32[64,1024]{1,0:T(8,128)}, f32[64,1024]{1,0:T(8,128)}) custom-call(s32[3]{0:T(128)S(1)} %pad_add_fusion.place, f32[1152,128]{1,0:T(8,128)S(1)} %pad_maximum_fusion.b0, f32[1152,128]{1,0:T(8,128)S(1)} %collective-permute-done.13.b1, f32[1152,128]{1,0:T(8,128)S(1)} %collective-permute-done.18.b0_twin, ...), custom_call_target="tpu_custom_call" | custom-call | tf_op jit(solution)/shard_map/second_chain/pallas_call | solution.py:453
  (18 shorter events, 0.2 us)
Async XLA Ops:
  0.6 8.3 %collective-permute-start = (bf16[512,2048]{1,0:T(8,128)(2,1)}, bf16[512,2048]{1,0:T(8,128)(2,1)}, u32[]{:S(2)}, u32[]{:S(2)}) collective-permute-start(bf16[512,2048]{1,0:T(8,128)(2,1)} %pred_own.1), channel_id=1, source_target_pairs={{0,1},{1,0},{2,3},{3,2},{4,5},{5,4},{6,7},{7,6},{8,9},{9,8},{10,11... | collective-permute-start | bytes 6291464 | tf_op jit(solution)/shard_map/ppermute | solution.py:227
  1.1 14.6 %collective-permute-start.1 = (bf16[512,2048]{1,0:T(8,128)(2,1)}, bf16[512,2048]{1,0:T(8,128)(2,1)}, u32[]{:S(2)}, u32[]{:S(2)}) collective-permute-start(bf16[512,2048]{1,0:T(8,128)(2,1)} %cell_own.1), channel_id=1, source_target_pairs={{0,1},{1,0},{2,3},{3,2},{4,5},{5,4},{6,7},{7,6},{8,9},{9,8},{10,11... | collective-permute-start | bytes 6291464 | tf_op jit(solution)/shard_map/ppermute | solution.py:227
  1.3 1.6 %copy-start = (bf16[512,2048]{1,0:T(8,128)(2,1)S(1)}, bf16[512,2048]{1,0:T(8,128)(2,1)}, u32[]{:S(2)}) copy-start(bf16[512,2048]{1,0:T(8,128)(2,1)} %pred_own.1) | copy-start | bytes 6291460
  2.9 1.6 %copy-start.2 = (bf16[512,2048]{1,0:T(8,128)(2,1)S(1)}, bf16[512,2048]{1,0:T(8,128)(2,1)}, u32[]{:S(2)}) copy-start(bf16[512,2048]{1,0:T(8,128)(2,1)} %cell_own.1) | copy-start | bytes 6291460
  4.5 0.9 copy-start.10
  5.4 0.7 copy-start.11
  6.1 2.9 %copy-start.1 = (bf16[512,2048]{1,0:T(8,128)(2,1)S(1)}, bf16[512,2048]{1,0:T(8,128)(2,1)}, u32[]{:S(2)}) copy-start(bf16[512,2048]{1,0:T(8,128)(2,1)} %pred_own.1) | copy-start | bytes 6291460
  9.0 6.7 %copy-start.12 = (s32[16]{0:T(128)S(1)}, s32[16]{0:T(128)}, u32[]{:S(2)}) copy-start(s32[16]{0:T(128)} %cell_map.3) | copy-start | bytes 196
  9.0 6.7 %copy-start.13 = (s32[16]{0:T(128)S(1)}, s32[16]{0:T(128)}, u32[]{:S(2)}) copy-start(s32[16]{0:T(128)} %pred_map.1) | copy-start | bytes 196
  12.1 0.7 copy-start.8
  12.8 12.9 %collective-permute-start.2 = (f32[704,128]{1,0:T(8,128)}, f32[704,128]{1,0:T(8,128)}, u32[]{:S(2)}, u32[]{:S(2)}) collective-permute-start(f32[704,128]{1,0:T(8,128)} %get-tuple-element.24), channel_id=1, source_target_pairs={{0,2},{1,5},{2,0},{3,7},{4,6},{5,1},{6,4},{7,3},{8,10},{9,13},{10,... | collective-permute-start | bytes 1081352 | tf_op jit(solution)/shard_map/ppermute | solution.py:223
  15.7 1.6 %copy-start.3 = (bf16[512,2048]{1,0:T(8,128)(2,1)S(1)}, bf16[512,2048]{1,0:T(8,128)(2,1)}, u32[]{:S(2)}) copy-start(bf16[512,2048]{1,0:T(8,128)(2,1)} %cell_own.1) | copy-start | bytes 6291460
  17.3 8.4 %copy-start.9 = (f32[704,128]{1,0:T(8,128)S(1)}, f32[704,128]{1,0:T(8,128)}, u32[]{:S(2)}) copy-start(f32[704,128]{1,0:T(8,128)} %copy-done.8) | copy-start | bytes 1081348
  23.0 1.4 %copy-start.4 = (bf16[1024,1024]{1,0:T(8,128)(2,1)}, bf16[1024,1024]{1,0:T(8,128)(2,1)S(1)}, u32[]{:S(2)}) copy-start(bf16[1024,1024]{1,0:T(8,128)(2,1)S(1)} %get-tuple-element.42.pred) | copy-start | bytes 6291460
  24.4 1.3 %copy-start.6 = (bf16[1024,1024]{1,0:T(8,128)(2,1)}, bf16[1024,1024]{1,0:T(8,128)(2,1)S(1)}, u32[]{:S(2)}) copy-start(bf16[1024,1024]{1,0:T(8,128)(2,1)S(1)} %get-tuple-element.43.cell) | copy-start | bytes 6291460
  26.7 11.8 %collective-permute-start.3 = (f32[1152,128]{1,0:T(8,128)}, f32[1152,128]{1,0:T(8,128)S(1)}, u32[]{:S(2)}, u32[]{:S(2)}) collective-permute-start(f32[1152,128]{1,0:T(8,128)} %get-tuple-element.30), channel_id=1, source_target_pairs={{0,2},{1,5},{2,0},{3,7},{4,6},{5,1},{6,4},{7,3},{8,10},{9,13},{10,... | collective-permute-start | bytes 1769480 | tf_op jit(solution)/shard_map/ppermute | solution.py:223
  26.7 7.5 %collective-permute-start.4 = (f32[352,128]{1,0:T(8,128)S(1)}, f32[352,128]{1,0:T(8,128)S(1)}, u32[]{:S(2)}, u32[]{:S(2)}) collective-permute-start(f32[352,128]{1,0:T(8,128)S(1)} %dynamic-slice_add_fusion.1), channel_id=1, source_target_pairs={{0,4},{1,3},{2,6},{3,1},{4,0},{5,7},{6,2},{7,5},{8,12},{9,11},{10,... | collective-permute-start | bytes 540680 | tf_op jit(solution)/shard_map/ppermute | solution.py:223
  35.3 10.2 %collective-permute-start.6 = (f32[352,128]{1,0:T(8,128)S(1)}, f32[352,128]{1,0:T(8,128)S(1)}, u32[]{:S(2)}, u32[]{:S(2)}) collective-permute-start(f32[352,128]{1,0:T(8,128)S(1)} %add_add_fusion.1), channel_id=1, source_target_pairs={{0,8},{1,9},{2,10},{3,11},{4,12},{5,13},{6,14},{7,15},{8,0},{9,1},... | collective-permute-start | bytes 540680 | tf_op jit(solution)/shard_map/ppermute | solution.py:223
  45.5 5.6 %collective-permute-start.8 = (f32[352,128]{1,0:T(8,128)S(1)}, f32[352,128]{1,0:T(8,128)S(1)}, u32[]{:S(2)}, u32[]{:S(2)}) collective-permute-start(f32[352,128]{1,0:T(8,128)S(1)} %add.50), channel_id=1, source_target_pairs={{0,4},{1,3},{2,6},{3,1},{4,0},{5,7},{6,2},{7,5},{8,12},{9,11},{10,... | collective-permute-start | bytes 540680 | tf_op jit(solution)/shard_map/ppermute | solution.py:223
  45.6 14.9 %collective-permute-start.5 = (f32[576,128]{1,0:T(8,128)S(1)}, f32[576,128]{1,0:T(8,128)S(1)}, u32[]{:S(2)}, u32[]{:S(2)}) collective-permute-start(f32[576,128]{1,0:T(8,128)S(1)} %dynamic-slice_add_fusion), channel_id=1, source_target_pairs={{0,4},{1,3},{2,6},{3,1},{4,0},{5,7},{6,2},{7,5},{8,12},{9,11},{10,... | collective-permute-start | bytes 884744 | tf_op jit(solution)/shard_map/ppermute | solution.py:223
  51.1 9.5 %collective-permute-start.9 = (f32[704,128]{1,0:T(8,128)S(1)}, f32[704,128]{1,0:T(8,128)S(1)}, u32[]{:S(2)}, u32[]{:S(2)}) collective-permute-start(f32[704,128]{1,0:T(8,128)S(1)} %pad_maximum_fusion.1.a0), channel_id=1, source_target_pairs={{0,2},{1,5},{2,0},{3,7},{4,6},{5,1},{6,4},{7,3},{8,10},{9,13},{10,... | collective-permute-start | bytes 1081352 | tf_op jit(solution)/shard_map/ppermute | solution.py:223
  52.8 17.6 %collective-permute-start.10 = (f32[704,128]{1,0:T(8,128)S(1)}, f32[704,128]{1,0:T(8,128)S(1)}, u32[]{:S(2)}, u32[]{:S(2)}) collective-permute-start(f32[704,128]{1,0:T(8,128)S(1)} %pad_maximum_fusion.1.a0), channel_id=1, source_target_pairs={{0,16},{16,0},{1,17},{17,1},{2,18},{18,2},{3,19},{19,3},{4,20},{20... | collective-permute-start | bytes 1081352 | tf_op jit(solution)/shard_map/ppermute | solution.py:231
  60.6 9.8 %collective-permute-start.7 = (f32[576,128]{1,0:T(8,128)S(1)}, f32[576,128]{1,0:T(8,128)S(1)}, u32[]{:S(2)}, u32[]{:S(2)}) collective-permute-start(f32[576,128]{1,0:T(8,128)S(1)} %add_add_fusion), channel_id=1, source_target_pairs={{0,8},{1,9},{2,10},{3,11},{4,12},{5,13},{6,14},{7,15},{8,0},{9,1},... | collective-permute-start | bytes 884744 | tf_op jit(solution)/shard_map/ppermute | solution.py:223
  60.7 18.6 %collective-permute-start.12 = (f32[704,128]{1,0:T(8,128)S(1)}, f32[704,128]{1,0:T(8,128)S(1)}, u32[]{:S(2)}, u32[]{:S(2)}) collective-permute-start(f32[704,128]{1,0:T(8,128)S(1)} %collective-permute-done.9.a1), channel_id=1, source_target_pairs={{0,16},{16,0},{1,17},{17,1},{2,18},{18,2},{3,19},{19,3},{4,20},{20... | collective-permute-start | bytes 1081352 | tf_op jit(solution)/shard_map/ppermute | solution.py:231
  70.4 22.2 %copy-start.7 = (bf16[1024,1024]{1,0:T(8,128)(2,1)S(1)}, bf16[1024,1024]{1,0:T(8,128)(2,1)}, u32[]{:S(2)}) copy-start(bf16[1024,1024]{1,0:T(8,128)(2,1)} %copy-done.6) | copy-start | bytes 6291460
  70.4 22.1 %copy-start.5 = (bf16[1024,1024]{1,0:T(8,128)(2,1)S(1)}, bf16[1024,1024]{1,0:T(8,128)(2,1)}, u32[]{:S(2)}) copy-start(bf16[1024,1024]{1,0:T(8,128)(2,1)} %copy-done.4) | copy-start | bytes 6291460
  70.4 8.8 %collective-permute-start.11 = (f32[576,128]{1,0:T(8,128)S(1)}, f32[576,128]{1,0:T(8,128)S(1)}, u32[]{:S(2)}, u32[]{:S(2)}) collective-permute-start(f32[576,128]{1,0:T(8,128)S(1)} %add.51), channel_id=1, source_target_pairs={{0,4},{1,3},{2,6},{3,1},{4,0},{5,7},{6,2},{7,5},{8,12},{9,11},{10,... | collective-permute-start | bytes 884744 | tf_op jit(solution)/shard_map/ppermute | solution.py:223
  79.3 11.2 %collective-permute-start.13 = (f32[1152,128]{1,0:T(8,128)S(1)}, f32[1152,128]{1,0:T(8,128)S(1)}, u32[]{:S(2)}, u32[]{:S(2)}) collective-permute-start(f32[1152,128]{1,0:T(8,128)S(1)} %pad_maximum_fusion.b0), channel_id=1, source_target_pairs={{0,2},{1,5},{2,0},{3,7},{4,6},{5,1},{6,4},{7,3},{8,10},{9,13},{10,... | collective-permute-start | bytes 1769480 | tf_op jit(solution)/shard_map/ppermute | solution.py:223
  80.9 1.7 %collective-permute-start.14 = (f32[704,128]{1,0:T(8,128)S(1)}, f32[704,128]{1,0:T(8,128)S(1)}, u32[]{:S(2)}, u32[]{:S(2)}) collective-permute-start(f32[704,128]{1,0:T(8,128)S(1)} %pad_maximum_fusion.1.a0), channel_id=1, source_target_pairs={{0,1},{1,0},{2,3},{3,2},{4,5},{5,4},{6,7},{7,6},{8,9},{9,8},{10,11... | collective-permute-start | bytes 1081352 | tf_op jit(solution)/shard_map/ppermute | solution.py:227
  80.9 2.2 %collective-permute-start.15 = (f32[704,128]{1,0:T(8,128)S(1)}, f32[704,128]{1,0:T(8,128)S(1)}, u32[]{:S(2)}, u32[]{:S(2)}) collective-permute-start(f32[704,128]{1,0:T(8,128)S(1)} %collective-permute-done.9.a1), channel_id=1, source_target_pairs={{0,1},{1,0},{2,3},{3,2},{4,5},{5,4},{6,7},{7,6},{8,9},{9,8},{10,11... | collective-permute-start | bytes 1081352 | tf_op jit(solution)/shard_map/ppermute | solution.py:227
  81.4 2.2 %collective-permute-start.16 = (f32[704,128]{1,0:T(8,128)S(1)}, f32[704,128]{1,0:T(8,128)S(1)}, u32[]{:S(2)}, u32[]{:S(2)}) collective-permute-start(f32[704,128]{1,0:T(8,128)S(1)} %collective-permute-done.10.y0), channel_id=1, source_target_pairs={{0,1},{1,0},{2,3},{3,2},{4,5},{5,4},{6,7},{7,6},{8,9},{9,8},{10,11... | collective-permute-start | bytes 1081352 | tf_op jit(solution)/shard_map/ppermute | solution.py:227
  81.4 2.7 %collective-permute-start.17 = (f32[704,128]{1,0:T(8,128)S(1)}, f32[704,128]{1,0:T(8,128)S(1)}, u32[]{:S(2)}, u32[]{:S(2)}) collective-permute-start(f32[704,128]{1,0:T(8,128)S(1)} %collective-permute-done.12.y1), channel_id=1, source_target_pairs={{0,1},{1,0},{2,3},{3,2},{4,5},{5,4},{6,7},{7,6},{8,9},{9,8},{10,11... | collective-permute-start | bytes 1081352 | tf_op jit(solution)/shard_map/ppermute | solution.py:227
  82.6 8.1 %collective-permute-start.18 = (f32[1152,128]{1,0:T(8,128)S(1)}, f32[1152,128]{1,0:T(8,128)S(1)}, u32[]{:S(2)}, u32[]{:S(2)}) collective-permute-start(f32[1152,128]{1,0:T(8,128)S(1)} %pad_maximum_fusion.b0), channel_id=1, source_target_pairs={{0,1},{1,0},{2,3},{3,2},{4,5},{5,4},{6,7},{7,6},{8,9},{9,8},{10,11... | collective-permute-start | bytes 1769480 | tf_op jit(solution)/shard_map/ppermute | solution.py:227
  90.5 2.1 %collective-permute-start.19 = (f32[1152,128]{1,0:T(8,128)S(1)}, f32[1152,128]{1,0:T(8,128)S(1)}, u32[]{:S(2)}, u32[]{:S(2)}) collective-permute-start(f32[1152,128]{1,0:T(8,128)S(1)} %collective-permute-done.13.b1), channel_id=1, source_target_pairs={{0,1},{1,0},{2,3},{3,2},{4,5},{5,4},{6,7},{7,6},{8,9},{9,8},{10,11... | collective-permute-start | bytes 1769480 | tf_op jit(solution)/shard_map/ppermute | solution.py:227

commit v7 on v6

--- a/solution.py
+++ b/solution.py
@@ -49,6 +49,10 @@
     return pl.BlockSpec(memory_space=pltpu.SMEM)
 
 
+def hbm_spec():
+    return pl.BlockSpec(memory_space=pltpu.HBM)
+
+
 def vmem_spec():
     return pl.BlockSpec(memory_space=pltpu.VMEM)
 
@@ -61,146 +65,154 @@
     return jnp.where(day == 0, (cell >> orders[0][0]) & 1, (cell >> orders[1][0]) & 1)
 
 
-def own_gram_kernel(place, cell_map, pred, cell, start, first, second, panel):
+def own_part_kernel(place, cell_map, pred_own, cell_own, start, out, pred, cell, panel, sems, tile_sems):
     group = place[1]
     number = cell_map.shape[0]
     height = panel.shape[0]
+    loads = [pltpu.make_async_copy(pred_own, pred, sems.at[0]), pltpu.make_async_copy(cell_own, cell, sems.at[1])]
     for t in range(number):
         slot = pl.multiple_of(lax.rem(cell_map[t], number) * LANES, LANES)
-        panel[:, t * LANES : (t + 1) * LANES] = start[:, pl.ds(slot, LANES)]
+        loads.append(
+            pltpu.make_async_copy(
+                start.at[:, pl.ds(slot, LANES)], panel.at[:, pl.ds(t * LANES, LANES)], tile_sems.at[t]
+            )
+        )
+    for copy in loads:
+        copy.start()
     count = cell.shape[0] // UNIT
+    loads[0].wait()
+    row = count * height
+    for (i0, j0), (i1, j1) in zip(shares(count)[0][0], shares(count)[1][0]):
+        left = rows_at(pred, i0 + group * (i1 - i0))
+        right = rows_at(pred, j0 + group * (j1 - j0))
+        out[row : row + UNIT, :] = lax.dot_general(left, right, NT, preferred_element_type=F32)
+        row += UNIT
+    for copy in loads[1:]:
+        copy.wait()
     row = 0
     scores = lax.dot_general(panel[...], cell[...], NT, preferred_element_type=F32)
     for c in range(count):
-        first[row : row + height, :] = scores[:, c * LANES : (c + 1) * LANES]
+        out[row : row + height, :] = scores[:, c * LANES : (c + 1) * LANES]
         row += height
-    for (i0, j0), (i1, j1) in zip(shares(count)[0][0], shares(count)[1][0]):
-        left = rows_at(pred, i0 + group * (i1 - i0))
-        right = rows_at(pred, j0 + group * (j1 - j0))
-        first[row : row + UNIT, :] = lax.dot_general(left, right, NT, preferred_element_type=F32)
-        row += UNIT
+
+
+def rows_at(whole, block):
+    return whole[pl.ds(pl.multiple_of(block * UNIT, UNIT), UNIT), :]
+
+
+def own_part(place, cell_map, pred_own, cell_own, start):
+    rows, width = pred_own.shape
+    height = start.shape[0]
+    count = rows // UNIT
+    size = len(own_blocks(count)) // 2 * UNIT + count * height
+    return pl.pallas_call(
+        own_part_kernel,
+        out_shape=jax.ShapeDtypeStruct((size, LANES), F32),
+        in_specs=[smem_spec()] * 2 + [hbm_spec()] * 3,
+        out_specs=vmem_spec(),
+        scratch_shapes=[
+            pltpu.VMEM((rows, width), BF16),
+            pltpu.VMEM((rows, width), BF16),
+            pltpu.VMEM((height, width), BF16),
+            pltpu.SemaphoreType.DMA((2,)),
+            pltpu.SemaphoreType.DMA((cell_map.shape[0],)),
+        ],
+        compiler_params=params(57),
+        name="own_part",
+    )(place, cell_map, pred_own, cell_own, start)
+
+
+def give(orders, place, scr, home, away):
+    bit = first_bit(orders, place[0], place[2])
+    rows = home.shape[0]
+    away[...] = scr[pl.ds(pl.multiple_of((1 - bit) * rows, SUB), rows), :]
+    home[...] = scr[pl.ds(pl.multiple_of(bit * rows, SUB), rows), :]
+
+
+def cross_blocks(place, own, recv, scr, row, at_left, at_right):
+    def run(left, right):
+        to = row
+        value = lax.dot_general(left[at_left, :], right[at_right, :], NT, preferred_element_type=F32)
+        for i in range(value.shape[0] // UNIT):
+            for j in range(value.shape[1] // UNIT):
+                scr[to : to + UNIT, :] = value[i * UNIT : (i + 1) * UNIT, j * UNIT : (j + 1) * UNIT]
+                to += UNIT
+        if to < scr.shape[0]:
+            scr[to:, :] = jnp.zeros((scr.shape[0] - to, LANES), F32)
+
+    @pl.when(place[0] == 0)
+    def _():
+        run(own, recv)
+
+    @pl.when(place[0] == 1)
+    def _():
+        run(recv, own)
+
+
+def first_cross_kernel(orders, place, own, recv, part, home, away, scr):
+    side = own.shape[0] // 2
+    row = part.shape[0]
+    scr[:row, :] = part[...]
+    at_left = pl.ds(pl.multiple_of(place[1] * side, side), side)
+    at_right = pl.ds(pl.multiple_of(place[0] * side, side), side)
+    cross_blocks(place, own, recv, scr, row, at_left, at_right)
+    give(orders, place, scr, home, away)
+
+
+def second_cross_kernel(orders, place, own, recv, home, away, scr):
+    count = own.shape[0] // UNIT
     row = 0
     for i in range(0, count, 2):
-        right = cell[i * UNIT :, :]
+        right = own[i * UNIT :, :]
         value = lax.dot_general(right[: 2 * UNIT, :], right, NT, preferred_element_type=F32)
         for r in range(2):
             for c in range(r, count - i):
-                second[row : row + UNIT, :] = value[r * UNIT : (r + 1) * UNIT, c * UNIT : (c + 1) * UNIT]
+                scr[row : row + UNIT, :] = value[r * UNIT : (r + 1) * UNIT, c * UNIT : (c + 1) * UNIT]
                 row += UNIT
-
-
-def rows_at(whole, block):
-    return whole[pl.ds(pl.multiple_of(block * UNIT, UNIT), UNIT), :]
-
-
-def own_gram(place, cell_map, pred_own, cell_own, start):
-    rows, width = pred_own.shape
-    height = start.shape[0]
-    count = rows // UNIT
-    number = len(own_blocks(count))
-    first = number // 2 * UNIT + count * height
-    second = number * UNIT
+    side = own.shape[0] // 2
+    at_right = pl.ds(pl.multiple_of(place[0] * side, side), side)
+    cross_blocks(place, own, recv, scr, row, pl.ds(0, own.shape[0]), at_right)
+    give(orders, place, scr, home, away)
+
+
+def cross(kernel, orders, total, name, place, own, recv, *part):
+    out = jax.ShapeDtypeStruct((total // 2, LANES), F32)
     return pl.pallas_call(
-        own_gram_kernel,
-        out_shape=(jax.ShapeDtypeStruct((first, LANES), F32), jax.ShapeDtypeStruct((second, LANES), F32)),
-        in_specs=[smem_spec()] * 2 + [vmem_spec()] * 3,
-        out_specs=(vmem_spec(), vmem_spec()),
-        scratch_shapes=[pltpu.VMEM((height, width), BF16)],
-        compiler_params=params(16),
-        name="own_gram",
-    )(place, cell_map, pred_own, cell_own, start)
-
-
-def own_tiles(tile_map, own, recv, whole, day):
-    number = tile_map.shape[0]
+        functools.partial(kernel, orders),
+        out_shape=(out, out),
+        in_specs=[smem_spec()] + [vmem_spec()] * (2 + len(part)),
+        out_specs=(vmem_spec(),) * 2,
+        scratch_shapes=[pltpu.VMEM((total, LANES), F32)],
+        compiler_params=params(12),
+        name=name,
+    )(place, own, recv, *part)
+
+
+def tiles_kernel(place, pred_map, cell_map, pred, pred_recv, cell, cell_recv, *outs):
+    number = pred_map.shape[0]
     half = number // 2
-    rows = own.shape[0]
-    mine = pl.ds(pl.multiple_of(day * rows, rows), rows)
-    theirs = pl.ds(pl.multiple_of((1 - day) * rows, rows), rows)
-    for t in range(number):
-        slot = lax.rem(tile_map[t], number)
-        to = pl.ds(pl.multiple_of(lax.rem(slot, half) * LANES, LANES), LANES)
-
-        @pl.when(lax.div(slot, half) == day)
-        def _():
-            whole[mine, to] = own[:, t * LANES : (t + 1) * LANES]
-            whole[theirs, to] = recv[:, t * LANES : (t + 1) * LANES]
-
-
-def cross_blocks(orders, shared, place, own, recv, part, home, away, left, right, scr):
-    day, group, index = place[0], place[1], place[2]
-    height, side = left.shape[0], right.shape[0]
-    at_left = pl.ds(pl.multiple_of(group * height, height), height) if shared else pl.ds(0, height)
-    at_right = pl.ds(pl.multiple_of(day * side, side), side)
-
-    @pl.when(day == 0)
-    def _():
-        left[...] = own[at_left, :]
-        right[...] = recv[at_right, :]
-
-    @pl.when(day == 1)
-    def _():
-        left[...] = recv[at_left, :]
-        right[...] = own[at_right, :]
-
-    row = part.shape[0]
-    scr[:row, :] = part[...]
-    value = lax.dot_general(left[...], right[...], NT, preferred_element_type=F32)
-    for i in range(height // UNIT):
-        for j in range(side // UNIT):
-            scr[row : row + UNIT, :] = value[i * UNIT : (i + 1) * UNIT, j * UNIT : (j + 1) * UNIT]
-            row += UNIT
-    if row < scr.shape[0]:
-        scr[row:, :] = jnp.zeros((scr.shape[0] - row, LANES), F32)
-    bit = first_bit(orders, day, index)
-    rows = home.shape[0]
-    home[...] = scr[pl.ds(pl.multiple_of(bit * rows, SUB), rows), :]
-    away[...] = scr[pl.ds(pl.multiple_of((1 - bit) * rows, SUB), rows), :]
-
-
-def first_cross_kernel(orders, place, own, recv, part, home, away, left, right, scr):
-    cross_blocks(orders, True, place, own, recv, part, home, away, left, right, scr)
-
-
-def second_cross_kernel(orders, place, pred_map, cell_map, pred_own, pred_recv, cell_own, cell_recv, part,
-                        home, away, pred_tiles, cell_tiles, left, right, scr):
-    cross_blocks(orders, False, place, cell_own, cell_recv, part, home, away, left, right, scr)
-    own_tiles(pred_map, pred_own, pred_recv, pred_tiles, place[0])
-    own_tiles(cell_map, cell_own, cell_recv, cell_tiles, place[0])
-
-
-def first_cross(orders, total, place, own, recv, part):
-    rows, width = own.shape
-    out = jax.ShapeDtypeStruct((total // 2, LANES), F32)
-    side = pltpu.VMEM((rows // 2, width), BF16)
+    sources = ((pred_map, pred), (pred_map, pred_recv), (cell_map, cell), (cell_map, cell_recv))
+    for (tile_map, stored), out in zip(sources, outs):
+        for t in range(number):
+            slot = lax.rem(tile_map[t], number)
+            to = pl.ds(pl.multiple_of(lax.rem(slot, half) * LANES, LANES), LANES)
+
+            @pl.when(lax.div(slot, half) == place[0])
+            def _():
+                out[:, to] = stored[:, t * LANES : (t + 1) * LANES]
+
+
+def own_tiles(place, pred_map, cell_map, *fields):
+    rows, width = fields[0].shape
+    half = jax.ShapeDtypeStruct((rows, width // 2), BF16)
     return pl.pallas_call(
-        functools.partial(first_cross_kernel, orders),
-        out_shape=(out, out),
-        in_specs=[smem_spec()] + [vmem_spec()] * 3,
-        out_specs=(vmem_spec(),) * 2,
-        scratch_shapes=[side, side, pltpu.VMEM((total, LANES), F32)],
-        compiler_params=params(12),
-        name="first_cross",
-    )(place, own, recv, part)
-
-
-def second_cross(orders, total, place, pred_map, cell_map, pred_own, pred_recv, cell_own, cell_recv, part):
-    rows, width = cell_own.shape
-    out = jax.ShapeDtypeStruct((total // 2, LANES), F32)
-    tiles = jax.ShapeDtypeStruct((2 * rows, width // 2), BF16)
-    return pl.pallas_call(
-        functools.partial(second_cross_kernel, orders),
-        out_shape=(out, out, tiles, tiles),
-        in_specs=[smem_spec()] * 3 + [vmem_spec()] * 5,
+        tiles_kernel,
+        out_shape=(half,) * 4,
+        in_specs=[smem_spec()] * 3 + [vmem_spec()] * 4,
         out_specs=(vmem_spec(),) * 4,
-        scratch_shapes=[
-            pltpu.VMEM((rows, width), BF16),
-            pltpu.VMEM((rows // 2, width), BF16),
-            pltpu.VMEM((total, LANES), F32),
-        ],
-        compiler_params=params(12),
-        name="second_cross",
-    )(place, pred_map, cell_map, pred_own, pred_recv, cell_own, cell_recv, part)
+        compiler_params=params(8),
+        name="own_tiles",
+    )(place, pred_map, cell_map, *fields)
 
 
 def after(value, gate):
@@ -261,8 +273,9 @@
     for stage in range(2, last):
         late_home, late_away = halve(orders, stage, late_home, late)
         late = cell_exchange(late_away, orders, stage, cells)
-    part = part + after(middle, late_away)
-    late_part = after(late_home + late, part)
+    late_part = late_home + late
+    part = part + after(middle, late_part)
+    late_part = after(late_part, part)
     for stage in reversed(range(1, last)):
         part = jnp.concatenate([part, cell_exchange(part, orders, stage, cells)], axis=0)
     late_middle = cell_exchange(late_part, orders, last, cells)
@@ -422,11 +435,12 @@
 
 
 def second_chain_kernel(bits, orders, counts, place, b0, b1, b0_twin, b1_twin, pred_gram,
-                        scores_in, loadings_in, pred, cell, pred_out, cell_out, beta, cell_gram):
+                        scores_in, loadings_in, pred, pred_recv, cell, cell_recv, pred_out, cell_out,
+                        beta, cell_gram):
     day, index = place[0], place[2]
     place_sums((b0, b1), beta, day, bits, orders, index)
     place_sums((b0_twin, b1_twin), beta, 1 - day, bits, orders, index)
-    days = pred.shape[0]
+    days = pred_gram.shape[1]
     count = days // UNIT // 2
     own = own_blocks(count)
     cross = [(i, j) for i in range(count) for j in range(count // 2)]
@@ -441,19 +455,26 @@
         cell_inverse, cell_value = half_step(loadings, cell_gram, counts[1])
         if iteration < ITERS - 1:
             pred_scores = next_scores(cell_inverse, cell_value)
-    raw = jnp.dot(pred_scores, pred[...], preferred_element_type=F32)
-    pred_out[...] = exact_dot(pred_inverse, raw)
-    raw = jnp.dot(loadings, cell[...], preferred_element_type=F32)
-    cell_out[...] = exact_dot(cell_inverse, raw)
-
-
-def second_chain(bits, orders, counts, place, sums, gram, scores, loadings, pred, cell):
+    pred_out[...] = exact_dot(pred_inverse, panel(pred_scores, pred, pred_recv, day))
+    cell_out[...] = exact_dot(cell_inverse, panel(loadings, cell, cell_recv, day))
+
+
+def panel(scores, own, recv, day):
+    half = own.shape[0]
+    first, second = scores[:, :half].astype(F32), scores[:, half:].astype(F32)
+    mine = jnp.where(day == 0, first, second).astype(BF16)
+    theirs = jnp.where(day == 0, second, first).astype(BF16)
+    value = jnp.dot(mine, own[...], preferred_element_type=F32)
+    return value + jnp.dot(theirs, recv[...], preferred_element_type=F32)
+
+
+def second_chain(bits, orders, counts, place, sums, gram, scores, loadings, tiles):
     height, days = scores.shape
-    out = jax.ShapeDtypeStruct((height, pred.shape[1]), F32)
+    out = jax.ShapeDtypeStruct((height, tiles[0].shape[1]), F32)
     return pl.pallas_call(
         functools.partial(second_chain_kernel, bits, orders, counts),
         out_shape=(out, out),
-        in_specs=[smem_spec()] + [vmem_spec()] * 9,
+        in_specs=[smem_spec()] + [vmem_spec()] * 11,
         out_specs=(vmem_spec(), vmem_spec()),
         scratch_shapes=[
             pltpu.VMEM((2, 2 * sums[0].shape[0], LANES), F32),
@@ -461,7 +482,7 @@
         ],
         compiler_params=params(24),
         name="second_chain",
-    )(place, *sums, gram, scores, loadings, pred, cell)
+    )(place, *sums, gram, scores, loadings, *tiles)
 
 
 def local(predictors, predictand, pred_map, cell_map, start_panel):
@@ -477,21 +498,26 @@
     pred_recv = other_core(predictors)
     cell_recv = other_core(predictand)
     count = predictors.shape[0] // UNIT
-    first_part, second_part = own_gram(place, cell_map, predictors, predictand, start_panel)
-    first = first_cross(orders, first_rows(count, height, bits), place, predictors, pred_recv, first_part)
-    home, away, pred, cell = second_cross(
-        orders, second_rows(count, bits), place, pred_map, cell_map,
-        predictors, pred_recv, predictand, after(cell_recv, first[1]), second_part,
+    part = own_part(place, cell_map, predictors, predictand, start_panel)
+    first = cross(
+        first_cross_kernel, orders, first_rows(count, height, bits), "first_cross", place, predictors, pred_recv, part
     )
-    second = (home, away)
+    second = cross(
+        second_cross_kernel, orders, second_rows(count, bits), "second_cross",
+        place, predictand, after(cell_recv, first[1]),
+    )
+
     mine, other, late = sum_chunks(orders, bits, cells, first, second)
+    pred_again = other_core(after(predictors, mine[0]))
+    cell_again = other_core(after(predictand, mine[0]))
+    tiles = own_tiles(place, pred_map, cell_map, predictors, pred_again, predictand, cell_again)
     sums = mine + other
     gram, scores, loadings = first_chain(
         bits, orders, counts, days, height, place, sums + tuple(other_core(part) for part in sums)
     )
     late = (late[0], after(late[1], loadings))
     late = late + tuple(other_core(part) for part in late)
-    return second_chain(bits, orders, counts, place, late, gram, scores, loadings, pred, cell)
+    return second_chain(bits, orders, counts, place, late, gram, scores, loadings, tiles)
 
 
 def solution(mesh):

time: 115 us -> 111 us (0.965)
  local copies, waits for them, and re-layouts: 9.82 us -> 1.18 us
  Pallas kernels: 39.6 us -> 42.4 us
  other arithmetic: 2.25 us -> 4.67 us
    unnamed x28 -> x14, local copies, waits for them, and re-layouts: 9.82 us -> 1.18 us
    pallas_call x3 -> x4, Pallas kernels: 11.6 us -> 14.5 us  [the longest x2 6.4 us: cross(): pl.pallas_call(functools.partial(kernel, orders), out_shape=(out, out), i...]
    ppermute x8 -> x10, waiting for transfers between devices: 3.93 us -> 1.93 us  [other_core(): return lax.ppermute(value, 'day', [(0, 1), (1, 0)])]
    ppermute x10, waiting for transfers between devices: 39.3 us -> 40.9 us  [cell_exchange(): return lax.ppermute(value, ('cell', 'day'), pairs)]
  transfers between devices with their start and end apart: 20 -> 22, of which waited for: 11 -> 12; matrix products, arithmetic and copies ran while one was open for 1% -> 2% of each run, Pallas kernels for 16% -> 19%
where the time goes in v7:
time: 111 us
  waiting for transfers between devices  42.8 us (39%)
  Pallas kernels  42.4 us (38%)
  starting transfers between devices  18.8 us (17%)
  other arithmetic  4.67 us (4%)
  local copies, waits for them, and re-layouts  1.18 us (1%)
    ppermute x10, waiting for transfers between devices, cell_exchange(): return lax.ppermute(value, ('cell', 'day'), pairs)  40.9 us
    pallas_call x1, Pallas kernels, second_chain(): pl.pallas_call(functools.partial(second_chain_kernel, bits, orders, count...  21.7 us
    ppermute x10, starting transfers between devices, cell_exchange(): return lax.ppermute(value, ('cell', 'day'), pairs)  14.1 us
    pallas_call x2, Pallas kernels, cross(): pl.pallas_call(functools.partial(kernel, orders), out_shape=(out, out), i...  6.4 us
    pallas_call x1, Pallas kernels, first_chain(): pl.pallas_call(functools.partial(first_chain_kernel, bits, orders, counts...  6.2 us
    pallas_call x1, Pallas kernels, own_part(): pl.pallas_call(own_part_kernel, out_shape=jax.ShapeDtypeStruct((size, LAN...  5.56 us
    ppermute x2, starting transfers between devices, other_group(): return lax.ppermute(value, 'group', [(0, 1), (1, 0)])  3.17 us
    pallas_call x1, Pallas kernels, own_tiles(): pl.pallas_call(tiles_kernel, out_shape=(half,) * 4, in_specs=[smem_spec()...  2.58 us
  transfers between devices with their start and end apart: 22, of which 12 were waited for; matrix products, arithmetic and copies ran while one was open for 2% of the time, Pallas kernels for 19%

profile of v7, /device:TPU:0, one launch (start us, length us, event | category | flops | bytes accessed | tf_op | source)
XLA Modules:
  0.0 110.7 jit_solution(13168387405741187117)
XLA Ops:
  0.6 0.5 collective-permute-start.1
  1.1 0.1 collective-permute-start
  1.2 0.6 pad_add_fusion.place
  1.9 5.6 %own_part.1.part = f32[896,128]{1,0:T(8,128)} custom-call(s32[3]{0:T(128)} %pad_add_fusion.place, s32[16]{0:T(128)} %cell_map.3, bf16[512,2048]{1,0:T(8,128)(2,1)} %pred_.1, bf16[512,2048]{1,0:T(8,128)(2,1)} %cell.1, bf16[64,2048]{1,0:T(8,128)(2,1)} %start.1), custom_call_target="tpu_custom_call" | custom-call | tf_op jit(solution)/shard_map/own_part/pallas_call | solution.py:108
  7.4 0.0 copy-start
  7.4 0.0 collective-permute-done.1.recv
  7.5 0.0 copy-done.1
  7.5 0.0 copy-done.4
  7.5 0.0 copy-start.3
  7.5 1.2 %copy-done.3 = f32[896,128]{1,0:T(8,128)S(1)} copy-done((f32[896,128]{1,0:T(8,128)S(1)}, f32[896,128]{1,0:T(8,128)}, u32[]{:S(2)}) %copy-start.3) | copy-done | bytes 458776
  8.6 2.2 %first_cross.1 = (f32[704,128]{1,0:T(8,128)S(1)}, f32[704,128]{1,0:T(8,128)S(1)}) custom-call(s32[3]{0:T(128)S(1)} %copy-done.4, bf16[512,2048]{1,0:T(8,128)(2,1)S(1)} %copy-done.1, bf16[512,2048]{1,0:T(8,128)(2,1)} %collective-permute-done.1.recv, f32[896,128]{1,0:T(8,128)S(1)} %copy-done.3), custom_call_target="tpu_custom_call" | custom-call | tf_op jit(solution)/shard_map/first_cross/pallas_call | solution.py:180
  10.8 3.0 %collective-permute-start.2 = (f32[704,128]{1,0:T(8,128)S(1)}, f32[704,128]{1,0:T(8,128)}, u32[]{:S(2)}, u32[]{:S(2)}) collective-permute-start(f32[704,128]{1,0:T(8,128)S(1)} %get-tuple-element.25), channel_id=1, source_target_pairs={{0,2},{1,5},{2,0},{3,7},{4,6},{5,1},{6,4},{7,3},{8,10},{9,13},{10,... | collective-permute-start | bytes 1081352 | tf_op jit(solution)/shard_map/ppermute | solution.py:235
  13.8 0.0 collective-permute-done.recv
  13.8 4.2 %second_cross.1 = (f32[1152,128]{1,0:T(8,128)S(1)}, f32[1152,128]{1,0:T(8,128)}) custom-call(s32[3]{0:T(128)S(1)} %copy-done.4, bf16[512,2048]{1,0:T(8,128)(2,1)S(1)} %copy-done, bf16[512,2048]{1,0:T(8,128)(2,1)} %collective-permute-done.recv), custom_call_target="tpu_custom_call" | custom-call | tf_op jit(solution)/shard_map/second_cross/pallas_call | solution.py:180
  18.1 1.3 %collective-permute-done.2 = f32[704,128]{1,0:T(8,128)} collective-permute-done((f32[704,128]{1,0:T(8,128)S(1)}, f32[704,128]{1,0:T(8,128)}, u32[]{:S(2)}, u32[]{:S(2)}) %collective-permute-start.2) | collective-permute-done | bytes 360480 | tf_op jit(solution)/shard_map/ppermute | solution.py:235
  19.3 0.9 dynamic-slice_add_fusion.1
  20.3 2.1 %collective-permute-start.3 = (f32[1152,128]{1,0:T(8,128)}, f32[1152,128]{1,0:T(8,128)}, u32[]{:S(2)}, u32[]{:S(2)}) collective-permute-start(f32[1152,128]{1,0:T(8,128)} %get-tuple-element.30), channel_id=1, source_target_pairs={{0,2},{1,5},{2,0},{3,7},{4,6},{5,1},{6,4},{7,3},{8,10},{9,13},{10,... | collective-permute-start | bytes 1769480 | tf_op jit(solution)/shard_map/ppermute | solution.py:235
  22.4 1.6 %collective-permute-start.4 = (f32[352,128]{1,0:T(8,128)S(1)}, f32[352,128]{1,0:T(8,128)S(1)}, u32[]{:S(2)}, u32[]{:S(2)}) collective-permute-start(f32[352,128]{1,0:T(8,128)S(1)} %dynamic-slice_add_fusion.1), channel_id=1, source_target_pairs={{0,4},{1,3},{2,6},{3,1},{4,0},{5,7},{6,2},{7,5},{8,12},{9,11},{10,... | collective-permute-start | bytes 540680 | tf_op jit(solution)/shard_map/ppermute | solution.py:235
  23.9 5.9 %collective-permute-done.4 = f32[352,128]{1,0:T(8,128)S(1)} collective-permute-done((f32[352,128]{1,0:T(8,128)S(1)}, f32[352,128]{1,0:T(8,128)S(1)}, u32[]{:S(2)}, u32[]{:S(2)}) %collective-permute-start.4) | collective-permute-done | bytes 180256 | tf_op jit(solution)/shard_map/ppermute | solution.py:235
  29.9 1.0 add_add_fusion.1
  30.8 1.5 %collective-permute-done.3 = f32[1152,128]{1,0:T(8,128)} collective-permute-done((f32[1152,128]{1,0:T(8,128)}, f32[1152,128]{1,0:T(8,128)}, u32[]{:S(2)}, u32[]{:S(2)}) %collective-permute-start.3) | collective-permute-done | bytes 589856 | tf_op jit(solution)/shard_map/ppermute | solution.py:235
  32.3 1.0 dynamic-slice_add_fusion
  33.3 0.4 collective-permute-start.5
  33.8 2.7 %collective-permute-start.6 = (f32[352,128]{1,0:T(8,128)S(1)}, f32[352,128]{1,0:T(8,128)S(1)}, u32[]{:S(2)}, u32[]{:S(2)}) collective-permute-start(f32[352,128]{1,0:T(8,128)S(1)} %add_add_fusion.1), channel_id=1, source_target_pairs={{0,8},{1,9},{2,10},{3,11},{4,12},{5,13},{6,14},{7,15},{8,0},{9,1},... | collective-permute-start | bytes 540680 | tf_op jit(solution)/shard_map/ppermute | solution.py:235
  36.4 7.6 %collective-permute-done.5 = f32[576,128]{1,0:T(8,128)S(1)} collective-permute-done((f32[576,128]{1,0:T(8,128)S(1)}, f32[576,128]{1,0:T(8,128)S(1)}, u32[]{:S(2)}, u32[]{:S(2)}) %collective-permute-start.5) | collective-permute-done | bytes 294944 | tf_op jit(solution)/shard_map/ppermute | solution.py:235
  44.0 1.0 add_add_fusion
  45.0 0.0 collective-permute-done.6
  45.0 0.7 collective-permute-start.8
  45.8 4.8 %collective-permute-done.8 = f32[352,128]{1,0:T(8,128)S(1)} collective-permute-done((f32[352,128]{1,0:T(8,128)S(1)}, f32[352,128]{1,0:T(8,128)S(1)}, u32[]{:S(2)}, u32[]{:S(2)}) %collective-permute-start.8) | collective-permute-done | bytes 180256 | tf_op jit(solution)/shard_map/ppermute | solution.py:235
  50.6 0.9 collective-permute-start.9
  51.5 0.0 collective-permute-start.20
  51.5 0.5 collective-permute-start.21
  52.0 1.6 %collective-permute-start.10 = (f32[704,128]{1,0:T(8,128)S(1)}, f32[704,128]{1,0:T(8,128)S(1)}, u32[]{:S(2)}, u32[]{:S(2)}) collective-permute-start(f32[704,128]{1,0:T(8,128)S(1)} %pad_maximum_fusion.1.a0), channel_id=1, source_target_pairs={{0,16},{16,0},{1,17},{17,1},{2,18},{18,2},{3,19},{19,3},{4,20},{20... | collective-permute-start | bytes 1081352 | tf_op jit(solution)/shard_map/ppermute | solution.py:243
  53.6 1.5 %collective-permute-start.7 = (f32[576,128]{1,0:T(8,128)S(1)}, f32[576,128]{1,0:T(8,128)S(1)}, u32[]{:S(2)}, u32[]{:S(2)}) collective-permute-start(f32[576,128]{1,0:T(8,128)S(1)} %add_add_fusion), channel_id=1, source_target_pairs={{0,8},{1,9},{2,10},{3,11},{4,12},{5,13},{6,14},{7,15},{8,0},{9,1},... | collective-permute-start | bytes 884744 | tf_op jit(solution)/shard_map/ppermute | solution.py:235
  55.1 3.0 %collective-permute-done.9.a1 = f32[704,128]{1,0:T(8,128)S(1)} collective-permute-done((f32[704,128]{1,0:T(8,128)S(1)}, f32[704,128]{1,0:T(8,128)S(1)}, u32[]{:S(2)}, u32[]{:S(2)}) %collective-permute-start.9) | collective-permute-done | bytes 360480 | tf_op jit(solution)/shard_map/ppermute | solution.py:235
  58.1 1.5 %collective-permute-start.12 = (f32[704,128]{1,0:T(8,128)S(1)}, f32[704,128]{1,0:T(8,128)S(1)}, u32[]{:S(2)}, u32[]{:S(2)}) collective-permute-start(f32[704,128]{1,0:T(8,128)S(1)} %collective-permute-done.9.a1), channel_id=1, source_target_pairs={{0,16},{16,0},{1,17},{17,1},{2,18},{18,2},{3,19},{19,3},{4,20},{20... | collective-permute-start | bytes 1081352 | tf_op jit(solution)/shard_map/ppermute | solution.py:243
  59.7 9.8 %collective-permute-done.7 = f32[576,128]{1,0:T(8,128)S(1)} collective-permute-done((f32[576,128]{1,0:T(8,128)S(1)}, f32[576,128]{1,0:T(8,128)S(1)}, u32[]{:S(2)}, u32[]{:S(2)}) %collective-permute-start.7) | collective-permute-done | bytes 294944 | tf_op jit(solution)/shard_map/ppermute | solution.py:235
  69.5 0.0 collective-permute-done.10.y0
  69.5 0.0 copy-start.5
  69.5 0.0 copy-start.6
  69.6 0.1 collective-permute-start.11
  69.6 0.1 collective-permute-start.14
  69.7 6.6 %collective-permute-done.11 = f32[576,128]{1,0:T(8,128)S(1)} collective-permute-done((f32[576,128]{1,0:T(8,128)S(1)}, f32[576,128]{1,0:T(8,128)S(1)}, u32[]{:S(2)}, u32[]{:S(2)}) %collective-permute-start.11) | collective-permute-done | bytes 294944 | tf_op jit(solution)/shard_map/ppermute | solution.py:235
  76.3 0.0 collective-permute-start.15
  76.4 0.0 collective-permute-done.12.y1
  76.4 1.2 %collective-permute-start.13 = (f32[1152,128]{1,0:T(8,128)S(1)}, f32[1152,128]{1,0:T(8,128)S(1)}, u32[]{:S(2)}, u32[]{:S(2)}) collective-permute-start(f32[1152,128]{1,0:T(8,128)S(1)} %pad_maximum_fusion.b0), channel_id=1, source_target_pairs={{0,2},{1,5},{2,0},{3,7},{4,6},{5,1},{6,4},{7,3},{8,10},{9,13},{10,... | collective-permute-start | bytes 1769480 | tf_op jit(solution)/shard_map/ppermute | solution.py:235
  77.6 0.0 collective-permute-done.14.a0_twin
  77.6 0.0 collective-permute-start.16
  77.6 0.4 collective-permute-done.15.a1_twin
  78.0 0.1 collective-permute-start.17
  78.2 1.1 %collective-permute-done.16.y0_twin = f32[704,128]{1,0:T(8,128)S(1)} collective-permute-done((f32[704,128]{1,0:T(8,128)S(1)}, f32[704,128]{1,0:T(8,128)S(1)}, u32[]{:S(2)}, u32[]{:S(2)}) %collective-permute-start.16) | collective-permute-done | bytes 360480 | tf_op jit(solution)/shard_map/ppermute | solution.py:239
  79.3 0.1 collective-permute-start.18
  79.4 0.4 collective-permute-done.17.y1_twin
  79.8 6.2 %first_chain.1 = (bf16[3,1024,1024]{2,1,0:T(8,128)(2,1)S(1)}, bf16[64,1024]{1,0:T(8,128)(2,1)S(1)}, bf16[64,1024]{1,0:T(8,128)(2,1)S(1)}) custom-call(s32[3]{0:T(128)S(1)} %copy-done.4, f32[704,128]{1,0:T(8,128)S(1)} %pad_maximum_fusion.1.a0, f32[704,128]{1,0:T(8,128)S(1)} %collective-permute-done.9.a1, f32[704,128]{1,0:T(8,128)S(1)} %collective-permute-done.10.y0, ...), custom_call_target="tpu_custom_call" | custom-call | tf_op jit(solution)/shard_map/first_chain/pallas_call | solution.py:426
  86.0 0.3 collective-permute-done.13.b1
  86.3 0.0 collective-permute-start.19
  86.3 0.0 collective-permute-done.20.pred_recv
  86.4 0.0 collective-permute-done.21.cell_recv
  86.4 0.0 copy-done.5
  86.4 0.0 copy-done.6
  86.4 2.6 %own_tiles.1 = (bf16[512,1024]{1,0:T(8,128)(2,1)S(1)}, bf16[512,1024]{1,0:T(8,128)(2,1)S(1)}, bf16[512,1024]{1,0:T(8,128)(2,1)S(1)}, bf16[512,1024]{1,0:T(8,128)(2,1)S(1)}) custom-call(s32[3]{0:T(128)S(1)} %copy-done.4, s32[16]{0:T(128)S(1)} %copy-done.6, s32[16]{0:T(128)S(1)} %copy-done.5, bf16[512,2048]{1,0:T(8,128)(2,1)S(1)} %copy-done.2, ...), custom_call_target="tpu_custom_call" | custom-call | tf_op jit(solution)/shard_map/own_tiles/pallas_call | solution.py:208
  89.0 0.0 collective-permute-done.18.b0_twin
  89.0 0.0 collective-permute-done.19.b1_twin
  89.0 21.7 %second_chain.1 = (f32[64,1024]{1,0:T(8,128)}, f32[64,1024]{1,0:T(8,128)}) custom-call(s32[3]{0:T(128)S(1)} %copy-done.4, f32[1152,128]{1,0:T(8,128)S(1)} %pad_maximum_fusion.b0, f32[1152,128]{1,0:T(8,128)S(1)} %collective-permute-done.13.b1, f32[1152,128]{1,0:T(8,128)S(1)} %collective-permute-done.18.b0_twin, ...), custom_call_target="tpu_custom_call" | custom-call | tf_op jit(solution)/shard_map/second_chain/pallas_call | solution.py:474
  (9 shorter events, 0.1 us)
Async XLA Ops:
  0.6 6.8 %collective-permute-start.1 = (bf16[512,2048]{1,0:T(8,128)(2,1)}, bf16[512,2048]{1,0:T(8,128)(2,1)}, u32[]{:S(2)}, u32[]{:S(2)}) collective-permute-start(bf16[512,2048]{1,0:T(8,128)(2,1)} %pred_.1), channel_id=1, source_target_pairs={{0,1},{1,0},{2,3},{3,2},{4,5},{5,4},{6,7},{7,6},{8,9},{9,8},{10,11... | collective-permute-start | bytes 6291464 | tf_op jit(solution)/shard_map/ppermute | solution.py:239
  1.1 12.7 %collective-permute-start = (bf16[512,2048]{1,0:T(8,128)(2,1)}, bf16[512,2048]{1,0:T(8,128)(2,1)}, u32[]{:S(2)}, u32[]{:S(2)}) collective-permute-start(bf16[512,2048]{1,0:T(8,128)(2,1)} %cell.1), channel_id=1, source_target_pairs={{0,1},{1,0},{2,3},{3,2},{4,5},{5,4},{6,7},{7,6},{8,9},{9,8},{10,11... | collective-permute-start | bytes 6291464 | tf_op jit(solution)/shard_map/ppermute | solution.py:239
  1.9 5.6 %copy-start.1 = (bf16[512,2048]{1,0:T(8,128)(2,1)S(1)}, bf16[512,2048]{1,0:T(8,128)(2,1)}, u32[]{:S(2)}) copy-start(bf16[512,2048]{1,0:T(8,128)(2,1)} %pred_.1) | copy-start | bytes 6291460
  1.9 5.6 %copy-start.4 = (s32[3]{0:T(128)S(1)}, s32[3]{0:T(128)}, u32[]{:S(2)}) copy-start(s32[3]{0:T(128)} %pad_add_fusion.place) | copy-start | bytes 40
  7.4 6.4 %copy-start = (bf16[512,2048]{1,0:T(8,128)(2,1)S(1)}, bf16[512,2048]{1,0:T(8,128)(2,1)}, u32[]{:S(2)}) copy-start(bf16[512,2048]{1,0:T(8,128)(2,1)} %cell.1) | copy-start | bytes 6291460
  7.5 1.2 %copy-start.3 = (f32[896,128]{1,0:T(8,128)S(1)}, f32[896,128]{1,0:T(8,128)}, u32[]{:S(2)}) copy-start(f32[896,128]{1,0:T(8,128)} %own_part.1.part) | copy-start | bytes 1376260
  10.8 8.5 %collective-permute-start.2 = (f32[704,128]{1,0:T(8,128)S(1)}, f32[704,128]{1,0:T(8,128)}, u32[]{:S(2)}, u32[]{:S(2)}) collective-permute-start(f32[704,128]{1,0:T(8,128)S(1)} %get-tuple-element.25), channel_id=1, source_target_pairs={{0,2},{1,5},{2,0},{3,7},{4,6},{5,1},{6,4},{7,3},{8,10},{9,13},{10,... | collective-permute-start | bytes 1081352 | tf_op jit(solution)/shard_map/ppermute | solution.py:235
  20.3 12.1 %collective-permute-start.3 = (f32[1152,128]{1,0:T(8,128)}, f32[1152,128]{1,0:T(8,128)}, u32[]{:S(2)}, u32[]{:S(2)}) collective-permute-start(f32[1152,128]{1,0:T(8,128)} %get-tuple-element.30), channel_id=1, source_target_pairs={{0,2},{1,5},{2,0},{3,7},{4,6},{5,1},{6,4},{7,3},{8,10},{9,13},{10,... | collective-permute-start | bytes 1769480 | tf_op jit(solution)/shard_map/ppermute | solution.py:235
  22.4 7.5 %collective-permute-start.4 = (f32[352,128]{1,0:T(8,128)S(1)}, f32[352,128]{1,0:T(8,128)S(1)}, u32[]{:S(2)}, u32[]{:S(2)}) collective-permute-start(f32[352,128]{1,0:T(8,128)S(1)} %dynamic-slice_add_fusion.1), channel_id=1, source_target_pairs={{0,4},{1,3},{2,6},{3,1},{4,0},{5,7},{6,2},{7,5},{8,12},{9,11},{10,... | collective-permute-start | bytes 540680 | tf_op jit(solution)/shard_map/ppermute | solution.py:235
  33.3 10.7 %collective-permute-start.5 = (f32[576,128]{1,0:T(8,128)S(1)}, f32[576,128]{1,0:T(8,128)S(1)}, u32[]{:S(2)}, u32[]{:S(2)}) collective-permute-start(f32[576,128]{1,0:T(8,128)S(1)} %dynamic-slice_add_fusion), channel_id=1, source_target_pairs={{0,4},{1,3},{2,6},{3,1},{4,0},{5,7},{6,2},{7,5},{8,12},{9,11},{10,... | collective-permute-start | bytes 884744 | tf_op jit(solution)/shard_map/ppermute | solution.py:235
  33.8 17.7 %copy-start.2 = (bf16[512,2048]{1,0:T(8,128)(2,1)S(1)}, bf16[512,2048]{1,0:T(8,128)(2,1)}, u32[]{:S(2)}) copy-start(bf16[512,2048]{1,0:T(8,128)(2,1)} %pred_.1) | copy-start | bytes 6291460
  33.8 11.3 %collective-permute-start.6 = (f32[352,128]{1,0:T(8,128)S(1)}, f32[352,128]{1,0:T(8,128)S(1)}, u32[]{:S(2)}, u32[]{:S(2)}) collective-permute-start(f32[352,128]{1,0:T(8,128)S(1)} %add_add_fusion.1), channel_id=1, source_target_pairs={{0,8},{1,9},{2,10},{3,11},{4,12},{5,13},{6,14},{7,15},{8,0},{9,1},... | collective-permute-start | bytes 540680 | tf_op jit(solution)/shard_map/ppermute | solution.py:235
  45.0 5.6 %collective-permute-start.8 = (f32[352,128]{1,0:T(8,128)S(1)}, f32[352,128]{1,0:T(8,128)S(1)}, u32[]{:S(2)}, u32[]{:S(2)}) collective-permute-start(f32[352,128]{1,0:T(8,128)S(1)} %add.50), channel_id=1, source_target_pairs={{0,4},{1,3},{2,6},{3,1},{4,0},{5,7},{6,2},{7,5},{8,12},{9,11},{10,... | collective-permute-start | bytes 540680 | tf_op jit(solution)/shard_map/ppermute | solution.py:235
  50.6 7.5 %collective-permute-start.9 = (f32[704,128]{1,0:T(8,128)S(1)}, f32[704,128]{1,0:T(8,128)S(1)}, u32[]{:S(2)}, u32[]{:S(2)}) collective-permute-start(f32[704,128]{1,0:T(8,128)S(1)} %pad_maximum_fusion.1.a0), channel_id=1, source_target_pairs={{0,2},{1,5},{2,0},{3,7},{4,6},{5,1},{6,4},{7,3},{8,10},{9,13},{10,... | collective-permute-start | bytes 1081352 | tf_op jit(solution)/shard_map/ppermute | solution.py:235
  51.5 34.9 %collective-permute-start.20 = (bf16[512,2048]{1,0:T(8,128)(2,1)S(1)}, bf16[512,2048]{1,0:T(8,128)(2,1)S(1)}, u32[]{:S(2)}, u32[]{:S(2)}) collective-permute-start(bf16[512,2048]{1,0:T(8,128)(2,1)S(1)} %copy-done.2), channel_id=1, source_target_pairs={{0,1},{1,0},{2,3},{3,2},{4,5},{5,4},{6,7},{7,6},{8,9},{9,8},{10,11... | collective-permute-start | bytes 6291464 | tf_op jit(solution)/shard_map/ppermute | solution.py:239
  51.5 34.9 %collective-permute-start.21 = (bf16[512,2048]{1,0:T(8,128)(2,1)S(1)}, bf16[512,2048]{1,0:T(8,128)(2,1)S(1)}, u32[]{:S(2)}, u32[]{:S(2)}) collective-permute-start(bf16[512,2048]{1,0:T(8,128)(2,1)S(1)} %copy-done), channel_id=1, source_target_pairs={{0,1},{1,0},{2,3},{3,2},{4,5},{5,4},{6,7},{7,6},{8,9},{9,8},{10,11... | collective-permute-start | bytes 6291464 | tf_op jit(solution)/shard_map/ppermute | solution.py:239
  52.0 17.5 %collective-permute-start.10 = (f32[704,128]{1,0:T(8,128)S(1)}, f32[704,128]{1,0:T(8,128)S(1)}, u32[]{:S(2)}, u32[]{:S(2)}) collective-permute-start(f32[704,128]{1,0:T(8,128)S(1)} %pad_maximum_fusion.1.a0), channel_id=1, source_target_pairs={{0,16},{16,0},{1,17},{17,1},{2,18},{18,2},{3,19},{19,3},{4,20},{20... | collective-permute-start | bytes 1081352 | tf_op jit(solution)/shard_map/ppermute | solution.py:243
  53.6 15.9 %collective-permute-start.7 = (f32[576,128]{1,0:T(8,128)S(1)}, f32[576,128]{1,0:T(8,128)S(1)}, u32[]{:S(2)}, u32[]{:S(2)}) collective-permute-start(f32[576,128]{1,0:T(8,128)S(1)} %add_add_fusion), channel_id=1, source_target_pairs={{0,8},{1,9},{2,10},{3,11},{4,12},{5,13},{6,14},{7,15},{8,0},{9,1},... | collective-permute-start | bytes 884744 | tf_op jit(solution)/shard_map/ppermute | solution.py:235
  58.1 18.2 %collective-permute-start.12 = (f32[704,128]{1,0:T(8,128)S(1)}, f32[704,128]{1,0:T(8,128)S(1)}, u32[]{:S(2)}, u32[]{:S(2)}) collective-permute-start(f32[704,128]{1,0:T(8,128)S(1)} %collective-permute-done.9.a1), channel_id=1, source_target_pairs={{0,16},{16,0},{1,17},{17,1},{2,18},{18,2},{3,19},{19,3},{4,20},{20... | collective-permute-start | bytes 1081352 | tf_op jit(solution)/shard_map/ppermute | solution.py:243
  69.5 16.8 %copy-start.5 = (s32[16]{0:T(128)S(1)}, s32[16]{0:T(128)}, u32[]{:S(2)}) copy-start(s32[16]{0:T(128)} %cell_map.3) | copy-start | bytes 196
  69.5 16.8 %copy-start.6 = (s32[16]{0:T(128)S(1)}, s32[16]{0:T(128)}, u32[]{:S(2)}) copy-start(s32[16]{0:T(128)} %pred_map.1) | copy-start | bytes 196
  69.6 6.8 %collective-permute-start.11 = (f32[576,128]{1,0:T(8,128)S(1)}, f32[576,128]{1,0:T(8,128)S(1)}, u32[]{:S(2)}, u32[]{:S(2)}) collective-permute-start(f32[576,128]{1,0:T(8,128)S(1)} %add.51), channel_id=1, source_target_pairs={{0,4},{1,3},{2,6},{3,1},{4,0},{5,7},{6,2},{7,5},{8,12},{9,11},{10,... | collective-permute-start | bytes 884744 | tf_op jit(solution)/shard_map/ppermute | solution.py:235
  69.6 8.0 %collective-permute-start.14 = (f32[704,128]{1,0:T(8,128)S(1)}, f32[704,128]{1,0:T(8,128)S(1)}, u32[]{:S(2)}, u32[]{:S(2)}) collective-permute-start(f32[704,128]{1,0:T(8,128)S(1)} %pad_maximum_fusion.1.a0), channel_id=1, source_target_pairs={{0,1},{1,0},{2,3},{3,2},{4,5},{5,4},{6,7},{7,6},{8,9},{9,8},{10,11... | collective-permute-start | bytes 1081352 | tf_op jit(solution)/shard_map/ppermute | solution.py:239
  76.3 1.7 %collective-permute-start.15 = (f32[704,128]{1,0:T(8,128)S(1)}, f32[704,128]{1,0:T(8,128)S(1)}, u32[]{:S(2)}, u32[]{:S(2)}) collective-permute-start(f32[704,128]{1,0:T(8,128)S(1)} %collective-permute-done.9.a1), channel_id=1, source_target_pairs={{0,1},{1,0},{2,3},{3,2},{4,5},{5,4},{6,7},{7,6},{8,9},{9,8},{10,11... | collective-permute-start | bytes 1081352 | tf_op jit(solution)/shard_map/ppermute | solution.py:239
  76.4 9.9 %collective-permute-start.13 = (f32[1152,128]{1,0:T(8,128)S(1)}, f32[1152,128]{1,0:T(8,128)S(1)}, u32[]{:S(2)}, u32[]{:S(2)}) collective-permute-start(f32[1152,128]{1,0:T(8,128)S(1)} %pad_maximum_fusion.b0), channel_id=1, source_target_pairs={{0,2},{1,5},{2,0},{3,7},{4,6},{5,1},{6,4},{7,3},{8,10},{9,13},{10,... | collective-permute-start | bytes 1769480 | tf_op jit(solution)/shard_map/ppermute | solution.py:235
  77.6 1.7 %collective-permute-start.16 = (f32[704,128]{1,0:T(8,128)S(1)}, f32[704,128]{1,0:T(8,128)S(1)}, u32[]{:S(2)}, u32[]{:S(2)}) collective-permute-start(f32[704,128]{1,0:T(8,128)S(1)} %collective-permute-done.10.y0), channel_id=1, source_target_pairs={{0,1},{1,0},{2,3},{3,2},{4,5},{5,4},{6,7},{7,6},{8,9},{9,8},{10,11... | collective-permute-start | bytes 1081352 | tf_op jit(solution)/shard_map/ppermute | solution.py:239
  78.0 1.8 %collective-permute-start.17 = (f32[704,128]{1,0:T(8,128)S(1)}, f32[704,128]{1,0:T(8,128)S(1)}, u32[]{:S(2)}, u32[]{:S(2)}) collective-permute-start(f32[704,128]{1,0:T(8,128)S(1)} %collective-permute-done.12.y1), channel_id=1, source_target_pairs={{0,1},{1,0},{2,3},{3,2},{4,5},{5,4},{6,7},{7,6},{8,9},{9,8},{10,11... | collective-permute-start | bytes 1081352 | tf_op jit(solution)/shard_map/ppermute | solution.py:239
  79.3 9.7 %collective-permute-start.18 = (f32[1152,128]{1,0:T(8,128)S(1)}, f32[1152,128]{1,0:T(8,128)S(1)}, u32[]{:S(2)}, u32[]{:S(2)}) collective-permute-start(f32[1152,128]{1,0:T(8,128)S(1)} %pad_maximum_fusion.b0), channel_id=1, source_target_pairs={{0,1},{1,0},{2,3},{3,2},{4,5},{5,4},{6,7},{7,6},{8,9},{9,8},{10,11... | collective-permute-start | bytes 1769480 | tf_op jit(solution)/shard_map/ppermute | solution.py:239
  86.3 2.6 %collective-permute-start.19 = (f32[1152,128]{1,0:T(8,128)S(1)}, f32[1152,128]{1,0:T(8,128)S(1)}, u32[]{:S(2)}, u32[]{:S(2)}) collective-permute-start(f32[1152,128]{1,0:T(8,128)S(1)} %collective-permute-done.13.b1), channel_id=1, source_target_pairs={{0,1},{1,0},{2,3},{3,2},{4,5},{5,4},{6,7},{7,6},{8,9},{9,8},{10,11... | collective-permute-start | bytes 1769480 | tf_op jit(solution)/shard_map/ppermute | solution.py:239

commit v8 on v7

--- a/solution.py
+++ b/solution.py
@@ -191,15 +191,16 @@
 def tiles_kernel(place, pred_map, cell_map, pred, pred_recv, cell, cell_recv, *outs):
     number = pred_map.shape[0]
     half = number // 2
-    sources = ((pred_map, pred), (pred_map, pred_recv), (cell_map, cell), (cell_map, cell_recv))
-    for (tile_map, stored), out in zip(sources, outs):
-        for t in range(number):
-            slot = lax.rem(tile_map[t], number)
-            to = pl.ds(pl.multiple_of(lax.rem(slot, half) * LANES, LANES), LANES)
-
-            @pl.when(lax.div(slot, half) == place[0])
-            def _():
-                out[:, to] = stored[:, t * LANES : (t + 1) * LANES]
+    outs = (outs[:2], outs[2:])
+    for tile_map, own, recv, (mine, theirs) in ((pred_map, pred, pred_recv, outs[0]), (cell_map, cell, cell_recv, outs[1])):
+        slots = [lax.rem(tile_map[t], number) for t in range(number)]
+        for n in range(half):
+            source = jnp.int32(0)
+            for t in range(1, number):
+                source = jnp.where(slots[t] == place[0] * half + n, t, source)
+            at = pl.ds(pl.multiple_of(source * LANES, LANES), LANES)
+            mine[:, n * LANES : (n + 1) * LANES] = own[:, at]
+            theirs[:, n * LANES : (n + 1) * LANES] = recv[:, at]
 
 
 def own_tiles(place, pred_map, cell_map, *fields):
@@ -343,30 +344,25 @@
     sub = lax.broadcasted_iota(jnp.int32, shape, 0)
     rows = [work[SUB * i : SUB * i + SUB, :] for i in range(size // SUB)]
     out = []
-    for b in range(size // SUB):
-        lane = size + SUB * b
-        head = rows[b]
-        cols = [jnp.broadcast_to(head[:, lane + c : lane + c + 1], shape) for c in range(SUB)]
-        entry = [[jnp.broadcast_to(cols[c][r : r + 1, :], shape) for c in range(r + 1)] for r in range(SUB)]
+    while rows:
+        lane = size + SUB * len(out)
+        head, rows = rows[0], rows[1:]
+        column = [[jnp.broadcast_to(r[:, lane + k : lane + k + 1], shape) for k in range(SUB)] for r in [head] + rows]
+        top, column = column[0], column[1:]
+        entry = [[jnp.broadcast_to(top[c][r : r + 1, :], shape) for c in range(r + 1)] for r in range(SUB)]
         y = [jnp.broadcast_to(head[r : r + 1, :], shape) for r in range(SUB)]
-        inverse = []
-        factor = [[None] * SUB for _ in range(SUB)]
         for k in range(SUB):
-            inverse.append(1.0 / entry[k][k])
+            inverse = 1.0 / entry[k][k]
+            scaled = y[k] * inverse
+            factor = [entry[i][k] * inverse if i > k else None for i in range(SUB)]
             for i in range(k + 1, SUB):
-                factor[i][k] = entry[i][k] * inverse[k]
                 for j in range(k + 1, i + 1):
-                    entry[i][j] = entry[i][j] - factor[i][k] * entry[j][k]
-                y[i] = y[i] - factor[i][k] * y[k]
-        p = [y[k] * inverse[k] for k in range(SUB)]
-        for i in reversed(range(SUB)):
-            for k in range(i):
-                p[k] = p[k] - factor[i][k] * p[i]
-        for i in range(b + 1, size // SUB):
-            terms = [jnp.broadcast_to(rows[i][:, lane + k : lane + k + 1], shape) * p[k] for k in range(SUB)]
-            while len(terms) > 1:
-                terms = [terms[t] + terms[t + 1] for t in range(0, len(terms), 2)]
-            rows[i] = rows[i] - terms[0]
+                    entry[i][j] = entry[i][j] - factor[i] * entry[j][k]
+                y[i] = y[i] - factor[i] * y[k]
+            for g in range(len(rows)):
+                rows[g] = rows[g] - column[g][k] * scaled
+                for i in range(k + 1, SUB):
+                    column[g][i] = column[g][i] - factor[i] * column[g][k]
         result, pivot = y[0], entry[0][0]
         for k in range(1, SUB):
             result = jnp.where(sub == k, y[k], result)

time: 111 us -> 109 us (0.982)
  Pallas kernels: 42.4 us -> 40.3 us
    pallas_call x1, Pallas kernels: 21.7 us -> 20.4 us  [second_chain(): pl.pallas_call(functools.partial(second_chain_kernel, bits, orders, count...]
  transfers between devices with their start and end apart: 22 -> 22, of which waited for: 12 -> 13; matrix products, arithmetic and copies ran while one was open for 2% -> 2% of each run, Pallas kernels for 19% -> 18%
where the time goes in v8:
time: 109 us
  waiting for transfers between devices  43.1 us (40%)
  Pallas kernels  40.3 us (37%)
  starting transfers between devices  18.6 us (17%)
  other arithmetic  4.67 us (4%)
  local copies, waits for them, and re-layouts  1.18 us (1%)
    ppermute x10, waiting for transfers between devices, cell_exchange(): return lax.ppermute(value, ('cell', 'day'), pairs)  41.1 us
    pallas_call x1, Pallas kernels, second_chain(): pl.pallas_call(functools.partial(second_chain_kernel, bits, orders, count...  20.4 us
    ppermute x10, starting transfers between devices, cell_exchange(): return lax.ppermute(value, ('cell', 'day'), pairs)  14 us
    pallas_call x2, Pallas kernels, cross(): pl.pallas_call(functools.partial(kernel, orders), out_shape=(out, out), i...  6.4 us
    pallas_call x1, Pallas kernels, first_chain(): pl.pallas_call(functools.partial(first_chain_kernel, bits, orders, counts...  6.08 us
    pallas_call x1, Pallas kernels, own_part(): pl.pallas_call(own_part_kernel, out_shape=jax.ShapeDtypeStruct((size, LAN...  5.52 us
    ppermute x2, starting transfers between devices, other_group(): return lax.ppermute(value, 'group', [(0, 1), (1, 0)])  3.13 us
  transfers between devices with their start and end apart: 22, of which 13 were waited for; matrix products, arithmetic and copies ran while one was open for 2% of the time, Pallas kernels for 18%

profile of v8, /device:TPU:0, one launch (start us, length us, event | category | flops | bytes accessed | tf_op | source)
XLA Modules:
  0.0 108.7 jit_solution(6435734104763427161)
XLA Ops:
  0.6 0.5 collective-permute-start.1
  1.1 0.1 collective-permute-start
  1.2 0.6 pad_add_fusion.place
  1.9 5.5 %own_part.1.part = f32[896,128]{1,0:T(8,128)} custom-call(s32[3]{0:T(128)} %pad_add_fusion.place, s32[16]{0:T(128)} %cell_map.3, bf16[512,2048]{1,0:T(8,128)(2,1)} %pred_.1, bf16[512,2048]{1,0:T(8,128)(2,1)} %cell.1, bf16[64,2048]{1,0:T(8,128)(2,1)} %start.1), custom_call_target="tpu_custom_call" | custom-call | tf_op jit(solution)/shard_map/own_part/pallas_call | solution.py:108
  7.4 0.0 copy-start
  7.4 0.0 collective-permute-done.1.recv
  7.4 0.0 copy-done.1
  7.4 0.0 copy-done.4
  7.4 0.0 copy-start.3
  7.5 1.2 %copy-done.3 = f32[896,128]{1,0:T(8,128)S(1)} copy-done((f32[896,128]{1,0:T(8,128)S(1)}, f32[896,128]{1,0:T(8,128)}, u32[]{:S(2)}) %copy-start.3) | copy-done | bytes 458776
  8.6 2.2 %first_cross.1 = (f32[704,128]{1,0:T(8,128)S(1)}, f32[704,128]{1,0:T(8,128)S(1)}) custom-call(s32[3]{0:T(128)S(1)} %copy-done.4, bf16[512,2048]{1,0:T(8,128)(2,1)S(1)} %copy-done.1, bf16[512,2048]{1,0:T(8,128)(2,1)} %collective-permute-done.1.recv, f32[896,128]{1,0:T(8,128)S(1)} %copy-done.3), custom_call_target="tpu_custom_call" | custom-call | tf_op jit(solution)/shard_map/first_cross/pallas_call | solution.py:180
  10.8 3.0 %collective-permute-start.2 = (f32[704,128]{1,0:T(8,128)S(1)}, f32[704,128]{1,0:T(8,128)}, u32[]{:S(2)}, u32[]{:S(2)}) collective-permute-start(f32[704,128]{1,0:T(8,128)S(1)} %get-tuple-element.25), channel_id=1, source_target_pairs={{0,2},{1,5},{2,0},{3,7},{4,6},{5,1},{6,4},{7,3},{8,10},{9,13},{10,... | collective-permute-start | bytes 1081352 | tf_op jit(solution)/shard_map/ppermute | solution.py:236
  13.7 0.0 collective-permute-done.recv
  13.7 4.2 %second_cross.1 = (f32[1152,128]{1,0:T(8,128)S(1)}, f32[1152,128]{1,0:T(8,128)}) custom-call(s32[3]{0:T(128)S(1)} %copy-done.4, bf16[512,2048]{1,0:T(8,128)(2,1)S(1)} %copy-done, bf16[512,2048]{1,0:T(8,128)(2,1)} %collective-permute-done.recv), custom_call_target="tpu_custom_call" | custom-call | tf_op jit(solution)/shard_map/second_cross/pallas_call | solution.py:180
  18.0 1.3 %collective-permute-done.2 = f32[704,128]{1,0:T(8,128)} collective-permute-done((f32[704,128]{1,0:T(8,128)S(1)}, f32[704,128]{1,0:T(8,128)}, u32[]{:S(2)}, u32[]{:S(2)}) %collective-permute-start.2) | collective-permute-done | bytes 360480 | tf_op jit(solution)/shard_map/ppermute | solution.py:236
  19.3 0.9 dynamic-slice_add_fusion.1
  20.2 2.1 %collective-permute-start.3 = (f32[1152,128]{1,0:T(8,128)}, f32[1152,128]{1,0:T(8,128)}, u32[]{:S(2)}, u32[]{:S(2)}) collective-permute-start(f32[1152,128]{1,0:T(8,128)} %get-tuple-element.30), channel_id=1, source_target_pairs={{0,2},{1,5},{2,0},{3,7},{4,6},{5,1},{6,4},{7,3},{8,10},{9,13},{10,... | collective-permute-start | bytes 1769480 | tf_op jit(solution)/shard_map/ppermute | solution.py:236
  22.3 1.6 %collective-permute-start.4 = (f32[352,128]{1,0:T(8,128)S(1)}, f32[352,128]{1,0:T(8,128)S(1)}, u32[]{:S(2)}, u32[]{:S(2)}) collective-permute-start(f32[352,128]{1,0:T(8,128)S(1)} %dynamic-slice_add_fusion.1), channel_id=1, source_target_pairs={{0,4},{1,3},{2,6},{3,1},{4,0},{5,7},{6,2},{7,5},{8,12},{9,11},{10,... | collective-permute-start | bytes 540680 | tf_op jit(solution)/shard_map/ppermute | solution.py:236
  23.9 5.9 %collective-permute-done.4 = f32[352,128]{1,0:T(8,128)S(1)} collective-permute-done((f32[352,128]{1,0:T(8,128)S(1)}, f32[352,128]{1,0:T(8,128)S(1)}, u32[]{:S(2)}, u32[]{:S(2)}) %collective-permute-start.4) | collective-permute-done | bytes 180256 | tf_op jit(solution)/shard_map/ppermute | solution.py:236
  29.8 1.0 add_add_fusion.1
  30.7 1.5 %collective-permute-done.3 = f32[1152,128]{1,0:T(8,128)} collective-permute-done((f32[1152,128]{1,0:T(8,128)}, f32[1152,128]{1,0:T(8,128)}, u32[]{:S(2)}, u32[]{:S(2)}) %collective-permute-start.3) | collective-permute-done | bytes 589856 | tf_op jit(solution)/shard_map/ppermute | solution.py:236
  32.3 1.0 dynamic-slice_add_fusion
  33.3 0.4 collective-permute-start.5
  33.7 2.7 %collective-permute-start.6 = (f32[352,128]{1,0:T(8,128)S(1)}, f32[352,128]{1,0:T(8,128)S(1)}, u32[]{:S(2)}, u32[]{:S(2)}) collective-permute-start(f32[352,128]{1,0:T(8,128)S(1)} %add_add_fusion.1), channel_id=1, source_target_pairs={{0,8},{1,9},{2,10},{3,11},{4,12},{5,13},{6,14},{7,15},{8,0},{9,1},... | collective-permute-start | bytes 540680 | tf_op jit(solution)/shard_map/ppermute | solution.py:236
  36.4 7.5 %collective-permute-done.5 = f32[576,128]{1,0:T(8,128)S(1)} collective-permute-done((f32[576,128]{1,0:T(8,128)S(1)}, f32[576,128]{1,0:T(8,128)S(1)}, u32[]{:S(2)}, u32[]{:S(2)}) %collective-permute-start.5) | collective-permute-done | bytes 294944 | tf_op jit(solution)/shard_map/ppermute | solution.py:236
  43.9 1.0 add_add_fusion
  44.9 0.0 collective-permute-done.6
  45.0 0.7 collective-permute-start.8
  45.7 4.8 %collective-permute-done.8 = f32[352,128]{1,0:T(8,128)S(1)} collective-permute-done((f32[352,128]{1,0:T(8,128)S(1)}, f32[352,128]{1,0:T(8,128)S(1)}, u32[]{:S(2)}, u32[]{:S(2)}) %collective-permute-start.8) | collective-permute-done | bytes 180256 | tf_op jit(solution)/shard_map/ppermute | solution.py:236
  50.6 0.9 collective-permute-start.9
  51.4 0.0 collective-permute-start.20
  51.4 0.5 collective-permute-start.21
  52.0 1.6 %collective-permute-start.10 = (f32[704,128]{1,0:T(8,128)S(1)}, f32[704,128]{1,0:T(8,128)S(1)}, u32[]{:S(2)}, u32[]{:S(2)}) collective-permute-start(f32[704,128]{1,0:T(8,128)S(1)} %pad_maximum_fusion.1.a0), channel_id=1, source_target_pairs={{0,16},{16,0},{1,17},{17,1},{2,18},{18,2},{3,19},{19,3},{4,20},{20... | collective-permute-start | bytes 1081352 | tf_op jit(solution)/shard_map/ppermute | solution.py:244
  53.6 1.5 %collective-permute-start.7 = (f32[576,128]{1,0:T(8,128)S(1)}, f32[576,128]{1,0:T(8,128)S(1)}, u32[]{:S(2)}, u32[]{:S(2)}) collective-permute-start(f32[576,128]{1,0:T(8,128)S(1)} %add_add_fusion), channel_id=1, source_target_pairs={{0,8},{1,9},{2,10},{3,11},{4,12},{5,13},{6,14},{7,15},{8,0},{9,1},... | collective-permute-start | bytes 884744 | tf_op jit(solution)/shard_map/ppermute | solution.py:236
  55.1 3.0 %collective-permute-done.9.a1 = f32[704,128]{1,0:T(8,128)S(1)} collective-permute-done((f32[704,128]{1,0:T(8,128)S(1)}, f32[704,128]{1,0:T(8,128)S(1)}, u32[]{:S(2)}, u32[]{:S(2)}) %collective-permute-start.9) | collective-permute-done | bytes 360480 | tf_op jit(solution)/shard_map/ppermute | solution.py:236
  58.1 1.5 %collective-permute-start.12 = (f32[704,128]{1,0:T(8,128)S(1)}, f32[704,128]{1,0:T(8,128)S(1)}, u32[]{:S(2)}, u32[]{:S(2)}) collective-permute-start(f32[704,128]{1,0:T(8,128)S(1)} %collective-permute-done.9.a1), channel_id=1, source_target_pairs={{0,16},{16,0},{1,17},{17,1},{2,18},{18,2},{3,19},{19,3},{4,20},{20... | collective-permute-start | bytes 1081352 | tf_op jit(solution)/shard_map/ppermute | solution.py:244
  59.6 9.9 %collective-permute-done.7 = f32[576,128]{1,0:T(8,128)S(1)} collective-permute-done((f32[576,128]{1,0:T(8,128)S(1)}, f32[576,128]{1,0:T(8,128)S(1)}, u32[]{:S(2)}, u32[]{:S(2)}) %collective-permute-start.7) | collective-permute-done | bytes 294944 | tf_op jit(solution)/shard_map/ppermute | solution.py:236
  69.4 0.0 collective-permute-done.10.y0
  69.5 0.0 copy-start.5
  69.5 0.0 copy-start.6
  69.5 0.1 collective-permute-start.11
  69.6 0.1 collective-permute-start.14
  69.7 6.6 %collective-permute-done.11 = f32[576,128]{1,0:T(8,128)S(1)} collective-permute-done((f32[576,128]{1,0:T(8,128)S(1)}, f32[576,128]{1,0:T(8,128)S(1)}, u32[]{:S(2)}, u32[]{:S(2)}) %collective-permute-start.11) | collective-permute-done | bytes 294944 | tf_op jit(solution)/shard_map/ppermute | solution.py:236
  76.3 0.0 collective-permute-start.15
  76.3 0.0 collective-permute-done.12.y1
  76.3 1.2 %collective-permute-start.13 = (f32[1152,128]{1,0:T(8,128)S(1)}, f32[1152,128]{1,0:T(8,128)S(1)}, u32[]{:S(2)}, u32[]{:S(2)}) collective-permute-start(f32[1152,128]{1,0:T(8,128)S(1)} %pad_maximum_fusion.b0), channel_id=1, source_target_pairs={{0,2},{1,5},{2,0},{3,7},{4,6},{5,1},{6,4},{7,3},{8,10},{9,13},{10,... | collective-permute-start | bytes 1769480 | tf_op jit(solution)/shard_map/ppermute | solution.py:236
  77.5 0.0 collective-permute-done.14.a0_twin
  77.5 0.0 collective-permute-start.16
  77.5 0.5 collective-permute-done.15.a1_twin
  78.0 0.1 collective-permute-start.17
  78.1 1.1 collective-permute-done.16.y0_twin
  79.2 0.1 collective-permute-start.18
  79.3 0.4 collective-permute-done.17.y1_twin
  79.7 6.1 %first_chain.1 = (bf16[3,1024,1024]{2,1,0:T(8,128)(2,1)S(1)}, bf16[64,1024]{1,0:T(8,128)(2,1)S(1)}, bf16[64,1024]{1,0:T(8,128)(2,1)S(1)}) custom-call(s32[3]{0:T(128)S(1)} %copy-done.4, f32[704,128]{1,0:T(8,128)S(1)} %pad_maximum_fusion.1.a0, f32[704,128]{1,0:T(8,128)S(1)} %collective-permute-done.9.a1, f32[704,128]{1,0:T(8,128)S(1)} %collective-permute-done.10.y0, ...), custom_call_target="tpu_custom_call" | custom-call | tf_op jit(solution)/shard_map/first_chain/pallas_call | solution.py:422
  85.8 0.5 collective-permute-done.13.b1
  86.3 0.0 collective-permute-start.19
  86.3 0.0 collective-permute-done.20.pred_recv
  86.3 0.0 collective-permute-done.21.cell_recv
  86.3 0.0 copy-done.5
  86.3 0.0 copy-done.6
  86.3 1.8 %own_tiles.1 = (bf16[512,1024]{1,0:T(8,128)(2,1)S(1)}, bf16[512,1024]{1,0:T(8,128)(2,1)S(1)}, bf16[512,1024]{1,0:T(8,128)(2,1)S(1)}, bf16[512,1024]{1,0:T(8,128)(2,1)S(1)}) custom-call(s32[3]{0:T(128)S(1)} %copy-done.4, s32[16]{0:T(128)S(1)} %copy-done.6, s32[16]{0:T(128)S(1)} %copy-done.5, bf16[512,2048]{1,0:T(8,128)(2,1)S(1)} %copy-done.2, ...), custom_call_target="tpu_custom_call" | custom-call | tf_op jit(solution)/shard_map/own_tiles/pallas_call | solution.py:209
  88.2 0.0 collective-permute-done.18.b0_twin
  88.2 0.1 collective-permute-done.19.b1_twin
  88.3 20.4 %second_chain.1 = (f32[64,1024]{1,0:T(8,128)}, f32[64,1024]{1,0:T(8,128)}) custom-call(s32[3]{0:T(128)S(1)} %copy-done.4, f32[1152,128]{1,0:T(8,128)S(1)} %pad_maximum_fusion.b0, f32[1152,128]{1,0:T(8,128)S(1)} %collective-permute-done.13.b1, f32[1152,128]{1,0:T(8,128)S(1)} %collective-permute-done.18.b0_twin, ...), custom_call_target="tpu_custom_call" | custom-call | tf_op jit(solution)/shard_map/second_chain/pallas_call | solution.py:470
  (9 shorter events, 0.1 us)
Async XLA Ops:
  0.6 6.8 %collective-permute-start.1 = (bf16[512,2048]{1,0:T(8,128)(2,1)}, bf16[512,2048]{1,0:T(8,128)(2,1)}, u32[]{:S(2)}, u32[]{:S(2)}) collective-permute-start(bf16[512,2048]{1,0:T(8,128)(2,1)} %pred_.1), channel_id=1, source_target_pairs={{0,1},{1,0},{2,3},{3,2},{4,5},{5,4},{6,7},{7,6},{8,9},{9,8},{10,11... | collective-permute-start | bytes 6291464 | tf_op jit(solution)/shard_map/ppermute | solution.py:240
  1.1 12.6 %collective-permute-start = (bf16[512,2048]{1,0:T(8,128)(2,1)}, bf16[512,2048]{1,0:T(8,128)(2,1)}, u32[]{:S(2)}, u32[]{:S(2)}) collective-permute-start(bf16[512,2048]{1,0:T(8,128)(2,1)} %cell.1), channel_id=1, source_target_pairs={{0,1},{1,0},{2,3},{3,2},{4,5},{5,4},{6,7},{7,6},{8,9},{9,8},{10,11... | collective-permute-start | bytes 6291464 | tf_op jit(solution)/shard_map/ppermute | solution.py:240
  1.9 5.6 %copy-start.1 = (bf16[512,2048]{1,0:T(8,128)(2,1)S(1)}, bf16[512,2048]{1,0:T(8,128)(2,1)}, u32[]{:S(2)}) copy-start(bf16[512,2048]{1,0:T(8,128)(2,1)} %pred_.1) | copy-start | bytes 6291460
  1.9 5.6 %copy-start.4 = (s32[3]{0:T(128)S(1)}, s32[3]{0:T(128)}, u32[]{:S(2)}) copy-start(s32[3]{0:T(128)} %pad_add_fusion.place) | copy-start | bytes 40
  7.4 6.3 %copy-start = (bf16[512,2048]{1,0:T(8,128)(2,1)S(1)}, bf16[512,2048]{1,0:T(8,128)(2,1)}, u32[]{:S(2)}) copy-start(bf16[512,2048]{1,0:T(8,128)(2,1)} %cell.1) | copy-start | bytes 6291460
  7.4 1.2 %copy-start.3 = (f32[896,128]{1,0:T(8,128)S(1)}, f32[896,128]{1,0:T(8,128)}, u32[]{:S(2)}) copy-start(f32[896,128]{1,0:T(8,128)} %own_part.1.part) | copy-start | bytes 1376260
  10.8 8.5 %collective-permute-start.2 = (f32[704,128]{1,0:T(8,128)S(1)}, f32[704,128]{1,0:T(8,128)}, u32[]{:S(2)}, u32[]{:S(2)}) collective-permute-start(f32[704,128]{1,0:T(8,128)S(1)} %get-tuple-element.25), channel_id=1, source_target_pairs={{0,2},{1,5},{2,0},{3,7},{4,6},{5,1},{6,4},{7,3},{8,10},{9,13},{10,... | collective-permute-start | bytes 1081352 | tf_op jit(solution)/shard_map/ppermute | solution.py:236
  20.2 12.1 %collective-permute-start.3 = (f32[1152,128]{1,0:T(8,128)}, f32[1152,128]{1,0:T(8,128)}, u32[]{:S(2)}, u32[]{:S(2)}) collective-permute-start(f32[1152,128]{1,0:T(8,128)} %get-tuple-element.30), channel_id=1, source_target_pairs={{0,2},{1,5},{2,0},{3,7},{4,6},{5,1},{6,4},{7,3},{8,10},{9,13},{10,... | collective-permute-start | bytes 1769480 | tf_op jit(solution)/shard_map/ppermute | solution.py:236
  22.3 7.5 %collective-permute-start.4 = (f32[352,128]{1,0:T(8,128)S(1)}, f32[352,128]{1,0:T(8,128)S(1)}, u32[]{:S(2)}, u32[]{:S(2)}) collective-permute-start(f32[352,128]{1,0:T(8,128)S(1)} %dynamic-slice_add_fusion.1), channel_id=1, source_target_pairs={{0,4},{1,3},{2,6},{3,1},{4,0},{5,7},{6,2},{7,5},{8,12},{9,11},{10,... | collective-permute-start | bytes 540680 | tf_op jit(solution)/shard_map/ppermute | solution.py:236
  33.3 10.7 %collective-permute-start.5 = (f32[576,128]{1,0:T(8,128)S(1)}, f32[576,128]{1,0:T(8,128)S(1)}, u32[]{:S(2)}, u32[]{:S(2)}) collective-permute-start(f32[576,128]{1,0:T(8,128)S(1)} %dynamic-slice_add_fusion), channel_id=1, source_target_pairs={{0,4},{1,3},{2,6},{3,1},{4,0},{5,7},{6,2},{7,5},{8,12},{9,11},{10,... | collective-permute-start | bytes 884744 | tf_op jit(solution)/shard_map/ppermute | solution.py:236
  33.7 17.8 %copy-start.2 = (bf16[512,2048]{1,0:T(8,128)(2,1)S(1)}, bf16[512,2048]{1,0:T(8,128)(2,1)}, u32[]{:S(2)}) copy-start(bf16[512,2048]{1,0:T(8,128)(2,1)} %pred_.1) | copy-start | bytes 6291460
  33.7 11.3 %collective-permute-start.6 = (f32[352,128]{1,0:T(8,128)S(1)}, f32[352,128]{1,0:T(8,128)S(1)}, u32[]{:S(2)}, u32[]{:S(2)}) collective-permute-start(f32[352,128]{1,0:T(8,128)S(1)} %add_add_fusion.1), channel_id=1, source_target_pairs={{0,8},{1,9},{2,10},{3,11},{4,12},{5,13},{6,14},{7,15},{8,0},{9,1},... | collective-permute-start | bytes 540680 | tf_op jit(solution)/shard_map/ppermute | solution.py:236
  45.0 5.6 %collective-permute-start.8 = (f32[352,128]{1,0:T(8,128)S(1)}, f32[352,128]{1,0:T(8,128)S(1)}, u32[]{:S(2)}, u32[]{:S(2)}) collective-permute-start(f32[352,128]{1,0:T(8,128)S(1)} %add.50), channel_id=1, source_target_pairs={{0,4},{1,3},{2,6},{3,1},{4,0},{5,7},{6,2},{7,5},{8,12},{9,11},{10,... | collective-permute-start | bytes 540680 | tf_op jit(solution)/shard_map/ppermute | solution.py:236
  50.6 7.5 %collective-permute-start.9 = (f32[704,128]{1,0:T(8,128)S(1)}, f32[704,128]{1,0:T(8,128)S(1)}, u32[]{:S(2)}, u32[]{:S(2)}) collective-permute-start(f32[704,128]{1,0:T(8,128)S(1)} %pad_maximum_fusion.1.a0), channel_id=1, source_target_pairs={{0,2},{1,5},{2,0},{3,7},{4,6},{5,1},{6,4},{7,3},{8,10},{9,13},{10,... | collective-permute-start | bytes 1081352 | tf_op jit(solution)/shard_map/ppermute | solution.py:236
  51.4 34.9 %collective-permute-start.20 = (bf16[512,2048]{1,0:T(8,128)(2,1)S(1)}, bf16[512,2048]{1,0:T(8,128)(2,1)S(1)}, u32[]{:S(2)}, u32[]{:S(2)}) collective-permute-start(bf16[512,2048]{1,0:T(8,128)(2,1)S(1)} %copy-done.2), channel_id=1, source_target_pairs={{0,1},{1,0},{2,3},{3,2},{4,5},{5,4},{6,7},{7,6},{8,9},{9,8},{10,11... | collective-permute-start | bytes 6291464 | tf_op jit(solution)/shard_map/ppermute | solution.py:240
  51.4 34.9 %collective-permute-start.21 = (bf16[512,2048]{1,0:T(8,128)(2,1)S(1)}, bf16[512,2048]{1,0:T(8,128)(2,1)S(1)}, u32[]{:S(2)}, u32[]{:S(2)}) collective-permute-start(bf16[512,2048]{1,0:T(8,128)(2,1)S(1)} %copy-done), channel_id=1, source_target_pairs={{0,1},{1,0},{2,3},{3,2},{4,5},{5,4},{6,7},{7,6},{8,9},{9,8},{10,11... | collective-permute-start | bytes 6291464 | tf_op jit(solution)/shard_map/ppermute | solution.py:240
  52.0 17.5 %collective-permute-start.10 = (f32[704,128]{1,0:T(8,128)S(1)}, f32[704,128]{1,0:T(8,128)S(1)}, u32[]{:S(2)}, u32[]{:S(2)}) collective-permute-start(f32[704,128]{1,0:T(8,128)S(1)} %pad_maximum_fusion.1.a0), channel_id=1, source_target_pairs={{0,16},{16,0},{1,17},{17,1},{2,18},{18,2},{3,19},{19,3},{4,20},{20... | collective-permute-start | bytes 1081352 | tf_op jit(solution)/shard_map/ppermute | solution.py:244
  53.6 15.9 %collective-permute-start.7 = (f32[576,128]{1,0:T(8,128)S(1)}, f32[576,128]{1,0:T(8,128)S(1)}, u32[]{:S(2)}, u32[]{:S(2)}) collective-permute-start(f32[576,128]{1,0:T(8,128)S(1)} %add_add_fusion), channel_id=1, source_target_pairs={{0,8},{1,9},{2,10},{3,11},{4,12},{5,13},{6,14},{7,15},{8,0},{9,1},... | collective-permute-start | bytes 884744 | tf_op jit(solution)/shard_map/ppermute | solution.py:236
  58.1 18.2 %collective-permute-start.12 = (f32[704,128]{1,0:T(8,128)S(1)}, f32[704,128]{1,0:T(8,128)S(1)}, u32[]{:S(2)}, u32[]{:S(2)}) collective-permute-start(f32[704,128]{1,0:T(8,128)S(1)} %collective-permute-done.9.a1), channel_id=1, source_target_pairs={{0,16},{16,0},{1,17},{17,1},{2,18},{18,2},{3,19},{19,3},{4,20},{20... | collective-permute-start | bytes 1081352 | tf_op jit(solution)/shard_map/ppermute | solution.py:244
  69.5 16.8 %copy-start.5 = (s32[16]{0:T(128)S(1)}, s32[16]{0:T(128)}, u32[]{:S(2)}) copy-start(s32[16]{0:T(128)} %cell_map.3) | copy-start | bytes 196
  69.5 16.8 %copy-start.6 = (s32[16]{0:T(128)S(1)}, s32[16]{0:T(128)}, u32[]{:S(2)}) copy-start(s32[16]{0:T(128)} %pred_map.1) | copy-start | bytes 196
  69.5 6.8 %collective-permute-start.11 = (f32[576,128]{1,0:T(8,128)S(1)}, f32[576,128]{1,0:T(8,128)S(1)}, u32[]{:S(2)}, u32[]{:S(2)}) collective-permute-start(f32[576,128]{1,0:T(8,128)S(1)} %add.51), channel_id=1, source_target_pairs={{0,4},{1,3},{2,6},{3,1},{4,0},{5,7},{6,2},{7,5},{8,12},{9,11},{10,... | collective-permute-start | bytes 884744 | tf_op jit(solution)/shard_map/ppermute | solution.py:236
  69.6 7.9 %collective-permute-start.14 = (f32[704,128]{1,0:T(8,128)S(1)}, f32[704,128]{1,0:T(8,128)S(1)}, u32[]{:S(2)}, u32[]{:S(2)}) collective-permute-start(f32[704,128]{1,0:T(8,128)S(1)} %pad_maximum_fusion.1.a0), channel_id=1, source_target_pairs={{0,1},{1,0},{2,3},{3,2},{4,5},{5,4},{6,7},{7,6},{8,9},{9,8},{10,11... | collective-permute-start | bytes 1081352 | tf_op jit(solution)/shard_map/ppermute | solution.py:240
  76.3 1.7 %collective-permute-start.15 = (f32[704,128]{1,0:T(8,128)S(1)}, f32[704,128]{1,0:T(8,128)S(1)}, u32[]{:S(2)}, u32[]{:S(2)}) collective-permute-start(f32[704,128]{1,0:T(8,128)S(1)} %collective-permute-done.9.a1), channel_id=1, source_target_pairs={{0,1},{1,0},{2,3},{3,2},{4,5},{5,4},{6,7},{7,6},{8,9},{9,8},{10,11... | collective-permute-start | bytes 1081352 | tf_op jit(solution)/shard_map/ppermute | solution.py:240
  76.3 9.9 %collective-permute-start.13 = (f32[1152,128]{1,0:T(8,128)S(1)}, f32[1152,128]{1,0:T(8,128)S(1)}, u32[]{:S(2)}, u32[]{:S(2)}) collective-permute-start(f32[1152,128]{1,0:T(8,128)S(1)} %pad_maximum_fusion.b0), channel_id=1, source_target_pairs={{0,2},{1,5},{2,0},{3,7},{4,6},{5,1},{6,4},{7,3},{8,10},{9,13},{10,... | collective-permute-start | bytes 1769480 | tf_op jit(solution)/shard_map/ppermute | solution.py:236
  77.5 1.7 %collective-permute-start.16 = (f32[704,128]{1,0:T(8,128)S(1)}, f32[704,128]{1,0:T(8,128)S(1)}, u32[]{:S(2)}, u32[]{:S(2)}) collective-permute-start(f32[704,128]{1,0:T(8,128)S(1)} %collective-permute-done.10.y0), channel_id=1, source_target_pairs={{0,1},{1,0},{2,3},{3,2},{4,5},{5,4},{6,7},{7,6},{8,9},{9,8},{10,11... | collective-permute-start | bytes 1081352 | tf_op jit(solution)/shard_map/ppermute | solution.py:240
  78.0 1.7 %collective-permute-start.17 = (f32[704,128]{1,0:T(8,128)S(1)}, f32[704,128]{1,0:T(8,128)S(1)}, u32[]{:S(2)}, u32[]{:S(2)}) collective-permute-start(f32[704,128]{1,0:T(8,128)S(1)} %collective-permute-done.12.y1), channel_id=1, source_target_pairs={{0,1},{1,0},{2,3},{3,2},{4,5},{5,4},{6,7},{7,6},{8,9},{9,8},{10,11... | collective-permute-start | bytes 1081352 | tf_op jit(solution)/shard_map/ppermute | solution.py:240
  79.2 9.0 %collective-permute-start.18 = (f32[1152,128]{1,0:T(8,128)S(1)}, f32[1152,128]{1,0:T(8,128)S(1)}, u32[]{:S(2)}, u32[]{:S(2)}) collective-permute-start(f32[1152,128]{1,0:T(8,128)S(1)} %pad_maximum_fusion.b0), channel_id=1, source_target_pairs={{0,1},{1,0},{2,3},{3,2},{4,5},{5,4},{6,7},{7,6},{8,9},{9,8},{10,11... | collective-permute-start | bytes 1769480 | tf_op jit(solution)/shard_map/ppermute | solution.py:240
  86.3 2.0 %collective-permute-start.19 = (f32[1152,128]{1,0:T(8,128)S(1)}, f32[1152,128]{1,0:T(8,128)S(1)}, u32[]{:S(2)}, u32[]{:S(2)}) collective-permute-start(f32[1152,128]{1,0:T(8,128)S(1)} %collective-permute-done.13.b1), channel_id=1, source_target_pairs={{0,1},{1,0},{2,3},{3,2},{4,5},{5,4},{6,7},{7,6},{8,9},{9,8},{10,11... | collective-permute-start | bytes 1769480 | tf_op jit(solution)/shard_map/ppermute | solution.py:240
